TPU v7x, 32 devices: a whole 2x2x4 slice. The times are simulated.
32 devices in a mesh: seq: 8 (over z, core), tp: 4 (over y, x).
Axes of the slice: x: 2, y: 2, z: 4, core: 2. Of those that a mesh axis runs over, the one named last changes fastest.
Arguments:
- inputs: bfloat16 [4, 1024, 2048], P('tp', 'seq'), may hold values from -6 to 6
- query_weight: bfloat16 [2048, 2048], P(None, 'tp'), may hold values from -0.125 to 0.125
- key_weight: bfloat16 [2048, 2048], P(None, 'tp'), may hold values from -0.125 to 0.125
- value_weight: bfloat16 [2048, 4096], P(None, 'tp'), may hold values from -0.125 to 0.125
- swish_weight: bfloat16 [2048, 4096], P(None, 'tp'), may hold values from -0.125 to 0.125
- output_weight: bfloat16 [4096, 2048], P('tp'), may hold values from -0.1875 to 0.1875
- gate_weight: bfloat16 [2048, 4096], P(None, 'tp'), may hold values from -0.125 to 0.125
- up_weight: bfloat16 [2048, 4096], P(None, 'tp'), may hold values from -0.125 to 0.125
- down_weight: bfloat16 [4096, 2048], P('tp'), may hold values from -0.09375 to 0.09375
- attn_gain: float32 [2048], replicated, may hold values from 0.1 to 1.9
- attn_bias: float32 [2048], replicated, may hold values from -3 to 3
- mlp_gain: float32 [2048], replicated, may hold values from 0.1 to 1.9
- mlp_bias: float32 [2048], replicated, may hold values from -3 to 3
- output_grad: bfloat16 [4, 1024, 2048], P('tp', 'seq'), may hold values from -6 to 6
Outputs:
- outputs: bfloat16 [4, 1024, 2048], P('tp', 'seq')
- input_grad: bfloat16 [4, 1024, 2048], P('tp', 'seq')
- query_grad: float32 [2048, 2048], P('seq', 'tp')
- key_grad: float32 [2048, 2048], P('seq', 'tp')
- value_grad: float32 [2048, 4096], P('seq', 'tp')
- swish_grad: float32 [2048, 4096], P('seq', 'tp')
- mixer_grad: float32 [4096, 2048], P('tp', 'seq')
- gate_grad: float32 [2048, 4096], P('seq', 'tp')
- up_grad: float32 [2048, 4096], P('seq', 'tp')
- down_grad: float32 [4096, 2048], P('tp', 'seq')
- attngain_grad: float32 [2048], P(('seq', 'tp'))
- attnbias_grad: float32 [2048], P(('seq', 'tp'))
- mlpgain_grad: float32 [2048], P(('seq', 'tp'))
- mlpbias_grad: float32 [2048], P(('seq', 'tp'))
All inputs are finite; a program needn't handle non-finite values.
Results may differ from a plain program's by a relative error of at most 0.02.
Values may be sent and summed in bfloat16 or wider, within the bound.
A program may use at most 256 MiB of HBM per device.

v0:
```python
import jax
import jax.numpy as jnp
from jax import lax
from jax.sharding import PartitionSpec as P

DK = 256
DV = 512


EPS = 1e-05


def entering(part, axis, combine, identity):
    place = lax.axis_index(axis)
    gathered = jax.tree.map(lambda a: lax.all_gather(a, axis), part)
    state = jax.tree.map(lambda a, e: jnp.zeros_like(a) + jnp.asarray(e, a.dtype), part, identity)

    def entering_one(turn, state):
        return combine(
            state, jax.tree.map(lambda a: lax.dynamic_index_in_dim(a, turn, 0, False), gathered)
        )

    return lax.fori_loop(0, place, entering_one, state)


def prefix(value, axis, join, neutral):
    count = lax.axis_size(axis)
    place = lax.axis_index(axis)
    ahead = count - 1 - place
    gathered = jax.tree.map(
        lambda a, kind: lax.all_gather(a.astype(kind), axis), value, (jnp.bfloat16, jnp.bfloat16)
    )
    state = jax.tree.map(lambda a, e: jnp.zeros_like(a) + jnp.asarray(e, a.dtype), value, neutral)

    def prefix_one(turn, state):
        source = count - 1 - turn
        return join(
            state,
            jax.tree.map(
                lambda a, own: lax.dynamic_index_in_dim(a, source, 0, False).astype(own.dtype),
                gathered,
                value,
            ),
        )

    return lax.fori_loop(0, ahead, prefix_one, state)


def layer_norm(values, gain, bias):
    center = values - jnp.mean(values, -1, keepdims=True)
    spread = jnp.mean(center * center, -1, keepdims=True)
    return center * lax.rsqrt(spread + EPS) * gain + bias


def head_norm(values):
    center = values - jnp.mean(values, -1, keepdims=True)
    spread = jnp.mean(center * center, -1, keepdims=True)
    return center * lax.rsqrt(spread + EPS)


def rotation(values, angles):
    half_width = values.shape[-1] // 2
    cosine = jnp.cos(angles)
    sine = jnp.sin(angles)
    cosine = jnp.concatenate([cosine, cosine], -1)[:, None, :]
    sine = jnp.concatenate([sine, sine], -1)[:, None, :]
    turned = jnp.concatenate([-values[..., half_width:], values[..., :half_width]], -1)
    return values * cosine + turned * sine


def chain_join(earlier, later):
    return (earlier[0] * later[0], later[0][None, :, None, None] * earlier[1] + later[1])


def gated_mix(swish_pre, mixed):
    return jax.nn.silu(swish_pre) * head_norm(mixed)


def gated_mlp(gate, upper):
    return jax.nn.gelu(gate, approximate=True) * upper


def shards(
    inputs,
    query_weight,
    key_weight,
    value_weight,
    swish_weight,
    output_weight,
    gate_weight,
    up_weight,
    down_weight,
    attn_gain,
    attn_bias,
    mlp_gain,
    mlp_bias,
    output_grad,
):
    local_seqs, block_len, model_width = inputs.shape
    heads_local = query_weight.shape[1] // DK
    inputs_full = inputs.astype(jnp.float32)
    normed_one = layer_norm(inputs_full, attn_gain, attn_bias).astype(jnp.bfloat16)
    gathered_one = lax.all_gather(normed_one, "tp", axis=0, tiled=True)
    seq_count = gathered_one.shape[0]
    row_total = seq_count * block_len
    flat_one = gathered_one.reshape(row_total, model_width)
    query = jnp.dot(flat_one, query_weight, preferred_element_type=jnp.float32).reshape(
        seq_count, block_len, heads_local, DK
    )
    keys_pre = jnp.dot(flat_one, key_weight, preferred_element_type=jnp.float32).reshape(
        seq_count, block_len, heads_local, DK
    )
    value = (
        jnp.dot(flat_one, value_weight, preferred_element_type=jnp.float32)
        .astype(jnp.bfloat16)
        .reshape(seq_count, block_len, heads_local, DV)
    )
    swish_pre = jnp.dot(flat_one, swish_weight, preferred_element_type=jnp.float32).reshape(
        seq_count, block_len, heads_local, DV
    )
    half_width = DK // 2
    frequencies = jnp.power(10000.0, -jnp.arange(half_width, dtype=jnp.float32) / half_width)
    steps_in = jnp.arange(block_len, dtype=jnp.float32)
    positions = lax.axis_index("seq").astype(jnp.float32) * block_len + steps_in
    angles = positions[:, None] * frequencies[None, :]
    query_rot = rotation(query, angles).astype(jnp.bfloat16)
    key_rot = rotation(keys_pre, angles).astype(jnp.bfloat16)
    head_ids = (lax.axis_index("tp") * heads_local + jnp.arange(heads_local)).astype(jnp.float32)
    decays = 1.0 - jnp.exp2(-5.0 - head_ids)
    lag = steps_in[:, None] - steps_in[None, :]
    decay_mat = jnp.where(
        lag[None] >= 0, jnp.power(decays[:, None, None], jnp.maximum(lag, 0.0)[None]), 0.0
    )
    query_fac = jnp.power(decays[None, :], steps_in[:, None] + 1.0)
    key_fac = jnp.power(decays[None, :], block_len - 1.0 - steps_in[:, None])
    block_fac = jnp.power(decays, block_len * 1.0)
    raw = jnp.einsum("sthk,suhk->shtu", query_rot, key_rot, preferred_element_type=jnp.float32)
    scores = (raw * decay_mat[None]).astype(jnp.bfloat16)
    intra = jnp.einsum("shtu,suhv->sthv", scores, value, preferred_element_type=jnp.float32)
    key_dec = (key_rot * key_fac[None, :, :, None]).astype(jnp.bfloat16)
    local_state = jnp.einsum("suhk,suhv->shkv", key_dec, value, preferred_element_type=jnp.float32)
    unit_decay = jnp.ones_like(block_fac)
    zero_state = jnp.zeros_like(local_state)
    prior_parts = entering((block_fac, local_state), "seq", chain_join, (unit_decay, zero_state))
    prior_low = prior_parts[1].astype(jnp.bfloat16)
    query_dec = (query_rot * query_fac[None, :, :, None]).astype(jnp.bfloat16)
    mixed = intra + jnp.einsum(
        "sthk,shkv->sthv", query_dec, prior_low, preferred_element_type=jnp.float32
    )
    gated = (
        gated_mix(swish_pre, mixed)
        .astype(jnp.bfloat16)
        .reshape(seq_count, block_len, heads_local * DV)
    )
    picked = gated
    attn_out = lax.psum_scatter(
        jnp.dot(picked, output_weight, preferred_element_type=jnp.float32),
        "tp",
        scatter_dimension=0,
        tiled=True,
    )
    hidden_res = inputs_full + attn_out
    normed_two = layer_norm(hidden_res, mlp_gain, mlp_bias).astype(jnp.bfloat16)
    gathered_two = lax.all_gather(normed_two, "tp", axis=0, tiled=True)
    flat_two = gathered_two.reshape(row_total, model_width)
    gate = jnp.dot(flat_two, gate_weight, preferred_element_type=jnp.float32)
    upper = jnp.dot(flat_two, up_weight, preferred_element_type=jnp.float32)
    hidden = gated_mlp(gate, upper).astype(jnp.bfloat16)
    hidden_seq = hidden.reshape(seq_count, block_len, hidden.shape[1])
    picked = hidden_seq
    mlp_out = lax.psum_scatter(
        jnp.dot(picked, down_weight, preferred_element_type=jnp.float32).astype(jnp.bfloat16),
        "tp",
        scatter_dimension=0,
        tiled=True,
    ).astype(jnp.float32)
    outputs = (hidden_res + mlp_out).astype(jnp.bfloat16)
    grad_all = lax.all_gather(output_grad, "tp", axis=0, tiled=True)
    grad_flat = grad_all.reshape(row_total, model_width)
    down_grad = jnp.einsum("nf,nd->fd", hidden, grad_flat, preferred_element_type=jnp.float32)
    hidden_grad = jnp.einsum(
        "nd,fd->nf", grad_flat, down_weight, preferred_element_type=jnp.float32
    )
    _, pull_mlp = jax.vjp(gated_mlp, gate, upper)
    gate_back, upper_back = pull_mlp(hidden_grad)
    gate_low = gate_back.astype(jnp.bfloat16)
    upper_low = upper_back.astype(jnp.bfloat16)
    gate_grad = jnp.einsum("nd,nf->df", flat_two, gate_low, preferred_element_type=jnp.float32)
    up_grad = jnp.einsum("nd,nf->df", flat_two, upper_low, preferred_element_type=jnp.float32)
    gate_seq = gate_low.reshape(seq_count, block_len, gate_low.shape[1])
    upper_seq = upper_low.reshape(seq_count, block_len, upper_low.shape[1])
    normed_two_grad = lax.psum_scatter(
        (
            jnp.einsum("scf,df->scd", gate_seq, gate_weight, preferred_element_type=jnp.float32)
            + jnp.einsum("scf,df->scd", upper_seq, up_weight, preferred_element_type=jnp.float32)
        ).astype(jnp.bfloat16),
        "tp",
        scatter_dimension=0,
        tiled=True,
    ).astype(jnp.float32)
    _, pull_two = jax.vjp(layer_norm, hidden_res, mlp_gain, mlp_bias)
    res_back, mlpgain_part, mlpbias_part = pull_two(normed_two_grad)
    res_grad = output_grad.astype(jnp.float32) + res_back
    res_all = lax.all_gather(res_grad.astype(jnp.bfloat16), "tp", axis=0, tiled=True)
    res_flat = res_all.reshape(row_total, model_width)
    gated_flat = gated.reshape(row_total, heads_local * DV)
    mixer_grad = jnp.einsum("ne,nd->ed", gated_flat, res_flat, preferred_element_type=jnp.float32)
    gated_back = jnp.einsum(
        "nd,ed->ne", res_flat, output_weight, preferred_element_type=jnp.float32
    ).reshape(seq_count, block_len, heads_local, DV)
    _, pull_mix = jax.vjp(gated_mix, swish_pre, mixed)
    swish_back, mixed_back = pull_mix(gated_back)
    swish_low = swish_back.astype(jnp.bfloat16)
    mixed_low = mixed_back.astype(jnp.bfloat16)
    scores_back = jnp.einsum(
        "sthv,suhv->shtu", mixed_low, value, preferred_element_type=jnp.float32
    )
    raw_low = (scores_back * decay_mat[None]).astype(jnp.bfloat16)
    prior_back = jnp.einsum(
        "sthk,sthv->shkv", query_dec, mixed_low, preferred_element_type=jnp.float32
    )
    later_parts = prefix((block_fac, prior_back), "seq", chain_join, (unit_decay, zero_state))
    later_low = later_parts[1].astype(jnp.bfloat16)
    query_rot_back = (
        jnp.einsum("shtu,suhk->sthk", raw_low, key_rot, preferred_element_type=jnp.float32)
        + jnp.einsum("sthv,shkv->sthk", mixed_low, prior_low, preferred_element_type=jnp.float32)
        * query_fac[None, :, :, None]
    )
    key_rot_back = (
        jnp.einsum("shtu,sthk->suhk", raw_low, query_rot, preferred_element_type=jnp.float32)
        + jnp.einsum("suhv,shkv->suhk", value, later_low, preferred_element_type=jnp.float32)
        * key_fac[None, :, :, None]
    )
    value_low = (
        jnp.einsum("shtu,sthv->suhv", scores, mixed_low, preferred_element_type=jnp.float32)
        + jnp.einsum("suhk,shkv->suhv", key_dec, later_low, preferred_element_type=jnp.float32)
    ).astype(jnp.bfloat16)
    _, pull_rot = jax.vjp(lambda values: rotation(values, angles), query)
    query_low = (
        pull_rot(query_rot_back)[0]
        .astype(jnp.bfloat16)
        .reshape(seq_count, block_len, heads_local * DK)
    )
    key_low = (
        pull_rot(key_rot_back)[0]
        .astype(jnp.bfloat16)
        .reshape(seq_count, block_len, heads_local * DK)
    )
    value_seq = value_low.reshape(seq_count, block_len, heads_local * DV)
    swish_seq = swish_low.reshape(seq_count, block_len, heads_local * DV)
    query_grad = jnp.einsum(
        "nd,ne->de",
        flat_one,
        query_low.reshape(row_total, heads_local * DK),
        preferred_element_type=jnp.float32,
    )
    key_grad = jnp.einsum(
        "nd,ne->de",
        flat_one,
        key_low.reshape(row_total, heads_local * DK),
        preferred_element_type=jnp.float32,
    )
    value_grad = jnp.einsum(
        "nd,ne->de",
        flat_one,
        value_seq.reshape(row_total, heads_local * DV),
        preferred_element_type=jnp.float32,
    )
    swish_grad = jnp.einsum(
        "nd,ne->de",
        flat_one,
        swish_seq.reshape(row_total, heads_local * DV),
        preferred_element_type=jnp.float32,
    )
    total = jnp.zeros((local_seqs * lax.axis_size("tp"), block_len, model_width), jnp.float32)
    for source, weight in (
        (query_low, query_weight),
        (key_low, key_weight),
        (value_seq, value_weight),
        (swish_seq, swish_weight),
    ):
        picked = source
        total = total + jnp.einsum(
            "sce,de->scd", picked, weight, preferred_element_type=jnp.float32
        )
    normed_one_grad = lax.psum_scatter(
        total.astype(jnp.bfloat16), "tp", scatter_dimension=0, tiled=True
    ).astype(jnp.float32)
    _, pull_one = jax.vjp(layer_norm, inputs_full, attn_gain, attn_bias)
    input_back, attngain_part, attnbias_part = pull_one(normed_one_grad)
    input_grad = (res_grad + input_back).astype(jnp.bfloat16)
    attngain_grad, attnbias_grad, mlpgain_grad, mlpbias_grad = (
        lax.psum_scatter(attngain_part, ("seq", "tp"), scatter_dimension=0, tiled=True),
        lax.psum_scatter(attnbias_part, ("seq", "tp"), scatter_dimension=0, tiled=True),
        lax.psum_scatter(mlpgain_part, ("seq", "tp"), scatter_dimension=0, tiled=True),
        lax.psum_scatter(mlpbias_part, ("seq", "tp"), scatter_dimension=0, tiled=True),
    )
    query_grad, key_grad, value_grad, swish_grad, mixer_grad, gate_grad, up_grad, down_grad = (
        lax.psum_scatter(
            query_grad.astype(jnp.bfloat16), "seq", scatter_dimension=0, tiled=True
        ).astype(jnp.float32),
        lax.psum_scatter(
            key_grad.astype(jnp.bfloat16), "seq", scatter_dimension=0, tiled=True
        ).astype(jnp.float32),
        lax.psum_scatter(
            value_grad.astype(jnp.bfloat16), "seq", scatter_dimension=0, tiled=True
        ).astype(jnp.float32),
        lax.psum_scatter(
            swish_grad.astype(jnp.bfloat16), "seq", scatter_dimension=0, tiled=True
        ).astype(jnp.float32),
        lax.psum_scatter(
            mixer_grad.astype(jnp.bfloat16), "seq", scatter_dimension=1, tiled=True
        ).astype(jnp.float32),
        lax.psum_scatter(
            gate_grad.astype(jnp.bfloat16), "seq", scatter_dimension=0, tiled=True
        ).astype(jnp.float32),
        lax.psum_scatter(
            up_grad.astype(jnp.bfloat16), "seq", scatter_dimension=0, tiled=True
        ).astype(jnp.float32),
        lax.psum_scatter(
            down_grad.astype(jnp.bfloat16), "seq", scatter_dimension=1, tiled=True
        ).astype(jnp.float32),
    )
    return (
        outputs,
        input_grad,
        query_grad,
        key_grad,
        value_grad,
        swish_grad,
        mixer_grad,
        gate_grad,
        up_grad,
        down_grad,
        attngain_grad,
        attnbias_grad,
        mlpgain_grad,
        mlpbias_grad,
    )


def solution(mesh):
    return jax.shard_map(
        shards,
        mesh=mesh,
        in_specs=(
            P("tp", "seq", None),
            P(None, "tp"),
            P(None, "tp"),
            P(None, "tp"),
            P(None, "tp"),
            P("tp", None),
            P(None, "tp"),
            P(None, "tp"),
            P("tp", None),
            P(),
            P(),
            P(),
            P(),
            P("tp", "seq", None),
        ),
        out_specs=(
            P("tp", "seq", None),
            P("tp", "seq", None),
            P("seq", "tp"),
            P("seq", "tp"),
            P("seq", "tp"),
            P("seq", "tp"),
            P("tp", "seq"),
            P("seq", "tp"),
            P("seq", "tp"),
            P("tp", "seq"),
            P(("seq", "tp")),
            P(("seq", "tp")),
            P(("seq", "tp")),
            P(("seq", "tp")),
        ),
        check_vma=False,
    )
```

profile of v0, /device:TPU:0, one launch (start us, length us, event | category | flops | bytes accessed | tf_op | source)
XLA Modules:
  0.0 1264.1 jit_solution(1749934066752129977)
XLA Ops:
  19.3 31.0 %all-gather.11.cloned.1.call-done = bf16[4,128,2048]{2,1,0:T(8,128)(2,1)} async-done(((bf16[1,128,2048]{2,1,0:T(8,128)(2,1)}), bf16[4,128,2048]{2,1,0:T(8,128)(2,1)}) %all-gather.11.cloned.1.call-update) | async-done | bytes 2097168 | tf_op jit(solution)/shard_map/all_gather | solution.py:103
  65.1 11.7 all-gather.2
  76.9 7.1 copy.149
  84.6 269.2 %all-gather.19.cloned.1.call-done = f32[32,2,256,512]{3,2,1,0:T(8,128)} async-done(((f32[4,2,256,512]{3,2,1,0:T(8,128)}), f32[32,2,256,512]{3,2,1,0:T(8,128)}) %all-gather.19.cloned.1.call-update) | async-done | bytes 33554448 | tf_op jit(solution)/shard_map/all_gather | solution.py:15
  367.6 6.6 fusion.10
  374.8 95.8 %reduce-scatter.37.cloned.1.call-done = f32[1,128,2048]{2,1,0:T(8,128)} async-done(((f32[4,128,2048]{2,1,0:T(8,128)}), f32[1,128,2048]{2,1,0:T(8,128)}) %reduce-scatter.37.cloned.1.call-update) | async-done | bytes 1048592
  473.9 33.7 %all-gather.15.cloned.1.call-done = bf16[4,128,2048]{2,1,0:T(8,128)(2,1)} async-done(((bf16[1,128,2048]{2,1,0:T(8,128)(2,1)}), bf16[4,128,2048]{2,1,0:T(8,128)(2,1)}) %all-gather.15.cloned.1.call-update) | async-done | bytes 2097168 | tf_op jit(solution)/shard_map/all_gather | solution.py:178
  507.6 6.5 fusion.89
  514.2 30.9 %all-gather.13.cloned.1.call-done = bf16[4,128,2048]{2,1,0:T(8,128)(2,1)} async-done(((bf16[1,128,2048]{2,1,0:T(8,128)(2,1)}), bf16[4,128,2048]{2,1,0:T(8,128)(2,1)}) %all-gather.13.cloned.1.call-update) | async-done | bytes 2097168 | tf_op jit(solution)/shard_map/all_gather | solution.py:164
  561.8 6.2 fusion.14
  568.1 28.8 %reduce-scatter.41.cloned.1.call-done = bf16[1,128,2048]{2,1,0:T(8,128)(2,1)} async-done(((bf16[4,128,2048]{2,1,0:T(8,128)(2,1)}), bf16[1,128,2048]{2,1,0:T(8,128)(2,1)}) %reduce-scatter.41.cloned.1.call-update) | async-done | bytes 524304
  598.9 36.1 %reduce-scatter.39.cloned.1.call-done = bf16[1,128,2048]{2,1,0:T(8,128)(2,1)} async-done(((bf16[4,128,2048]{2,1,0:T(8,128)(2,1)}), bf16[1,128,2048]{2,1,0:T(8,128)(2,1)}) %reduce-scatter.39.cloned.1.call-update) | async-done | bytes 524304
  640.5 35.3 %all-gather.17.cloned.1.call-done = bf16[4,128,2048]{2,1,0:T(8,128)(2,1)} async-done(((bf16[1,128,2048]{2,1,0:T(8,128)(2,1)}), bf16[4,128,2048]{2,1,0:T(8,128)(2,1)}) %all-gather.17.cloned.1.call-update) | async-done | bytes 2097168 | tf_op jit(solution)/shard_map/all_gather | solution.py:204
  675.8 6.4 multiply_reduce_fusion
  689.3 6.0 convolution_convert_fusion.2
  696.6 6.3 convolution_convert_fusion.1
  704.2 6.0 convolution_convert_fusion
  717.4 12.5 all-gather.3
  750.8 88.6 %all-gather.21.cloned.1.call-done = bf16[32,2,256,512]{3,2,1,0:T(8,128)(2,1)} async-done(((bf16[4,2,256,512]{3,2,1,0:T(8,128)(2,1)}), bf16[32,2,256,512]{3,2,1,0:T(8,128)(2,1)}) %all-gather.21.cloned.1.call-update) | async-done | bytes 16777232 | tf_op jit(solution)/shard_map/all_gather | solution.py:31
  841.9 55.7 %while.27 = (s32[]{:T(128)}, f32[4,2,256,512]{3,2,1,0:T(8,128)}, s32[]{:T(128)}, bf16[8,2]{0,1:T(2,128)(2,1)}, bf16[8,4,2,256,512]{4,3,2,1,0:T(8,128)(2,1)}, /*index=5*/s32[]{:T(128)}, s32[]{:T(128)}, s32[]{:T(128)}, s32[]{:T(128)}) while((s32[]{:T(128)}, f32[4,2,256,512]{3,2,1,0:T(8,128)}, s32[]{:T(128)}, bf16[8,2]{0,1:T(2,128)(2,1)}, ...), condition=%wide.region_16.17_spmd, body=%wide.region_15.16_spmd.sunk | while | flops 3145736 | bytes 10485943 | solution.py:46
  843.9 6.2 convert_add_fusion.4
  852.2 5.9 convert_add_fusion.4
  860.1 5.9 convert_add_fusion.4
  868.0 5.9 convert_add_fusion.4
  876.0 5.9 convert_add_fusion.4
  942.5 48.4 %reduce-scatter.35.cloned.1.call-done = bf16[1024,256]{1,0:T(8,128)(2,1)} async-done(((bf16[1024,2048]{1,0:T(8,128)(2,1)}), bf16[1024,256]{1,0:T(8,128)(2,1)}) %reduce-scatter.35.cloned.1.call-update) | async-done | bytes 524304 | tf_op jit(solution)/shard_map/reduce_scatter | solution.py:320
  993.0 48.6 %reduce-scatter.29.cloned.1.call-done = bf16[1024,256]{1,0:T(8,128)(2,1)} async-done(((bf16[1024,2048]{1,0:T(8,128)(2,1)}), bf16[1024,256]{1,0:T(8,128)(2,1)}) %reduce-scatter.29.cloned.1.call-update) | async-done | bytes 524304 | tf_op jit(solution)/shard_map/reduce_scatter | solution.py:311
  1043.8 48.5 %reduce-scatter.27.cloned.1.call-done = bf16[256,1024]{1,0:T(8,128)(2,1)} async-done(((bf16[2048,1024]{1,0:T(8,128)(2,1)}), bf16[256,1024]{1,0:T(8,128)(2,1)}) %reduce-scatter.27.cloned.1.call-update) | async-done | bytes 524304 | tf_op jit(solution)/shard_map/reduce_scatter | solution.py:308
  1094.4 34.4 %reduce-scatter.43.cloned.1.call-done = bf16[1,128,2048]{2,1,0:T(8,128)(2,1)} async-done(((bf16[4,128,2048]{2,1,0:T(8,128)(2,1)}), bf16[1,128,2048]{2,1,0:T(8,128)(2,1)}) %reduce-scatter.43.cloned.1.call-update) | async-done | bytes 524304
  1131.9 40.2 %all-reduce.12 = (f32[2048]{0:T(1024)S(1)}, f32[2048]{0:T(1024)S(1)}, f32[2048]{0:T(1024)S(1)}, f32[2048]{0:T(1024)S(1)}) all-reduce(f32[2048]{0:T(1024)S(1)} %get-tuple-element.176, f32[2048]{0:T(1024)S(1)} %get-tuple-element.179, f32[2048]{0:T(1024)S(1)} %get-tuple-element.174, ...), channel_id=16, replica_groups=mesh['seq'=8,'tp'=4] {'seq','tp'}, use_global_device_ids=true, to_apply=%region_29.30.clone | all-reduce | flops 8192 | bytes 65536
  1176.2 28.0 %reduce-scatter.23.cloned.1.call-done = bf16[256,512]{1,0:T(8,128)(2,1)} async-done(((bf16[2048,512]{1,0:T(8,128)(2,1)}), bf16[256,512]{1,0:T(8,128)(2,1)}) %reduce-scatter.23.cloned.1.call-update) | async-done | bytes 262160 | tf_op jit(solution)/shard_map/reduce_scatter | solution.py:302
  1207.4 47.5 %reduce-scatter.25.cloned.1.call-done = bf16[256,1024]{1,0:T(8,128)(2,1)} async-done(((bf16[2048,1024]{1,0:T(8,128)(2,1)}), bf16[256,1024]{1,0:T(8,128)(2,1)}) %reduce-scatter.25.cloned.1.call-update) | async-done | bytes 524304 | tf_op jit(solution)/shard_map/reduce_scatter | solution.py:305
  (308 shorter events, 198.2 us)
Async XLA Ops:
  7.2 43.1 %all-gather.11.cloned.1.call-start = ((), (), s32[]{:S(2)}) async-start(), calls=%async_computation.12 | async-start | bytes 2621440 | tf_op jit(solution)/shard_map/all_gather | solution.py:103
  12.2 341.6 %all-gather.19.cloned.1.call-start = ((), (), s32[]{:S(2)}) async-start(), calls=%async_computation.24 | async-start | bytes 37748736 | tf_op jit(solution)/shard_map/all_gather | solution.py:15
  19.3 337.3 %copy-start.42 = (f32[128,2]{0,1:T(2,128)}, f32[128,2]{0,1:T(2,128)S(1)}, u32[]{:S(2)}) copy-start(f32[128,2]{0,1:T(2,128)S(1)} %get-tuple-element.232) | copy-start | bytes 3076
  56.2 303.0 %copy-start.4 = (bf16[4,128,2,512]{3,2,1,0:T(2,128)(2,1)}, bf16[4,128,2,512]{3,2,1,0:T(2,128)(2,1)S(1)}, u32[]{:S(2)}) copy-start(bf16[4,128,2,512]{3,2,1,0:T(2,128)(2,1)S(1)} %reshape.406) | copy-start | bytes 3145732
  62.2 294.3 %copy-start.6 = (bf16[4,128,2,256]{3,1,2,0:T(8,128)(2,1)}, bf16[4,128,2,256]{3,1,2,0:T(8,128)(2,1)S(1)}, u32[]{:S(2)}) copy-start(bf16[4,128,2,256]{3,1,2,0:T(8,128)(2,1)S(1)} %get-tuple-element.224) | copy-start | bytes 1572868
  65.1 405.6 %reduce-scatter.37.cloned.1.call-start = ((), (), s32[]{:S(2)}) async-start(), calls=%async_computation.26 | async-start | bytes 5242880
  84.3 272.1 %copy-start.34 = (f32[2,128,128]{2,1,0:T(8,128)}, f32[2,128,128]{2,1,0:T(8,128)S(1)}, u32[]{:S(2)}) copy-start(f32[2,128,128]{2,1,0:T(8,128)S(1)} %power_select_fusion) | copy-start | bytes 393220
  374.2 96.5 %copy-start.1 = (bf16[1,128,2048]{2,1,0:T(8,128)(2,1)S(1)}, bf16[1,128,2048]{2,1,0:T(8,128)(2,1)}, u32[]{:S(2)}) copy-start(bf16[1,128,2048]{2,1,0:T(8,128)(2,1)} %param.18) | copy-start | bytes 1572868
  374.2 98.2 %copy-start.36 = (f32[2048]{0:T(1024)S(1)}, f32[2048]{0:T(1024)}, u32[]{:S(2)}) copy-start(f32[2048]{0:T(1024)} %param.29) | copy-start | bytes 24580
  374.2 98.2 %copy-start.47 = (f32[2048]{0:T(1024)S(1)}, f32[2048]{0:T(1024)}, u32[]{:S(2)}) copy-start(f32[2048]{0:T(1024)} %param.30) | copy-start | bytes 24580
  374.2 133.4 %all-gather.15.cloned.1.call-start = ((), (), s32[]{:S(2)}) async-start(), calls=%async_computation.14 | async-start | bytes 2621440 | tf_op jit(solution)/shard_map/all_gather | solution.py:178
  374.8 170.3 %all-gather.13.cloned.1.call-start = ((), (), s32[]{:S(2)}) async-start(), calls=%async_computation.13 | async-start | bytes 2621440 | tf_op jit(solution)/shard_map/all_gather | solution.py:164
  473.5 123.4 %reduce-scatter.41.cloned.1.call-start = ((), (), s32[]{:S(2)}) async-start(), calls=%async_computation.28 | async-start | bytes 2621440
  561.5 73.5 %reduce-scatter.39.cloned.1.call-start = ((), (), s32[]{:S(2)}) async-start(), calls=%async_computation.27 | async-start | bytes 2621440
  568.0 107.8 %all-gather.17.cloned.1.call-start = ((), (), s32[]{:S(2)}) async-start(), calls=%async_computation.15 | async-start | bytes 2621440 | tf_op jit(solution)/shard_map/all_gather | solution.py:204
  640.5 198.9 %all-gather.21.cloned.1.call-start = ((), (), s32[]{:S(2)}) async-start(), calls=%async_computation.25 | async-start | bytes 18874368 | tf_op jit(solution)/shard_map/all_gather | solution.py:31
  688.1 247.3 %reduce-scatter.31.cloned.1.call-start = ((), (), s32[]{:S(2)}) async-start(), calls=%async_computation.21 | async-start | bytes 4718592 | tf_op jit(solution)/shard_map/reduce_scatter | solution.py:314
  695.3 245.1 %reduce-scatter.33.cloned.1.call-start = ((), (), s32[]{:S(2)}) async-start(), calls=%async_computation.22 | async-start | bytes 4718592 | tf_op jit(solution)/shard_map/reduce_scatter | solution.py:317
  703.0 288.0 %reduce-scatter.35.cloned.1.call-start = ((), (), s32[]{:S(2)}) async-start(), calls=%async_computation.23 | async-start | bytes 4718592 | tf_op jit(solution)/shard_map/reduce_scatter | solution.py:320
  710.2 331.4 %reduce-scatter.29.cloned.1.call-start = ((), (), s32[]{:S(2)}) async-start(), calls=%async_computation.20 | async-start | bytes 4718592 | tf_op jit(solution)/shard_map/reduce_scatter | solution.py:311
  717.4 374.9 %reduce-scatter.27.cloned.1.call-start = ((), (), s32[]{:S(2)}) async-start(), calls=%async_computation.19 | async-start | bytes 4718592 | tf_op jit(solution)/shard_map/reduce_scatter | solution.py:308
  740.4 388.4 %reduce-scatter.43.cloned.1.call-start = ((), (), s32[]{:S(2)}) async-start(), calls=%async_computation.29 | async-start | bytes 2621440
  917.7 256.7 %reduce-scatter.21.cloned.1.call-start = ((), (), s32[]{:S(2)}) async-start(), calls=%async_computation.16 | async-start | bytes 2359296 | tf_op jit(solution)/shard_map/reduce_scatter | solution.py:299
  922.0 282.2 %reduce-scatter.23.cloned.1.call-start = ((), (), s32[]{:S(2)}) async-start(), calls=%async_computation.17 | async-start | bytes 2359296 | tf_op jit(solution)/shard_map/reduce_scatter | solution.py:302
  927.2 327.6 %reduce-scatter.25.cloned.1.call-start = ((), (), s32[]{:S(2)}) async-start(), calls=%async_computation.18 | async-start | bytes 4718592 | tf_op jit(solution)/shard_map/reduce_scatter | solution.py:305
  942.5 186.2 %copy-start.35 = (f32[2048]{0:T(1024)S(1)}, f32[2048]{0:T(1024)}, u32[]{:S(2)}) copy-start(f32[2048]{0:T(1024)} %param.27) | copy-start | bytes 24580
  942.5 186.2 %copy-start.46 = (f32[128]{0:T(128)S(1)}, f32[128]{0:T(128)}, u32[]{:S(2)}) copy-start(f32[128]{0:T(128)} %copy-done.45) | copy-start | bytes 1540
  993.0 137.2 %copy-start.53 = (f32[128]{0:T(128)S(1)}, f32[128]{0:T(128)}, u32[]{:S(2)}) copy-start(f32[128]{0:T(128)} %copy-done.52) | copy-start | bytes 1540
  993.0 137.2 %copy-start.49 = (f32[128]{0:T(128)S(1)}, f32[128]{0:T(128)}, u32[]{:S(2)}) copy-start(f32[128]{0:T(128)} %copy-done.48) | copy-start | bytes 1540
  1094.4 111.7 %copy-start.10 = (f32[1,128,2048]{2,1,0:T(8,128)S(1)}, f32[1,128,2048]{2,1,0:T(8,128)}, u32[]{:S(2)}) copy-start(f32[1,128,2048]{2,1,0:T(8,128)} %copy-done.9) | copy-start | bytes 3145732
  1094.4 111.7 %copy-start.16 = (bf16[1,128,2048]{2,1,0:T(8,128)(2,1)S(1)}, bf16[1,128,2048]{2,1,0:T(8,128)(2,1)}, u32[]{:S(2)}) copy-start(bf16[1,128,2048]{2,1,0:T(8,128)(2,1)} %param.31) | copy-start | bytes 1572868
  1094.4 111.7 %copy-start.51 = (f32[128]{0:T(128)S(1)}, f32[128]{0:T(128)}, u32[]{:S(2)}) copy-start(f32[128]{0:T(128)} %copy-done.50) | copy-start | bytes 1540
  (56 other events, 511.3 us)
Sparse Core Ops, SparseCore 0:
  12.3 37.8 all-gather.10
  65.2 288.5 all-gather.18
  374.3 96.3 reduce-scatter.36
  472.4 35.1 all-gather.14
  509.9 35.1 all-gather.12
  561.7 35.1 reduce-scatter.40
  599.8 35.1 reduce-scatter.38
  640.6 35.1 all-gather.16
  688.2 151.1 all-gather.20
  841.5 48.0 reduce-scatter.30
  892.0 48.3 reduce-scatter.32
  942.5 48.3 reduce-scatter.34
  993.2 48.3 reduce-scatter.28
  1043.8 48.3 reduce-scatter.26
  1095.1 33.6 reduce-scatter.42
  1130.9 36.0 reduce-scatter.20
  1169.2 35.0 reduce-scatter.22
  1206.4 48.4 reduce-scatter.24
where the time goes:
time: 1270 us; the launch traced here: 1260 us
  waiting for transfers between devices  909 us (72%)
  matrix products  127 us (10%)
  other arithmetic  86.4 us (7%)
  blocking collectives  64.4 us (5%)
  local copies, waits for them, and re-layouts  59.7 us (5%)
  between operations  15.4 us (1%)
    all_gather x1, waiting for transfers between devices, entering(): gathered = jax.tree.map(lambda a: lax.all_gather(a, axis), part)  269 us
    unnamed x22, waiting for transfers between devices  196 us
    all_gather x1, waiting for transfers between devices, prefix(): lax.all_gather(a.astype(kind), axis)  88.6 us
    reduce_scatter x1, waiting for transfers between devices, shards(): lax.psum_scatter(mixer_grad.astype(jnp.bfloat16), 'seq', scatter_dimensio...  48.6 us
    reduce_scatter x1, waiting for transfers between devices, shards(): lax.psum_scatter(swish_grad.astype(jnp.bfloat16), 'seq', scatter_dimensio...  48.5 us
    reduce_scatter x1, waiting for transfers between devices, shards(): lax.psum_scatter(down_grad.astype(jnp.bfloat16), 'seq', scatter_dimension...  48.4 us
    reduce_scatter x1, waiting for transfers between devices, shards(): lax.psum_scatter(value_grad.astype(jnp.bfloat16), 'seq', scatter_dimensio...  47.5 us
    add x7, other arithmetic, chain_join(): later[0][None, :, None, None] * earlier[1] + later[1]  41.7 us
  transfers between devices with their start and end apart: 18, of which 16 were waited for; matrix products, arithmetic and copies ran while one was open for 14% of the time, Pallas kernels for 0%

commit v1 on v0

--- a/solution.py
+++ b/solution.py
@@ -1,6 +1,10 @@
+import functools
+
 import jax
 import jax.numpy as jnp
 from jax import lax
+from jax.experimental import pallas as pl
+from jax.experimental.pallas import tpu as pltpu
 from jax.sharding import PartitionSpec as P
 
 DK = 256
@@ -8,42 +12,282 @@
 
 
 EPS = 1e-05
-
-
-def entering(part, axis, combine, identity):
-    place = lax.axis_index(axis)
-    gathered = jax.tree.map(lambda a: lax.all_gather(a, axis), part)
-    state = jax.tree.map(lambda a, e: jnp.zeros_like(a) + jnp.asarray(e, a.dtype), part, identity)
-
-    def entering_one(turn, state):
-        return combine(
-            state, jax.tree.map(lambda a: lax.dynamic_index_in_dim(a, turn, 0, False), gathered)
-        )
-
-    return lax.fori_loop(0, place, entering_one, state)
-
-
-def prefix(value, axis, join, neutral):
-    count = lax.axis_size(axis)
-    place = lax.axis_index(axis)
-    ahead = count - 1 - place
-    gathered = jax.tree.map(
-        lambda a, kind: lax.all_gather(a.astype(kind), axis), value, (jnp.bfloat16, jnp.bfloat16)
-    )
-    state = jax.tree.map(lambda a, e: jnp.zeros_like(a) + jnp.asarray(e, a.dtype), value, neutral)
-
-    def prefix_one(turn, state):
-        source = count - 1 - turn
-        return join(
-            state,
-            jax.tree.map(
-                lambda a, own: lax.dynamic_index_in_dim(a, source, 0, False).astype(own.dtype),
-                gathered,
-                value,
-            ),
-        )
-
-    return lax.fori_loop(0, ahead, prefix_one, state)
+MESH = pl.DeviceIdType.MESH
+BF = jnp.bfloat16
+F32 = jnp.float32
+VMEM_LIMIT = 60 * 1024 * 1024
+
+
+def remote(src, dst, ssem, rsem, slot, dev):
+    return pltpu.make_async_remote_copy(
+        src_ref=src,
+        dst_ref=dst,
+        send_sem=ssem.at[slot],
+        recv_sem=rsem.at[slot],
+        device_id=dev,
+        device_id_type=MESH,
+    )
+
+
+def greet(devs):
+    barrier = pltpu.get_barrier_semaphore()
+    for dev in devs:
+        pl.semaphore_signal(barrier, inc=1, device_id=dev, device_id_type=MESH)
+    pl.semaphore_wait(barrier, len(devs))
+
+
+def params(cid):
+    return pltpu.CompilerParams(
+        collective_id=cid, has_side_effects=True, vmem_limit_bytes=VMEM_LIMIT
+    )
+
+
+def gather_kernel(n, x_ref, o_ref, ssem, rsem):
+    s = lax.axis_index("seq")
+    t = lax.axis_index("tp")
+    b, length, _ = x_ref.shape
+    if n == 4:
+        px, py = t + 1 - 2 * (t % 2), (t + 2) % 4
+        half = length // 2
+        lo, hi = pl.ds(0, half), pl.ds(half, half)
+        mine, from_x, from_y = pl.ds(t * b, b), pl.ds(px * b, b), pl.ds(py * b, b)
+        dx, dy = (s, px), (s, py)
+        greet([dx, dy])
+        first = [
+            remote(x_ref.at[:, lo], o_ref.at[mine, lo], ssem, rsem, 0, dx),
+            remote(x_ref.at[:, hi], o_ref.at[mine, hi], ssem, rsem, 1, dy),
+            remote(x_ref.at[:, hi], o_ref.at[mine, hi], ssem, rsem, 2, dx),
+            remote(x_ref.at[:, lo], o_ref.at[mine, lo], ssem, rsem, 3, dy),
+        ]
+        for copy in first:
+            copy.start()
+        o_ref[mine] = x_ref[...]
+        first[0].wait_recv()
+        relay_x = remote(o_ref.at[from_x, lo], o_ref.at[from_x, lo], ssem, rsem, 4, dy)
+        relay_x.start()
+        first[1].wait_recv()
+        relay_y = remote(o_ref.at[from_y, hi], o_ref.at[from_y, hi], ssem, rsem, 5, dx)
+        relay_y.start()
+        first[2].wait_recv()
+        first[3].wait_recv()
+        relay_x.wait_recv()
+        relay_y.wait_recv()
+        for copy in first:
+            copy.wait_send()
+        relay_x.wait_send()
+        relay_y.wait_send()
+    else:
+        peers = [(s, (t + k) % n) for k in range(1, n)]
+        greet(peers)
+        mine = pl.ds(t * b, b)
+        copies = [
+            remote(x_ref, o_ref.at[mine], ssem, rsem, k, dev) for k, dev in enumerate(peers)
+        ]
+        for copy in copies:
+            copy.start()
+        o_ref[mine] = x_ref[...]
+        for copy in copies:
+            copy.wait()
+
+
+def gather_tp(x, cid):
+    n = lax.axis_size("tp")
+    sems = max(6, n - 1)
+    return pl.pallas_call(
+        functools.partial(gather_kernel, n),
+        out_shape=jax.ShapeDtypeStruct((n * x.shape[0],) + x.shape[1:], x.dtype),
+        in_specs=[pl.BlockSpec(memory_space=pltpu.VMEM)],
+        out_specs=pl.BlockSpec(memory_space=pltpu.VMEM),
+        scratch_shapes=[pltpu.SemaphoreType.DMA((sems,)), pltpu.SemaphoreType.DMA((sems,))],
+        compiler_params=params(cid),
+        name=f"gather_tp_{cid}",
+    )(x)
+
+
+def scatter_kernel(n, p_ref, o_ref, near, far, hold, ssem, rsem):
+    s = lax.axis_index("seq")
+    t = lax.axis_index("tp")
+    b, _, width = o_ref.shape
+    if n == 4:
+        px, py, pd = t + 1 - 2 * (t % 2), (t + 2) % 4, 3 - t
+        half = width // 2
+        cols = (pl.ds(0, half), pl.ds(half, half))
+        dx, dy = (s, px), (s, py)
+        greet([dx, dy])
+
+        def own(who, side):
+            return p_ref.at[pl.ds(who * b, b), :, cols[side]]
+
+        steps = []
+        for side, (who, dev) in enumerate(((px, dx), (py, dy))):
+            steps.append(remote(own(pd, side), near.at[side, 1], ssem, rsem, 2 * side, dev))
+            steps.append(remote(own(who, side), near.at[side, 0], ssem, rsem, 2 * side + 1, dev))
+        steps[0].start()
+        steps[2].start()
+        steps[1].start()
+        steps[3].start()
+        later = []
+        for side, (who, dev) in enumerate(((py, dy), (px, dx))):
+            steps[2 * side].wait_recv()
+            total = own(who, side)[...].astype(F32) + near[side, 1].astype(F32)
+            hold[side] = total.astype(BF)
+            copy = remote(hold.at[side], far.at[side], ssem, rsem, 4 + side, dev)
+            copy.start()
+            later.append(copy)
+        for side in range(2):
+            steps[2 * side + 1].wait_recv()
+            partial = own(t, side)[...].astype(F32) + near[side, 0].astype(F32)
+            later[side].wait_recv()
+            o_ref[:, :, cols[side]] = partial + far[side].astype(F32)
+        for copy in steps + later:
+            copy.wait_send()
+    else:
+        peers = [(s, (t + k) % n) for k in range(1, n)]
+        greet(peers)
+        copies = [
+            remote(p_ref.at[pl.ds(((t + k) % n) * b, b)], near.at[k - 1], ssem, rsem, k - 1, (s, (t + k) % n))
+            for k in range(1, n)
+        ]
+        for copy in copies:
+            copy.start()
+        total = p_ref[pl.ds(t * b, b)].astype(F32)
+        for k, copy in enumerate(copies):
+            copy.wait_recv()
+            total = total + near[k].astype(F32)
+        o_ref[...] = total
+        for copy in copies:
+            copy.wait_send()
+
+
+def scatter_tp(parts, cid):
+    n = lax.axis_size("tp")
+    rows, length, width = parts.shape
+    b = rows // n
+    sems = max(6, n - 1)
+    if n == 4:
+        near, far = (2, 2, b, length, width // 2), (2, b, length, width // 2)
+    else:
+        near, far = (n - 1, b, length, width), (1, b, 16, 128)
+    return pl.pallas_call(
+        functools.partial(scatter_kernel, n),
+        out_shape=jax.ShapeDtypeStruct((b, length, width), F32),
+        in_specs=[pl.BlockSpec(memory_space=pltpu.VMEM)],
+        out_specs=pl.BlockSpec(memory_space=pltpu.VMEM),
+        scratch_shapes=[
+            pltpu.VMEM(near, BF),
+            pltpu.VMEM(far, BF),
+            pltpu.VMEM(far, BF),
+            pltpu.SemaphoreType.DMA((sems,)),
+            pltpu.SemaphoreType.DMA((sems,)),
+        ],
+        compiler_params=params(cid),
+        name=f"scatter_tp_{cid}",
+    )(parts)
+
+
+def chain_kernel(chips, heads, flip, fac_ref, l_ref, o_ref, pair, enter, leave, ps, pr, zs, zr, bs, br):
+    s = lax.axis_index("seq")
+    t = lax.axis_index("tp")
+    core = s % 2
+    chip = s // 2
+    pieces = l_ref.shape[0]
+    partner = (s + 1 - 2 * core, t)
+    if flip:
+        first, place, ahead = core == 1, chips - 1 - chip, (s - 2 + 2 * chips) % (2 * chips)
+        behind = (s + 2) % (2 * chips)
+    else:
+        first, place, ahead = core == 0, chip, (s + 2) % (2 * chips)
+        behind = (s - 2 + 2 * chips) % (2 * chips)
+    last = jnp.logical_not(first)
+    barrier = pltpu.get_barrier_semaphore()
+    for dev in (partner, (ahead, t), (behind, t)):
+        pl.semaphore_signal(barrier, inc=1, device_id=dev, device_id_type=MESH)
+    pl.semaphore_wait(barrier, 3)
+
+    def give(p):
+        return remote(l_ref.at[p], pair.at[p], ps, pr, p, partner)
+
+    def back(p):
+        return remote(enter.at[p], o_ref.at[p], bs, br, p, partner)
+
+    def onward(p):
+        return remote(leave.at[p], enter.at[p], zs, zr, p, (ahead, t))
+
+    @pl.when(first)
+    def _():
+        @pl.loop(0, pieces)
+        def _(p):
+            give(p).start()
+
+        @pl.when(place == 0)
+        def _():
+            o_ref[...] = jnp.zeros_like(o_ref)
+
+        @pl.when(place > 0)
+        def _():
+            @pl.loop(0, pieces)
+            def _(p):
+                back(p).wait_recv()
+
+        @pl.loop(0, pieces)
+        def _(p):
+            give(p).wait_send()
+
+    @pl.when(last)
+    def _():
+        @pl.loop(0, pieces)
+        def _(p):
+            fac = fac_ref[p % heads]
+            give(p).wait_recv()
+            early = pair[p].astype(F32)
+            chip_sum = early * fac + l_ref[p].astype(F32)
+
+            @pl.when(place == 0)
+            def _():
+                leave[p] = chip_sum.astype(BF)
+                o_ref[p] = pair[p]
+
+            @pl.when(place > 0)
+            def _():
+                onward(p).wait_recv()
+                back(p).start()
+                came = enter[p].astype(F32)
+                leave[p] = (came * (fac * fac) + chip_sum).astype(BF)
+                o_ref[p] = (came * fac + early).astype(BF)
+
+            @pl.when(place < chips - 1)
+            def _():
+                onward(p).start()
+
+        @pl.loop(0, pieces)
+        def _(p):
+            @pl.when(place > 0)
+            def _():
+                back(p).wait_send()
+
+            @pl.when(place < chips - 1)
+            def _():
+                onward(p).wait_send()
+
+
+def chain_seq(local, fac, flip, cid):
+    shape = local.shape
+    pieces = shape[0] * shape[1]
+    chips = lax.axis_size("seq") // 2
+    out = pl.pallas_call(
+        functools.partial(chain_kernel, chips, shape[1], flip),
+        out_shape=jax.ShapeDtypeStruct((pieces,) + shape[2:], BF),
+        in_specs=[
+            pl.BlockSpec(memory_space=pltpu.SMEM),
+            pl.BlockSpec(memory_space=pltpu.VMEM),
+        ],
+        out_specs=pl.BlockSpec(memory_space=pltpu.VMEM),
+        scratch_shapes=[pltpu.VMEM((pieces,) + shape[2:], BF)] * 3
+        + [pltpu.SemaphoreType.DMA((pieces,))] * 6,
+        compiler_params=params(cid),
+        name=f"chain_{cid}",
+    )(fac, local.astype(BF).reshape((pieces,) + shape[2:]))
+    return out.reshape(shape)
 
 
 def layer_norm(values, gain, bias):
@@ -66,10 +310,6 @@
     sine = jnp.concatenate([sine, sine], -1)[:, None, :]
     turned = jnp.concatenate([-values[..., half_width:], values[..., :half_width]], -1)
     return values * cosine + turned * sine
-
-
-def chain_join(earlier, later):
-    return (earlier[0] * later[0], later[0][None, :, None, None] * earlier[1] + later[1])
 
 
 def gated_mix(swish_pre, mixed):
@@ -100,7 +340,7 @@
     heads_local = query_weight.shape[1] // DK
     inputs_full = inputs.astype(jnp.float32)
     normed_one = layer_norm(inputs_full, attn_gain, attn_bias).astype(jnp.bfloat16)
-    gathered_one = lax.all_gather(normed_one, "tp", axis=0, tiled=True)
+    gathered_one = gather_tp(normed_one, 0)
     seq_count = gathered_one.shape[0]
     row_total = seq_count * block_len
     flat_one = gathered_one.reshape(row_total, model_width)
@@ -139,10 +379,7 @@
     intra = jnp.einsum("shtu,suhv->sthv", scores, value, preferred_element_type=jnp.float32)
     key_dec = (key_rot * key_fac[None, :, :, None]).astype(jnp.bfloat16)
     local_state = jnp.einsum("suhk,suhv->shkv", key_dec, value, preferred_element_type=jnp.float32)
-    unit_decay = jnp.ones_like(block_fac)
-    zero_state = jnp.zeros_like(local_state)
-    prior_parts = entering((block_fac, local_state), "seq", chain_join, (unit_decay, zero_state))
-    prior_low = prior_parts[1].astype(jnp.bfloat16)
+    prior_low = chain_seq(local_state, block_fac, False, 1)
     query_dec = (query_rot * query_fac[None, :, :, None]).astype(jnp.bfloat16)
     mixed = intra + jnp.einsum(
         "sthk,shkv->sthv", query_dec, prior_low, preferred_element_type=jnp.float32
@@ -153,29 +390,23 @@
         .reshape(seq_count, block_len, heads_local * DV)
     )
     picked = gated
-    attn_out = lax.psum_scatter(
-        jnp.dot(picked, output_weight, preferred_element_type=jnp.float32),
-        "tp",
-        scatter_dimension=0,
-        tiled=True,
+    attn_out = scatter_tp(
+        jnp.dot(picked, output_weight, preferred_element_type=jnp.float32).astype(jnp.bfloat16), 2
     )
     hidden_res = inputs_full + attn_out
     normed_two = layer_norm(hidden_res, mlp_gain, mlp_bias).astype(jnp.bfloat16)
-    gathered_two = lax.all_gather(normed_two, "tp", axis=0, tiled=True)
+    gathered_two = gather_tp(normed_two, 3)
     flat_two = gathered_two.reshape(row_total, model_width)
     gate = jnp.dot(flat_two, gate_weight, preferred_element_type=jnp.float32)
     upper = jnp.dot(flat_two, up_weight, preferred_element_type=jnp.float32)
     hidden = gated_mlp(gate, upper).astype(jnp.bfloat16)
     hidden_seq = hidden.reshape(seq_count, block_len, hidden.shape[1])
     picked = hidden_seq
-    mlp_out = lax.psum_scatter(
-        jnp.dot(picked, down_weight, preferred_element_type=jnp.float32).astype(jnp.bfloat16),
-        "tp",
-        scatter_dimension=0,
-        tiled=True,
-    ).astype(jnp.float32)
+    mlp_out = scatter_tp(
+        jnp.dot(picked, down_weight, preferred_element_type=jnp.float32).astype(jnp.bfloat16), 4
+    )
     outputs = (hidden_res + mlp_out).astype(jnp.bfloat16)
-    grad_all = lax.all_gather(output_grad, "tp", axis=0, tiled=True)
+    grad_all = gather_tp(output_grad, 5)
     grad_flat = grad_all.reshape(row_total, model_width)
     down_grad = jnp.einsum("nf,nd->fd", hidden, grad_flat, preferred_element_type=jnp.float32)
     hidden_grad = jnp.einsum(
@@ -189,19 +420,17 @@
     up_grad = jnp.einsum("nd,nf->df", flat_two, upper_low, preferred_element_type=jnp.float32)
     gate_seq = gate_low.reshape(seq_count, block_len, gate_low.shape[1])
     upper_seq = upper_low.reshape(seq_count, block_len, upper_low.shape[1])
-    normed_two_grad = lax.psum_scatter(
+    normed_two_grad = scatter_tp(
         (
             jnp.einsum("scf,df->scd", gate_seq, gate_weight, preferred_element_type=jnp.float32)
             + jnp.einsum("scf,df->scd", upper_seq, up_weight, preferred_element_type=jnp.float32)
         ).astype(jnp.bfloat16),
-        "tp",
-        scatter_dimension=0,
-        tiled=True,
-    ).astype(jnp.float32)
+        6,
+    )
     _, pull_two = jax.vjp(layer_norm, hidden_res, mlp_gain, mlp_bias)
     res_back, mlpgain_part, mlpbias_part = pull_two(normed_two_grad)
     res_grad = output_grad.astype(jnp.float32) + res_back
-    res_all = lax.all_gather(res_grad.astype(jnp.bfloat16), "tp", axis=0, tiled=True)
+    res_all = gather_tp(res_grad.astype(jnp.bfloat16), 7)
     res_flat = res_all.reshape(row_total, model_width)
     gated_flat = gated.reshape(row_total, heads_local * DV)
     mixer_grad = jnp.einsum("ne,nd->ed", gated_flat, res_flat, preferred_element_type=jnp.float32)
@@ -219,8 +448,7 @@
     prior_back = jnp.einsum(
         "sthk,sthv->shkv", query_dec, mixed_low, preferred_element_type=jnp.float32
     )
-    later_parts = prefix((block_fac, prior_back), "seq", chain_join, (unit_decay, zero_state))
-    later_low = later_parts[1].astype(jnp.bfloat16)
+    later_low = chain_seq(prior_back, block_fac, True, 8)
     query_rot_back = (
         jnp.einsum("shtu,suhk->sthk", raw_low, key_rot, preferred_element_type=jnp.float32)
         + jnp.einsum("sthv,shkv->sthk", mixed_low, prior_low, preferred_element_type=jnp.float32)
@@ -283,9 +511,7 @@
         total = total + jnp.einsum(
             "sce,de->scd", picked, weight, preferred_element_type=jnp.float32
         )
-    normed_one_grad = lax.psum_scatter(
-        total.astype(jnp.bfloat16), "tp", scatter_dimension=0, tiled=True
-    ).astype(jnp.float32)
+    normed_one_grad = scatter_tp(total.astype(jnp.bfloat16), 9)
     _, pull_one = jax.vjp(layer_norm, inputs_full, attn_gain, attn_bias)
     input_back, attngain_part, attnbias_part = pull_one(normed_one_grad)
     input_grad = (res_grad + input_back).astype(jnp.bfloat16)

time: 1270 us -> 761 us (0.60)
  waiting for transfers between devices: 909 us -> 225 us
  Pallas kernels: 0 us -> 258 us
  other arithmetic: 86.4 us -> 38.8 us
  blocking collectives: 64.4 us -> 38.4 us
  local copies, waits for them, and re-layouts: 59.7 us -> 45.8 us
    all_gather x6 -> x0, waiting for transfers between devices: 489 us -> none  [the longest x1 269 us: entering(): gathered = jax.tree.map(lambda a: lax.all_gather(a, axis), part)]
    pallas_call x0 -> x10, Pallas kernels: none -> 258 us  [the longest x2 102 us: chain_seq(): pl.pallas_call(functools.partial(chain_kernel, chips, shape[1], flip), ou...]
    unnamed x22 -> x8, waiting for transfers between devices: 196 us -> 0.13 us
    reduce_scatter x1, waiting for transfers between devices: 0.02 us -> 48.6 us  [shards(): lax.psum_scatter(gate_grad.astype(jnp.bfloat16), 'seq', scatter_dimension...]
    reduce_scatter x1, waiting for transfers between devices: 48.4 us -> 0.01 us  [shards(): lax.psum_scatter(down_grad.astype(jnp.bfloat16), 'seq', scatter_dimension...]
    reduce_scatter x1, waiting for transfers between devices: 2.87 us -> 48.6 us  [shards(): lax.psum_scatter(up_grad.astype(jnp.bfloat16), 'seq', scatter_dimension=0...]
    add x7 -> x0, other arithmetic: 41.7 us -> none  [chain_join(): later[0][None, :, None, None] * earlier[1] + later[1]]
    reduce_scatter x1, waiting for transfers between devices: 28 us -> 0.01 us  [shards(): lax.psum_scatter(key_grad.astype(jnp.bfloat16), 'seq', scatter_dimension=...]
  transfers between devices with their start and end apart: 18 -> 8, of which waited for: 16 -> 5; matrix products, arithmetic and copies ran while one was open for 14% -> 10% of each run, Pallas kernels for 0% -> 3%
where the time goes in v1:
time: 761 us; the launch traced here: 751 us
  Pallas kernels  258 us (34%)
  waiting for transfers between devices  225 us (30%)
  matrix products  121 us (16%)
  local copies, waits for them, and re-layouts  45.8 us (6%)
  other arithmetic  38.8 us (5%)
  blocking collectives  38.4 us (5%)
  between operations  23.5 us (3%)
    pallas_call x2, Pallas kernels, chain_seq(): pl.pallas_call(functools.partial(chain_kernel, chips, shape[1], flip), ou...  102 us
    pallas_call x4, Pallas kernels, gather_tp(): pl.pallas_call(functools.partial(gather_kernel, n), out_shape=jax.ShapeDt...  85.8 us
    pallas_call x4, Pallas kernels, scatter_tp(): pl.pallas_call(functools.partial(scatter_kernel, n), out_shape=jax.ShapeD...  69.8 us
    reduce_scatter x1, waiting for transfers between devices, shards(): lax.psum_scatter(gate_grad.astype(jnp.bfloat16), 'seq', scatter_dimension...  48.6 us
    reduce_scatter x1, waiting for transfers between devices, shards(): lax.psum_scatter(up_grad.astype(jnp.bfloat16), 'seq', scatter_dimension=0...  48.6 us
    reduce_scatter x1, waiting for transfers between devices, shards(): lax.psum_scatter(mixer_grad.astype(jnp.bfloat16), 'seq', scatter_dimensio...  48.5 us
    reduce_scatter x1, waiting for transfers between devices, shards(): lax.psum_scatter(swish_grad.astype(jnp.bfloat16), 'seq', scatter_dimensio...  48.4 us
    unnamed x1, blocking collectives  38.4 us
  transfers between devices with their start and end apart: 8, of which 5 were waited for; matrix products, arithmetic and copies ran while one was open for 10% of the time, Pallas kernels for 3%

profile of v1, /device:TPU:0, one launch (start us, length us, event | category | flops | bytes accessed | tf_op | source)
XLA Modules:
  0.0 751.2 jit_solution(1700409423738292246)
XLA Ops:
  13.2 24.3 %gather_tp_0.1 = bf16[4,128,2048]{2,1,0:T(8,128)(2,1)} custom-call(bf16[1,128,2048]{2,1,0:T(8,128)(2,1)} %fusion.55.x_ref), custom_call_target="tpu_custom_call" | custom-call | tf_op jit(solution)/shard_map/gather_tp_0/pallas_call | solution.py:96
  37.5 6.1 convolution_convert_fusion.10
  48.1 4.6 fusion.35
  58.7 21.1 %gather_tp_5.1 = bf16[4,128,2048]{2,1,0:T(8,128)(2,1)} custom-call(bf16[1,128,2048]{2,1,0:T(8,128)(2,1)} %x_ref.1), custom_call_target="tpu_custom_call" | custom-call | tf_op jit(solution)/shard_map/gather_tp_5/pallas_call | solution.py:96
  84.1 11.1 %chain_1.1 = bf16[8,256,512]{2,1,0:T(8,128)(2,1)} custom-call(f32[2]{0:T(128)} %get-tuple-element.62.fac_ref, bf16[8,256,512]{2,1,0:T(8,128)(2,1)} %bitcast.185), custom_call_target="tpu_custom_call" | custom-call | tf_op jit(solution)/shard_map/chain_1/pallas_call | solution.py:277
  98.4 6.5 copy.137
  104.9 7.1 multiply_convert_fusion.2
  114.3 6.2 fusion.14.p_ref
  120.5 14.9 %scatter_tp_2.1 = f32[1,128,2048]{2,1,0:T(8,128)} custom-call(bf16[4,128,2048]{2,1,0:T(8,128)(2,1)} %fusion.14.p_ref), custom_call_target="tpu_custom_call" | custom-call | tf_op jit(solution)/shard_map/scatter_tp_2/pallas_call | solution.py:171
  138.2 20.1 %gather_tp_3.1 = bf16[4,128,2048]{2,1,0:T(8,128)(2,1)} custom-call(bf16[1,128,2048]{2,1,0:T(8,128)(2,1)} %add_convert_fusion.8.x_ref), custom_call_target="tpu_custom_call" | custom-call | tf_op jit(solution)/shard_map/gather_tp_3/pallas_call | solution.py:96
  158.4 5.3 fusion.83
  166.1 5.2 fusion.26
  184.3 14.9 %scatter_tp_4.1 = f32[1,128,2048]{2,1,0:T(8,128)} custom-call(bf16[4,128,2048]{2,1,0:T(8,128)(2,1)} %fusion.17.p_ref), custom_call_target="tpu_custom_call" | custom-call | tf_op jit(solution)/shard_map/scatter_tp_4/pallas_call | solution.py:171
  199.2 5.0 fusion.4
  208.0 17.2 %scatter_tp_6.1 = f32[1,128,2048]{2,1,0:T(8,128)} custom-call(bf16[4,128,2048]{2,1,0:T(8,128)(2,1)} %add_convert_fusion.1.p_ref), custom_call_target="tpu_custom_call" | custom-call | tf_op jit(solution)/shard_map/scatter_tp_6/pallas_call | solution.py:171
  230.1 20.4 %gather_tp_7.1 = bf16[4,128,2048]{2,1,0:T(8,128)(2,1)} custom-call(bf16[1,128,2048]{2,1,0:T(8,128)(2,1)} %fusion.67.x_ref), custom_call_target="tpu_custom_call" | custom-call | tf_op jit(solution)/shard_map/gather_tp_7/pallas_call | solution.py:96
  250.6 6.4 multiply_reduce_fusion
  266.0 91.0 %chain_8.1 = bf16[8,256,512]{2,1,0:T(8,128)(2,1)} custom-call(f32[2]{0:T(128)} %get-tuple-element.62.fac_ref, bf16[8,256,512]{2,1,0:T(8,128)(2,1)} %bitcast.184), custom_call_target="tpu_custom_call" | custom-call | tf_op jit(solution)/shard_map/chain_8/pallas_call | solution.py:277
  367.6 4.2 convolution_convert_fusion.6
  373.4 5.6 convolution_convert_fusion
  385.7 4.4 convolution_convert_fusion.5
  393.0 4.4 convolution_convert_fusion.4
  400.2 4.3 convolution_convert_fusion.3
  405.7 6.0 convolution_convert_fusion.2
  412.9 6.0 convolution_convert_fusion.1
  435.0 22.8 %scatter_tp_9.1 = f32[1,128,2048]{2,1,0:T(8,128)} custom-call(bf16[4,128,2048]{2,1,0:T(8,128)(2,1)} %add_convert_fusion.p_ref), custom_call_target="tpu_custom_call" | custom-call | tf_op jit(solution)/shard_map/scatter_tp_9/pallas_call | solution.py:171
  460.1 38.4 %all-reduce.8 = (f32[2048]{0:T(1024)S(1)}, f32[2048]{0:T(1024)S(1)}, f32[2048]{0:T(1024)S(1)}, f32[2048]{0:T(1024)S(1)}) all-reduce(f32[2048]{0:T(1024)S(1)} %get-tuple-element.16, f32[2048]{0:T(1024)S(1)} %get-tuple-element.19, f32[2048]{0:T(1024)S(1)} %get-tuple-element.14, ...), channel_id=10, replica_groups=mesh['seq'=8,'tp'=4] {'seq','tp'}, use_global_device_ids=true, to_apply=%region_21.22.clone | all-reduce | flops 8192 | bytes 65536
  509.0 30.5 %reduce-scatter.13.cloned.1.call-done = bf16[256,1024]{1,0:T(8,128)(2,1)} async-done(((bf16[2048,1024]{1,0:T(8,128)(2,1)}), bf16[256,1024]{1,0:T(8,128)(2,1)}) %reduce-scatter.13.cloned.1.call-update) | async-done | bytes 524304 | tf_op jit(solution)/shard_map/reduce_scatter | solution.py:531
  541.6 48.4 %reduce-scatter.15.cloned.1.call-done = bf16[256,1024]{1,0:T(8,128)(2,1)} async-done(((bf16[2048,1024]{1,0:T(8,128)(2,1)}), bf16[256,1024]{1,0:T(8,128)(2,1)}) %reduce-scatter.15.cloned.1.call-update) | async-done | bytes 524304 | tf_op jit(solution)/shard_map/reduce_scatter | solution.py:534
  592.1 48.5 %reduce-scatter.17.cloned.1.call-done = bf16[1024,256]{1,0:T(8,128)(2,1)} async-done(((bf16[1024,2048]{1,0:T(8,128)(2,1)}), bf16[1024,256]{1,0:T(8,128)(2,1)}) %reduce-scatter.17.cloned.1.call-update) | async-done | bytes 524304 | tf_op jit(solution)/shard_map/reduce_scatter | solution.py:537
  642.7 48.6 %reduce-scatter.19.cloned.1.call-done = bf16[256,1024]{1,0:T(8,128)(2,1)} async-done(((bf16[2048,1024]{1,0:T(8,128)(2,1)}), bf16[256,1024]{1,0:T(8,128)(2,1)}) %reduce-scatter.19.cloned.1.call-update) | async-done | bytes 524304 | tf_op jit(solution)/shard_map/reduce_scatter | solution.py:540
  693.4 48.6 %reduce-scatter.21.cloned.1.call-done = bf16[256,1024]{1,0:T(8,128)(2,1)} async-done(((bf16[2048,1024]{1,0:T(8,128)(2,1)}), bf16[256,1024]{1,0:T(8,128)(2,1)}) %reduce-scatter.21.cloned.1.call-update) | async-done | bytes 524304 | tf_op jit(solution)/shard_map/reduce_scatter | solution.py:543
  (231 shorter events, 119.4 us)
Async XLA Ops:
  7.2 496.1 %reduce-scatter.9.cloned.1.call-start = ((), (), s32[]{:S(2)}) async-start(), calls=%async_computation.8 | async-start | bytes 2359296 | tf_op jit(solution)/shard_map/reduce_scatter | solution.py:525
  8.6 28.9 %copy-start.44 = (f32[128]{0:T(128)}, f32[128]{0:T(128)S(1)}, u32[]{:S(2)}) copy-start(f32[128]{0:T(128)S(1)} %broadcast_multiply_fusion.4) | copy-start | bytes 1540
  10.4 27.1 %copy-start.47 = (f32[128]{0:T(128)}, f32[128]{0:T(128)S(1)}, u32[]{:S(2)}) copy-start(f32[128]{0:T(128)S(1)} %fusion.73) | copy-start | bytes 1540
  45.6 36.3 %copy-start.6 = (bf16[4,128,2,512]{3,2,1,0:T(2,128)(2,1)}, bf16[4,128,2,512]{3,2,1,0:T(2,128)(2,1)S(1)}, u32[]{:S(2)}) copy-start(bf16[4,128,2,512]{3,2,1,0:T(2,128)(2,1)S(1)} %reshape.382) | copy-start | bytes 3145732
  48.1 4.6 copy-start.19
  58.7 21.8 %copy-start.28 = (f32[4,128,2,256]{3,1,2,0:T(8,128)S(1)}, f32[4,128,2,256]{3,1,2,0:T(8,128)}, u32[]{:S(2)}) copy-start(f32[4,128,2,256]{3,1,2,0:T(8,128)} %fusion.35) | copy-start | bytes 3145732
  81.6 2.5 copy-start.11
  81.6 13.6 %copy-start.9 = (bf16[4,128,2,256]{3,1,2,0:T(8,128)(2,1)}, bf16[4,128,2,256]{3,1,2,0:T(8,128)(2,1)S(1)}, u32[]{:S(2)}) copy-start(bf16[4,128,2,256]{3,1,2,0:T(8,128)(2,1)S(1)} %get-tuple-element.44) | copy-start | bytes 1572868
  120.5 14.9 %copy-start = (bf16[1,128,2048]{2,1,0:T(8,128)(2,1)S(1)}, bf16[1,128,2048]{2,1,0:T(8,128)(2,1)}, u32[]{:S(2)}) copy-start(bf16[1,128,2048]{2,1,0:T(8,128)(2,1)} %param.14) | copy-start | bytes 1572868
  158.4 5.4 copy-start.32
  158.4 5.4 copy-start.52
  166.1 6.2 copy-start.51
  199.1 5.1 copy-start.54
  199.1 5.1 copy-start.57
  250.5 6.5 copy-start.36
  362.3 4.7 copy-start.22
  366.9 138.1 %reduce-scatter.11.cloned.1.call-start = ((), (), s32[]{:S(2)}) async-start(), calls=%async_computation.9 | async-start | bytes 2359296 | tf_op jit(solution)/shard_map/reduce_scatter | solution.py:528
  371.9 135.0 %reduce-scatter.23.cloned.1.call-start = ((), (), s32[]{:S(2)}) async-start(), calls=%async_computation.15 | async-start | bytes 4718592 | tf_op jit(solution)/shard_map/reduce_scatter | solution.py:546
  379.0 160.4 %reduce-scatter.13.cloned.1.call-start = ((), (), s32[]{:S(2)}) async-start(), calls=%async_computation.10 | async-start | bytes 4718592 | tf_op jit(solution)/shard_map/reduce_scatter | solution.py:531
  390.1 199.9 %reduce-scatter.15.cloned.1.call-start = ((), (), s32[]{:S(2)}) async-start(), calls=%async_computation.11 | async-start | bytes 4718592 | tf_op jit(solution)/shard_map/reduce_scatter | solution.py:534
  397.4 243.2 %reduce-scatter.17.cloned.1.call-start = ((), (), s32[]{:S(2)}) async-start(), calls=%async_computation.12 | async-start | bytes 4718592 | tf_op jit(solution)/shard_map/reduce_scatter | solution.py:537
  404.5 286.8 %reduce-scatter.19.cloned.1.call-start = ((), (), s32[]{:S(2)}) async-start(), calls=%async_computation.13 | async-start | bytes 4718592 | tf_op jit(solution)/shard_map/reduce_scatter | solution.py:540
  411.7 330.3 %reduce-scatter.21.cloned.1.call-start = ((), (), s32[]{:S(2)}) async-start(), calls=%async_computation.14 | async-start | bytes 4718592 | tf_op jit(solution)/shard_map/reduce_scatter | solution.py:543
  420.3 4.2 copy-start.20
  424.5 2.5 copy-start.25
  424.5 2.7 copy-start.39
  427.2 2.6 copy-start.55
  435.0 22.9 %copy-start.42 = (f32[2048]{0:T(1024)S(1)}, f32[2048]{0:T(1024)}, u32[]{:S(2)}) copy-start(f32[2048]{0:T(1024)} %param.23) | copy-start | bytes 24580
  435.0 22.9 %copy-start.45 = (f32[128]{0:T(128)S(1)}, f32[128]{0:T(128)}, u32[]{:S(2)}) copy-start(f32[128]{0:T(128)} %copy-done.44) | copy-start | bytes 1540
  435.0 24.6 %copy-start.50 = (f32[128]{0:T(128)S(1)}, f32[128]{0:T(128)}, u32[]{:S(2)}) copy-start(f32[128]{0:T(128)} %copy-done.49) | copy-start | bytes 1540
  435.0 24.6 %copy-start.48 = (f32[128]{0:T(128)S(1)}, f32[128]{0:T(128)}, u32[]{:S(2)}) copy-start(f32[128]{0:T(128)} %copy-done.47) | copy-start | bytes 1540
  457.8 43.1 %copy-start.14 = (f32[1,128,2048]{2,1,0:T(8,128)S(1)}, f32[1,128,2048]{2,1,0:T(8,128)}, u32[]{:S(2)}) copy-start(f32[1,128,2048]{2,1,0:T(8,128)} %copy-done.13) | copy-start | bytes 3145732
  (36 other events, 58.9 us)
Sparse Core Ops, SparseCore 0:
  367.1 33.3 reduce-scatter.8
  402.8 34.5 reduce-scatter.10
  439.7 49.4 reduce-scatter.22
  491.4 48.0 reduce-scatter.12
  541.6 48.3 reduce-scatter.14
  592.2 48.3 reduce-scatter.16
  642.9 48.3 reduce-scatter.18
  693.6 48.3 reduce-scatter.20

commit v2 on v0

v2 whole, which is shorter than its diff:
```python
import functools

import jax
import jax.numpy as jnp
from jax import lax
from jax.experimental import pallas as pl
from jax.experimental.pallas import tpu as pltpu
from jax.sharding import PartitionSpec as P

DK = 256
DV = 512


EPS = 1e-05
MESH = pl.DeviceIdType.MESH
BF = jnp.bfloat16
F32 = jnp.float32
VMEM_LIMIT = 60 * 1024 * 1024


def remote(src, dst, ssem, rsem, slot, dev):
    return pltpu.make_async_remote_copy(
        src_ref=src,
        dst_ref=dst,
        send_sem=ssem.at[slot],
        recv_sem=rsem.at[slot],
        device_id=dev,
        device_id_type=MESH,
    )


def greet(devs):
    barrier = pltpu.get_barrier_semaphore()
    for dev in devs:
        pl.semaphore_signal(barrier, inc=1, device_id=dev, device_id_type=MESH)
    pl.semaphore_wait(barrier, len(devs))


def params(cid):
    return pltpu.CompilerParams(
        collective_id=cid, has_side_effects=True, vmem_limit_bytes=VMEM_LIMIT
    )


class Gather:
    def __init__(self, n, x, o, ssem, rsem):
        s, t = lax.axis_index("seq"), lax.axis_index("tp")
        self.n, self.t = n, t
        rows = x.shape[0]
        if n == 4:
            px, py = t + 1 - 2 * (t % 2), (t + 2) % 4
            dx, dy = (s, px), (s, py)
            self.peers = [dx, dy]
            half = rows // 2
            lo, hi = pl.ds(0, half), pl.ds(half, half)
            self.first = [
                remote(x.at[lo], o.at[t, lo], ssem, rsem, 0, dx),
                remote(x.at[hi], o.at[t, hi], ssem, rsem, 1, dy),
                remote(x.at[hi], o.at[t, hi], ssem, rsem, 2, dx),
                remote(x.at[lo], o.at[t, lo], ssem, rsem, 3, dy),
            ]
            self.relay = [
                remote(o.at[px, lo], o.at[px, lo], ssem, rsem, 4, dy),
                remote(o.at[py, hi], o.at[py, hi], ssem, rsem, 5, dx),
            ]
        else:
            self.peers = [(s, (t + k) % n) for k in range(1, n)]
            self.first = [
                remote(x, o.at[t], ssem, rsem, k, dev) for k, dev in enumerate(self.peers)
            ]
            self.relay = []

    def source(self, i):
        t = self.t
        if self.n == 4:
            near = jnp.where(i == 1, t + 1 - 2 * (t % 2), (t + 2) % 4)
            return jnp.where(i == 0, t, jnp.where(i == 3, 3 - t, near))
        return (t - i + self.n) % self.n

    def start(self):
        for copy in self.first:
            copy.start()

    def arrive(self, i):
        if self.n == 4:

            @pl.when(i == 1)
            def _():
                self.first[0].wait_recv()
                self.relay[0].start()
                self.first[1].wait_recv()
                self.relay[1].start()
                self.first[2].wait_recv()

            @pl.when(i == 2)
            def _():
                self.first[3].wait_recv()

            @pl.when(i == 3)
            def _():
                self.relay[0].wait_recv()
                self.relay[1].wait_recv()

        else:
            for k, copy in enumerate(self.first):

                @pl.when(i == k + 1)
                def _(copy=copy):
                    copy.wait_recv()

    def drain(self):
        for copy in self.first + self.relay:
            copy.wait_send()


class Scatter:
    def __init__(self, n, parts, near, far, hold, ssem, rsem):
        s, t = lax.axis_index("seq"), lax.axis_index("tp")
        self.n, self.t = n, t
        self.parts, self.near, self.far, self.hold = parts, near, far, hold
        if n == 4:
            self.px, self.py, pd = t + 1 - 2 * (t % 2), (t + 2) % 4, 3 - t
            dx, dy = (s, self.px), (s, self.py)
            self.peers = [dx, dy]
            half = parts.shape[-1] // 2
            self.cols = a, b = pl.ds(0, half), pl.ds(half, half)
            self.far_a = remote(parts.at[pd, :, a], near.at[0, 1], ssem, rsem, 0, dx)
            self.far_b = remote(parts.at[pd, :, b], near.at[1, 1], ssem, rsem, 1, dy)
            self.near_a = remote(parts.at[self.px, :, a], near.at[0, 0], ssem, rsem, 2, dx)
            self.near_b = remote(parts.at[self.py, :, b], near.at[1, 0], ssem, rsem, 3, dy)
            self.sum_a = remote(hold.at[0], far.at[0], ssem, rsem, 4, dy)
            self.sum_b = remote(hold.at[1], far.at[1], ssem, rsem, 5, dx)
            self.copies = [self.far_a, self.far_b, self.near_a, self.near_b, self.sum_a, self.sum_b]
        else:
            self.peers = [(s, (t + k) % n) for k in range(1, n)]
            self.copies = [
                remote(parts.at[(t - k + n) % n], near.at[k - 1], ssem, rsem, k - 1, (s, (t - k + n) % n))
                for k in range(1, n)
            ]

    def send(self, i):
        if self.n == 4:

            @pl.when(i == 1)
            def _():
                self.near_a.start()

            @pl.when(i == 2)
            def _():
                self.near_b.start()

            @pl.when(i == 3)
            def _():
                self.far_a.start()
                self.far_b.start()

        else:
            for k, copy in enumerate(self.copies):

                @pl.when(i == k + 1)
                def _(copy=copy):
                    copy.start()

    def relay(self):
        if self.n == 4:
            a, b = self.cols
            self.far_a.wait_recv()
            self.hold[0] = (
                self.parts[self.py, :, a].astype(F32) + self.near[0, 1].astype(F32)
            ).astype(BF)
            self.sum_a.start()
            self.far_b.wait_recv()
            self.hold[1] = (
                self.parts[self.px, :, b].astype(F32) + self.near[1, 1].astype(F32)
            ).astype(BF)
            self.sum_b.start()

    def finish(self, write):
        if self.n == 4:
            for side, (one, two) in enumerate(
                ((self.near_a, self.sum_a), (self.near_b, self.sum_b))
            ):
                one.wait_recv()
                two.wait_recv()
                write(
                    self.cols[side],
                    self.parts[self.t, :, self.cols[side]].astype(F32)
                    + self.near[side, 0].astype(F32)
                    + self.far[side].astype(F32),
                )
        else:
            total = self.parts[self.t].astype(F32)
            for k, copy in enumerate(self.copies):
                copy.wait_recv()
                total = total + self.near[k].astype(F32)
            write(slice(None), total)

    def drain(self):
        for copy in self.copies:
            copy.wait_send()


def scatter_scratch(n, rows, width):
    if n == 4:
        near, far = (2, 2, rows, width // 2), (2, rows, width // 2)
    else:
        near, far = (n - 1, rows, width), (1, 16, 128)
    return [pltpu.VMEM(near, BF), pltpu.VMEM(far, BF), pltpu.VMEM(far, BF)]


class Chain:
    def __init__(self, chips, heads, flip, fac, local, out, pair, enter, leave, ps, pr, zs, zr, bs, br):
        s, t = lax.axis_index("seq"), lax.axis_index("tp")
        core, chip, span = s % 2, s // 2, 2 * chips
        self.chips, self.heads, self.fac = chips, heads, fac
        self.local, self.out, self.pair, self.enter, self.leave = local, out, pair, enter, leave
        self.sems = ps, pr, zs, zr, bs, br
        self.partner = (s + 1 - 2 * core, t)
        above, below = ((s + 2) % span, t), ((s - 2 + span) % span, t)
        self.peers = [self.partner, above, below]
        if flip:
            self.first, self.place, self.ahead = core == 1, chips - 1 - chip, below
        else:
            self.first, self.place, self.ahead = core == 0, chip, above
        self.last = jnp.logical_not(self.first)

    def give(self, p):
        return remote(self.local.at[p], self.pair.at[p], self.sems[0], self.sems[1], p, self.partner)

    def back(self, p):
        return remote(self.enter.at[p], self.out.at[p], self.sems[4], self.sems[5], p, self.partner)

    def onward(self, p):
        return remote(self.leave.at[p], self.enter.at[p], self.sems[2], self.sems[3], p, self.ahead)

    def begin(self, p):
        @pl.when(self.first)
        def _():
            self.give(p).start()

            @pl.when(self.place == 0)
            def _():
                self.out[p] = jnp.zeros(self.out.shape[1:], BF)

    def step(self, p):
        @pl.when(self.first)
        def _():
            @pl.when(self.place > 0)
            def _():
                self.back(p).wait_recv()

        @pl.when(self.last)
        def _():
            fac = self.fac[p % self.heads]
            self.give(p).wait_recv()
            early = self.pair[p].astype(F32)
            chip_sum = early * fac + self.local[p].astype(F32)

            @pl.when(self.place == 0)
            def _():
                self.leave[p] = chip_sum.astype(BF)
                self.out[p] = self.pair[p]

            @pl.when(self.place > 0)
            def _():
                self.onward(p).wait_recv()
                self.back(p).start()
                came = self.enter[p].astype(F32)
                self.leave[p] = (came * (fac * fac) + chip_sum).astype(BF)
                self.out[p] = (came * fac + early).astype(BF)

            @pl.when(self.place < self.chips - 1)
            def _():
                self.onward(p).start()

    def drain(self, p):
        @pl.when(self.first)
        def _():
            self.give(p).wait_send()

        @pl.when(self.last)
        def _():
            @pl.when(self.place > 0)
            def _():
                self.back(p).wait_send()

            @pl.when(self.place < self.chips - 1)
            def _():
                self.onward(p).wait_send()


def chain_scratch(pieces):
    dma = pltpu.SemaphoreType.DMA
    return [pltpu.VMEM((pieces, DK, DV), BF)] * 3 + [dma((pieces,))] * 6


def dot(a, b, ca=1, cb=0):
    return lax.dot_general(a, b, (((ca,), (cb,)), ((), ())), preferred_element_type=F32)


def turn(v, cos, sin):
    lo, hi = v[:, : DK // 2], v[:, DK // 2 :]
    return jnp.concatenate([lo * cos - hi * sin, hi * cos + lo * sin], 1)


def turn_back(g, cos, sin):
    lo, hi = g[:, : DK // 2], g[:, DK // 2 :]
    return jnp.concatenate([lo * cos + hi * sin, hi * cos - lo * sin], 1)


def norm_of(m):
    center = m - jnp.mean(m, -1, keepdims=True)
    inv = lax.rsqrt(jnp.mean(center * center, -1, keepdims=True) + EPS)
    return center * inv, inv


def mixer_kernel(n, chips, heads, *refs):
    (
        fac, x, og, wk_h, wv_h, wq_h, ws_h, wo_h, decay, qfac, kfac, cos, sin,
        x_all, og_all, q, k, v, sp, mx, prior, gated, attn,
        wk, wv, wq, ws, wo, acc, parts, local,
    ) = refs[:31]
    near, far, hold = refs[31:34]
    chain_refs = refs[34:43]
    wsem, gs, gr, os, orr, ss, sr = refs[43:]
    rows = x.shape[0]
    gather = Gather(n, x, x_all, gs, gr)
    gather_og = Gather(n, og, og_all, os, orr)
    scatter = Scatter(n, parts, near, far, hold, ss, sr)
    chain = Chain(chips, heads, False, fac, local, prior, *chain_refs)
    loads = [
        pltpu.make_async_copy(a, w, wsem.at[i])
        for i, (a, w) in enumerate(((wk_h, wk), (wv_h, wv), (wq_h, wq), (ws_h, ws), (wo_h, wo)))
    ]
    for load in loads:
        load.start()
    greet(gather.peers + chain.peers)
    gather.start()
    gather_og.start()
    me = gather.source(0)
    x_all[me] = x[...]
    og_all[me] = og[...]
    for load in loads[:4]:
        load.wait()

    @pl.loop(0, n)
    def _(i):
        j = gather.source(i)
        gather.arrive(i)
        at = pl.ds(pl.multiple_of(j * rows, rows), rows)
        acc[:, : heads * DK] = dot(x_all[j], wk[...])
        v[at] = dot(x_all[j], wv[...]).astype(BF)
        for h in range(heads):
            vc = slice(h * DV, (h + 1) * DV)
            kc = slice(h * DK, (h + 1) * DK)
            key = turn(acc[:, kc], cos[...], sin[...]).astype(BF)
            k[at, kc] = key
            key_dec = (key.astype(F32) * kfac[h]).astype(BF)
            p = j * heads + h
            local[p] = dot(key_dec, v[at, vc], 0, 0).astype(BF)
            chain.begin(p)
        acc[:, : heads * DK] = dot(x_all[j], wq[...])
        for h in range(heads):
            kc = slice(h * DK, (h + 1) * DK)
            q[at, kc] = turn(acc[:, kc], cos[...], sin[...]).astype(BF)
        sp[at] = dot(x_all[j], ws[...])

    loads[4].wait()

    @pl.loop(0, n)
    def _(step):
        i = (step + 1) % n
        j = gather.source(i)
        gather_og.arrive(i)
        at = pl.ds(pl.multiple_of(j * rows, rows), rows)
        for h in range(heads):
            vc = slice(h * DV, (h + 1) * DV)
            kc = slice(h * DK, (h + 1) * DK)
            p = j * heads + h
            query = q[at, kc]
            scores = (dot(query, k[at, kc], 1, 1) * decay[h]).astype(BF)
            mx[at, vc] = dot(scores, v[at, vc])
            query_dec = (query.astype(F32) * qfac[h]).astype(BF)
            chain.step(p)
            mx[at, vc] += dot(query_dec, prior[p])
            pre = sp[at, vc]
            gated[at, vc] = (pre * jax.nn.sigmoid(pre) * norm_of(mx[at, vc])[0]).astype(BF)
        parts[j] = dot(gated[at], wo[...]).astype(BF)
        scatter.send(i)

    scatter.relay()

    def write(cols, total):
        attn[:, cols] = total

    scatter.finish(write)
    gather.drain()
    gather_og.drain()
    scatter.drain()

    @pl.loop(0, n * heads)
    def _(p):
        chain.drain(p)


def mixer(fac, x, og, wk, wv, wq, ws, wo, decay, qfac, kfac, cos, sin, cid):
    n = lax.axis_size("tp")
    chips = lax.axis_size("seq") // 2
    rows, model = x.shape
    heads = wk.shape[1] // DK
    pieces = n * heads
    total = n * rows
    dma = pltpu.SemaphoreType.DMA
    sems = max(6, n - 1)
    vmem = pl.BlockSpec(memory_space=pltpu.VMEM)
    hbm = pl.BlockSpec(memory_space=pl.ANY)
    shape = jax.ShapeDtypeStruct
    return pl.pallas_call(
        functools.partial(mixer_kernel, n, chips, heads),
        out_shape=(
            shape((n, rows, model), BF),
            shape((n, rows, model), BF),
            shape((total, heads * DK), BF),
            shape((total, heads * DK), BF),
            shape((total, heads * DV), BF),
            shape((total, heads * DV), F32),
            shape((total, heads * DV), F32),
            shape((pieces, DK, DV), BF),
            shape((total, heads * DV), BF),
            shape((rows, model), F32),
        ),
        in_specs=[pl.BlockSpec(memory_space=pltpu.SMEM), vmem, vmem] + [hbm] * 5 + [vmem] * 5,
        out_specs=(vmem,) * 10,
        scratch_shapes=[pltpu.VMEM(w.shape, BF) for w in (wk, wv, wq, ws, wo)]
        + [
            pltpu.VMEM((rows, heads * DK), F32),
            pltpu.VMEM((n, rows, model), BF),
            pltpu.VMEM((pieces, DK, DV), BF),
        ]
        + scatter_scratch(n, rows, model)
        + chain_scratch(pieces)
        + [dma((5,))] + [dma((sems,))] * 6,
        compiler_params=params(cid),
        name="mixer",
    )(fac, x, og, wk, wv, wq, ws, wo, decay, qfac, kfac, cos, sin)


GELU_C = 0.7978845608028654
GELU_A = 0.044715


def mlp_kernel(n, *refs):
    (
        x, og_all, wg_h, wu_h, wd_h,
        x_all, hidden, gate_low, upper_low, mlp_parts, grad_two,
        wg, wu, wd, hg, acc_g, acc_u, acc, parts, near, far, hold,
        wsem, gs, gr, ss, sr,
    ) = refs
    rows = x.shape[0]
    gather = Gather(n, x, x_all, gs, gr)
    scatter = Scatter(n, parts, near, far, hold, ss, sr)
    loads = [
        pltpu.make_async_copy(a, w, wsem.at[i])
        for i, (a, w) in enumerate(((wd_h, wd), (wg_h, wg), (wu_h, wu)))
    ]
    for load in loads:
        load.start()
    greet(gather.peers)
    gather.start()
    me = gather.source(0)
    x_all[me] = x[...]
    loads[0].wait()

    @pl.loop(0, n)
    def _(j):
        at = pl.ds(pl.multiple_of(j * rows, rows), rows)
        hg[at] = dot(og_all[j], wd[...], 1, 1)

    loads[1].wait()
    loads[2].wait()
    slab = 16

    @pl.loop(0, n)
    def _(i):
        j = gather.source(i)
        gather.arrive(i)
        start = pl.multiple_of(j * rows, rows)
        at = pl.ds(start, rows)
        acc_g[...] = dot(x_all[j], wg[...])
        acc_u[...] = dot(x_all[j], wu[...])

        @pl.loop(0, rows // slab)
        def _(r):
            here = pl.ds(pl.multiple_of(r * slab, slab), slab)
            there = pl.ds(pl.multiple_of(start + r * slab, slab), slab)
            g, u, back = acc_g[here], acc_u[here], hg[there]
            square = g * g
            th = jnp.tanh(GELU_C * (g + GELU_A * (square * g)))
            half = 0.5 * (1.0 + th)
            gelu = g * half
            slope = half + 0.5 * g * (1.0 - th * th) * (GELU_C * (1.0 + 3.0 * GELU_A * square))
            hidden[there] = (gelu * u).astype(BF)
            gate_low[there] = (back * u * slope).astype(BF)
            upper_low[there] = (back * gelu).astype(BF)

        acc[...] = dot(gate_low[at], wg[...], 1, 1)
        parts[j] = (acc[...] + dot(upper_low[at], wu[...], 1, 1)).astype(BF)
        scatter.send(i)

    @pl.loop(0, n)
    def _(j):
        at = pl.ds(pl.multiple_of(j * rows, rows), rows)
        mlp_parts[j] = dot(hidden[at], wd[...]).astype(BF)

    scatter.relay()

    def write(cols, total):
        grad_two[:, cols] = total

    scatter.finish(write)
    gather.drain()
    scatter.drain()


def mlp(x, og_all, wg, wu, wd, cid):
    n = lax.axis_size("tp")
    rows, model = x.shape
    width = wg.shape[1]
    total = n * rows
    dma = pltpu.SemaphoreType.DMA
    sems = max(6, n - 1)
    vmem = pl.BlockSpec(memory_space=pltpu.VMEM)
    hbm = pl.BlockSpec(memory_space=pl.ANY)
    shape = jax.ShapeDtypeStruct
    return pl.pallas_call(
        functools.partial(mlp_kernel, n),
        out_shape=(
            shape((n, rows, model), BF),
            shape((total, width), BF),
            shape((total, width), BF),
            shape((total, width), BF),
            shape((n, rows, model), BF),
            shape((rows, model), F32),
        ),
        in_specs=[vmem, vmem] + [hbm] * 3,
        out_specs=(vmem,) * 6,
        scratch_shapes=[pltpu.VMEM(w.shape, BF) for w in (wg, wu, wd)]
        + [
            pltpu.VMEM((total, width), F32),
            pltpu.VMEM((rows, width), F32),
            pltpu.VMEM((rows, width), F32),
            pltpu.VMEM((rows, model), F32),
            pltpu.VMEM((n, rows, model), BF),
        ]
        + scatter_scratch(n, rows, model)
        + [dma((3,))] + [dma((sems,))] * 4,
        compiler_params=params(cid),
        name="mlp",
    )(x, og_all, wg, wu, wd)


def mixer_back_kernel(n, chips, heads, *refs):
    (
        fac, res, wo_h, wq_h, wk_h, wv_h, ws_h, q, k, v, sp, mx, prior, mlp_parts, decay, qfac, kfac, cos, sin,
        res_all, swish_low, value_low, qk_low, grad_one, mlp_out,
        wo, wq, wk, wv, ws, mixed_low, acc, parts, local, later,
    ) = refs[:35]
    near, far, hold, mlp_near, mlp_far, mlp_hold = refs[35:41]
    chain_refs = refs[41:50]
    wsem, gs, gr, ss, sr, ms, mr = refs[50:]
    rows = res.shape[0]
    gather = Gather(n, res, res_all, gs, gr)
    scatter = Scatter(n, parts, near, far, hold, ss, sr)
    scatter_mlp = Scatter(n, mlp_parts, mlp_near, mlp_far, mlp_hold, ms, mr)
    chain = Chain(chips, heads, True, fac, local, later, *chain_refs)
    loads = [
        pltpu.make_async_copy(a, w, wsem.at[i])
        for i, (a, w) in enumerate(((wo_h, wo), (ws_h, ws), (wq_h, wq), (wk_h, wk), (wv_h, wv)))
    ]
    for load in loads:
        load.start()
    greet(gather.peers + chain.peers)
    gather.start()
    me = gather.source(0)
    res_all[me] = res[...]
    loads[0].wait()

    @pl.loop(0, n)
    def _(i):
        j = gather.source(i)
        gather.arrive(i)
        at = pl.ds(pl.multiple_of(j * rows, rows), rows)
        acc[:, : heads * DV] = dot(res_all[j], wo[...], 1, 1)
        for h in range(heads):
            vc = slice(h * DV, (h + 1) * DV)
            kc = slice(h * DK, (h + 1) * DK)
            back = acc[:, vc]
            normed, inv = norm_of(mx[at, vc])
            pre = sp[at, vc]
            sig = jax.nn.sigmoid(pre)
            swish_low[at, vc] = (back * normed * (sig * (1.0 + pre * (1.0 - sig)))).astype(BF)
            g = back * (pre * sig)
            g = inv * (
                g
                - jnp.mean(g, -1, keepdims=True)
                - normed * jnp.mean(g * normed, -1, keepdims=True)
            )
            g = g.astype(BF)
            mixed_low[at, vc] = g
            query_dec = (q[at, kc].astype(F32) * qfac[h]).astype(BF)
            p = j * heads + h
            local[p] = dot(query_dec, g, 0, 0).astype(BF)
            chain.begin(p)

    for load in loads[1:]:
        load.wait()
    for i in range(1, n):
        scatter_mlp.send(i)

    @pl.loop(0, n)
    def _(step):
        i = (step + 1) % n
        j = gather.source(i)
        at = pl.ds(pl.multiple_of(j * rows, rows), rows)
        for h in range(heads):
            vc = slice(h * DV, (h + 1) * DV)
            kc = slice(h * DK, (h + 1) * DK)
            p = j * heads + h
            g, value, query, key = mixed_low[at, vc], v[at, vc], q[at, kc], k[at, kc]
            raw_low = (dot(g, value, 1, 1) * decay[h]).astype(BF)
            query_back = dot(raw_low, key) + dot(g, prior[p], 1, 1) * qfac[h]
            qk_low[at, kc] = turn_back(query_back, cos[...], sin[...]).astype(BF)
            scores = (dot(query, key, 1, 1) * decay[h]).astype(BF)
            key_part = dot(raw_low, query, 0, 0)
            value_part = dot(scores, g, 0, 0)
            key_dec = (key.astype(F32) * kfac[h]).astype(BF)
            chain.step(p)
            after = later[p]
            key_back = key_part + dot(value, after, 1, 1) * kfac[h]
            qk_low[at, slice((heads + h) * DK, (heads + h + 1) * DK)] = turn_back(
                key_back, cos[...], sin[...]
            ).astype(BF)
            value_low[at, vc] = (value_part + dot(key_dec, after)).astype(BF)
        acc[...] = dot(swish_low[at], ws[...], 1, 1)
        acc[...] += dot(value_low[at], wv[...], 1, 1)
        acc[...] += dot(qk_low[at, : heads * DK], wq[...], 1, 1)
        parts[j] = (acc[...] + dot(qk_low[at, heads * DK :], wk[...], 1, 1)).astype(BF)
        scatter.send(i)

        @pl.when(step == n - 2)
        def _():
            scatter_mlp.relay()

    scatter.relay()

    def write(cols, total):
        grad_one[:, cols] = total

    scatter.finish(write)

    def write_mlp(cols, total):
        mlp_out[:, cols] = total

    scatter_mlp.finish(write_mlp)
    gather.drain()
    scatter.drain()
    scatter_mlp.drain()

    @pl.loop(0, n * heads)
    def _(p):
        chain.drain(p)


def mixer_back(fac, res, wo, wq, wk, wv, ws, q, k, v, sp, mx, prior, mlp_parts, decay, qfac, kfac, cos, sin, cid):
    n = lax.axis_size("tp")
    chips = lax.axis_size("seq") // 2
    rows, model = res.shape
    heads = q.shape[1] // DK
    pieces = n * heads
    total = n * rows
    dma = pltpu.SemaphoreType.DMA
    sems = max(6, n - 1)
    vmem = pl.BlockSpec(memory_space=pltpu.VMEM)
    hbm = pl.BlockSpec(memory_space=pl.ANY)
    shape = jax.ShapeDtypeStruct
    return pl.pallas_call(
        functools.partial(mixer_back_kernel, n, chips, heads),
        out_shape=(
            shape((n, rows, model), BF),
            shape((total, heads * DV), BF),
            shape((total, heads * DV), BF),
            shape((total, 2 * heads * DK), BF),
            shape((rows, model), F32),
            shape((rows, model), F32),
        ),
        in_specs=[pl.BlockSpec(memory_space=pltpu.SMEM), vmem] + [hbm] * 5 + [vmem] * 12,
        out_specs=(vmem,) * 6,
        scratch_shapes=[pltpu.VMEM(w.shape, BF) for w in (wo, wq, wk, wv, ws)]
        + [
            pltpu.VMEM((total, heads * DV), BF),
            pltpu.VMEM((rows, model), F32),
            pltpu.VMEM((n, rows, model), BF),
            pltpu.VMEM((pieces, DK, DV), BF),
            pltpu.VMEM((pieces, DK, DV), BF),
        ]
        + scatter_scratch(n, rows, model)
        + scatter_scratch(n, rows, model)
        + chain_scratch(pieces)
        + [dma((5,))]
        + [dma((sems,))] * 6,
        compiler_params=params(cid),
        name="mixer_back",
    )(fac, res, wo, wq, wk, wv, ws, q, k, v, sp, mx, prior, mlp_parts, decay, qfac, kfac, cos, sin)


def weights_kernel(
    chips, units, kinds, *refs
):
    kind_count = max(kinds) + 1
    wide = refs[:kind_count]
    deep = refs[kind_count : kind_count + units]
    vec = refs[kind_count + units]
    rest = refs[kind_count + units + 1 :]
    vec_near, vec_sum, vec_far, vs, vr, us, ur = rest[-7:]
    rest = rest[:-7]
    o_ref, vec_out, xs, ys, from_low, from_high, out, xsem, ysem, psx, prx, psy, pry, ssem, lsem, hsem = rest
    s = lax.axis_index("seq")
    t = lax.axis_index("tp")
    core = s % 2
    chip = s // 2
    tokens = ys.shape[1] // 2
    cut = xs.shape[3]
    span = 2 * chips
    partner = (s + 1 - 2 * core, t)
    above = ((s + 2) % span, t)
    below = ((s - 2 + span) % span, t)
    tp = vec.shape[0]
    ring = [((s + d) % span, t) for d in range(1, span)]
    cross = [(s, (t + d) % tp) for d in range(1, tp)]
    greet(ring + cross)
    vec_first = [
        remote(vec.at[(t + d) % tp], vec_near.at[d - 1], vs, vr, d - 1, cross[d - 1])
        for d in range(1, tp)
    ]
    vec_last = [
        remote(vec_sum.at[(s + d) % span], vec_far.at[d - 1], us, ur, d - 1, ring[d - 1])
        for d in range(1, span)
    ]
    for copy in vec_first:
        copy.start()

    def wide_own(kind, j):
        cols = pl.ds(pl.multiple_of((2 * j + core) * cut, cut), cut)
        return pltpu.make_async_copy(
            wide[kind].at[:, cols], xs.at[kind, j, pl.ds(0, tokens)], xsem.at[kind, j]
        )

    def wide_give(kind, j):
        cols = pl.ds(pl.multiple_of((2 * j + 1 - core) * cut, cut), cut)
        return pltpu.make_async_remote_copy(
            src_ref=wide[kind].at[:, cols],
            dst_ref=xs.at[kind, j, pl.ds(tokens, tokens)],
            send_sem=psx.at[kind, j],
            recv_sem=prx.at[kind, j],
            device_id=partner,
            device_id_type=MESH,
        )

    def deep_own(u):
        return pltpu.make_async_copy(deep[u], ys.at[u, pl.ds(0, tokens)], ysem.at[u])

    def deep_give(u):
        return pltpu.make_async_remote_copy(
            src_ref=deep[u],
            dst_ref=ys.at[u, pl.ds(tokens, tokens)],
            send_sem=psy.at[u],
            recv_sem=pry.at[u],
            device_id=partner,
            device_id_type=MESH,
        )

    seen = set()
    for u in range(units):
        deep_give(u).start()
        deep_own(u).start()
        if kinds[u] not in seen:
            seen.add(kinds[u])
            for j in range(chips):
                wide_give(kinds[u], j).start()
                wide_own(kinds[u], j).start()

    def ready(u):
        deep_own(u).wait()
        deep_give(u).wait_recv()
        if kinds[u] not in kinds[:u]:
            for j in range(chips):
                wide_own(kinds[u], j).wait()
                wide_give(kinds[u], j).wait_recv()

    def up(u, j):
        return pltpu.make_async_remote_copy(
            src_ref=out.at[u, j],
            dst_ref=from_low.at[u, j],
            send_sem=ssem.at[u, j],
            recv_sem=lsem.at[u, j],
            device_id=above,
            device_id_type=MESH,
        )

    def down(u, j):
        return pltpu.make_async_remote_copy(
            src_ref=out.at[u, j],
            dst_ref=from_high.at[u, j],
            send_sem=ssem.at[u, j],
            recv_sem=hsem.at[u, j],
            device_id=below,
            device_id_type=MESH,
        )

    def kind_of(u):
        kind = 0
        for w in range(units):
            if kinds[w]:
                kind = kind + jnp.where(u == w, kinds[w], 0)
        return kind

    def product(u, j):
        return lax.dot_general(
            xs[kind_of(u), j], ys[u], (((0,), (0,)), ((), ())), preferred_element_type=F32
        )

    low_half = chip < chips // 2
    rights = chips - 1 - chip

    def finish(u):
        total = product(u, chip)
        o_ref[u] = total

        @pl.when(chip > 0)
        def _():
            up(u, chip).wait_recv()
            o_ref[u] = o_ref[u] + from_low[u, chip].astype(F32)

        @pl.when(chip < chips - 1)
        def _():
            down(u, chip).wait_recv()
            o_ref[u] = o_ref[u] + from_high[u, chip].astype(F32)

    @pl.loop(0, units)
    def _(u):
        for w in range(units):

            @pl.when(u == w)
            def _(w=w):
                ready(w)

        @pl.loop(0, chips - 1)
        def _(k):
            j = jnp.where(
                low_half,
                jnp.where(k < rights, chips - 1 - k, k - rights),
                jnp.where(k < chip, k, chips - 1 - (k - chip)),
            )
            total = product(u, j)

            @pl.when(j > chip)
            def _():
                @pl.when(chip == 0)
                def _():
                    out[u, j] = total.astype(BF)

                @pl.when(chip > 0)
                def _():
                    up(u, j).wait_recv()
                    out[u, j] = (total + from_low[u, j].astype(F32)).astype(BF)

                up(u, j).start()

            @pl.when(j < chip)
            def _():
                @pl.when(chip == chips - 1)
                def _():
                    out[u, j] = total.astype(BF)

                @pl.when(chip < chips - 1)
                def _():
                    down(u, j).wait_recv()
                    out[u, j] = (total + from_high[u, j].astype(F32)).astype(BF)

                down(u, j).start()

        @pl.when(u == 0)
        def _():
            total = vec[t]
            for copy in vec_first:
                copy.wait_recv()
            vec_sum[...] = total + jnp.sum(vec_near[...], 0)
            for copy in vec_last:
                copy.start()

        @pl.when(u > 0)
        def _():
            finish(u - 1)

    vec_total = vec_sum[s]
    for copy in vec_last:
        copy.wait_recv()
    vec_out[...] = vec_total + jnp.sum(vec_far[...], 0)
    finish(units - 1)

    @pl.loop(0, units)
    def _(u):
        @pl.loop(0, chips)
        def _(j):
            @pl.when(j > chip)
            def _():
                up(u, j).wait_send()

            @pl.when(j < chip)
            def _():
                down(u, j).wait_send()

    for copy in vec_first + vec_last:
        copy.wait_send()
    for u in range(units):
        deep_give(u).wait_send()
    for kind in range(kind_count):
        for j in range(chips):
            wide_give(kind, j).wait_send()


def weight_sums(wide, deep, vec, kinds, cid):
    chips = lax.axis_size("seq") // 2
    tokens, model = wide[0].shape
    width = deep[0].shape[1]
    units = len(deep)
    cut = model // (2 * chips)
    block = (units, chips, cut, width)
    dma = pltpu.SemaphoreType.DMA
    return pl.pallas_call(
        functools.partial(weights_kernel, chips, units, kinds),
        out_shape=(
            jax.ShapeDtypeStruct((units, cut, width), F32),
            jax.ShapeDtypeStruct(vec.shape[2:], F32),
        ),
        in_specs=[pl.BlockSpec(memory_space=pl.ANY)] * (len(wide) + units)
        + [pl.BlockSpec(memory_space=pltpu.VMEM)],
        out_specs=(pl.BlockSpec(memory_space=pltpu.VMEM),) * 2,
        scratch_shapes=[
            pltpu.VMEM((len(wide), chips, 2 * tokens, cut), BF),
            pltpu.VMEM((units, 2 * tokens, width), BF),
            pltpu.VMEM(block, BF),
            pltpu.VMEM(block, BF),
            pltpu.VMEM(block, BF),
            dma((len(wide), chips)),
            dma((units,)),
            dma((len(wide), chips)),
            dma((len(wide), chips)),
            dma((units,)),
            dma((units,)),
            dma((units, chips)),
            dma((units, chips)),
            dma((units, chips)),
            pltpu.VMEM((vec.shape[0] - 1,) + vec.shape[1:], F32),
            pltpu.VMEM(vec.shape[1:], F32),
            pltpu.VMEM((2 * chips - 1,) + vec.shape[2:], F32),
            dma((vec.shape[0] - 1,)),
            dma((vec.shape[0] - 1,)),
            dma((2 * chips - 1,)),
            dma((2 * chips - 1,)),
        ],
        compiler_params=params(cid),
        name=f"weights_{cid}",
    )(*wide, *deep, vec)


def layer_norm(values, gain, bias):
    center = values - jnp.mean(values, -1, keepdims=True)
    spread = jnp.mean(center * center, -1, keepdims=True)
    return center * lax.rsqrt(spread + EPS) * gain + bias


def shards(
    inputs,
    query_weight,
    key_weight,
    value_weight,
    swish_weight,
    output_weight,
    gate_weight,
    up_weight,
    down_weight,
    attn_gain,
    attn_bias,
    mlp_gain,
    mlp_bias,
    output_grad,
):
    _, rows, model = inputs.shape
    heads = query_weight.shape[1] // DK
    inputs_full = inputs[0].astype(F32)
    cotangent = output_grad[0]

    half_width = DK // 2
    frequencies = jnp.power(10000.0, -jnp.arange(half_width, dtype=F32) / half_width)
    steps_in = jnp.arange(rows, dtype=F32)
    positions = lax.axis_index("seq").astype(F32) * rows + steps_in
    angles = positions[:, None] * frequencies[None, :]
    cosine, sine = jnp.cos(angles), jnp.sin(angles)
    head_ids = (lax.axis_index("tp") * heads + jnp.arange(heads)).astype(F32)
    decays = 1.0 - jnp.exp2(-5.0 - head_ids)
    lag = steps_in[:, None] - steps_in[None, :]
    decay_mat = jnp.where(
        lag[None] >= 0, jnp.power(decays[:, None, None], jnp.maximum(lag, 0.0)[None]), 0.0
    )
    query_fac = jnp.power(decays[:, None], steps_in[None, :] + 1.0)[:, :, None]
    key_fac = jnp.power(decays[:, None], rows - 1.0 - steps_in[None, :])[:, :, None]
    block_fac = jnp.power(decays, rows * 1.0)

    normed_one = layer_norm(inputs_full, attn_gain, attn_bias).astype(BF)
    one_all, grad_all, query, key, value, swish_pre, mixed, prior, gated, attn_out = mixer(
        block_fac, normed_one, cotangent, key_weight, value_weight, query_weight, swish_weight,
        output_weight, decay_mat, query_fac, key_fac, cosine, sine, 0,
    )
    hidden_res = inputs_full + attn_out
    normed_two = layer_norm(hidden_res, mlp_gain, mlp_bias).astype(BF)
    two_all, hidden, gate_low, upper_low, mlp_parts, normed_two_grad = mlp(
        normed_two, grad_all, gate_weight, up_weight, down_weight, 1
    )
    flat = lambda a: a.reshape(-1, model)
    product = lambda a, b: jnp.einsum("na,nb->ab", a, b, preferred_element_type=F32).astype(BF)
    _, pull_two = jax.vjp(layer_norm, hidden_res, mlp_gain, mlp_bias)
    res_back, mlpgain_part, mlpbias_part = pull_two(normed_two_grad)
    res_grad = cotangent.astype(F32) + res_back
    down_low = product(hidden, flat(grad_all))
    gatew_low = product(flat(two_all), gate_low)
    upw_low = product(flat(two_all), upper_low)
    down_low, gatew_low, upw_low, res_low = lax.optimization_barrier(
        (down_low, gatew_low, upw_low, res_grad.astype(BF))
    )
    scatter = functools.partial(lax.psum_scatter, axis_name="seq", tiled=True)
    gate_grad = scatter(gatew_low, scatter_dimension=0).astype(F32)
    up_grad = scatter(upw_low, scatter_dimension=0).astype(F32)
    down_grad = scatter(down_low, scatter_dimension=1).astype(F32)

    res_all, swish_low, value_low, qk_low, normed_one_grad, mlp_out = mixer_back(
        block_fac, res_low, output_weight, query_weight, key_weight, value_weight, swish_weight,
        query, key, value, swish_pre, mixed, prior, mlp_parts, decay_mat, query_fac, key_fac,
        cosine, sine, 2,
    )
    outputs = (hidden_res + mlp_out).astype(BF)
    _, pull_one = jax.vjp(layer_norm, inputs_full, attn_gain, attn_bias)
    input_back, attngain_part, attnbias_part = pull_one(normed_one_grad)
    input_grad = (res_grad + input_back).astype(BF)

    seqs, tps = lax.axis_size("seq"), lax.axis_size("tp")
    each = model // (seqs * tps)
    vectors = jnp.stack([attngain_part, attnbias_part, mlpgain_part, mlpbias_part])
    vectors = vectors.reshape(4, seqs, tps, each).transpose(2, 1, 0, 3).reshape(tps, seqs, 4 * each)
    vectors = jnp.pad(vectors, ((0, 0), (0, 0), (0, 1024 - 4 * each))).reshape(tps, seqs, 8, 128)
    sums, vector_sums = weight_sums(
        (flat(one_all), flat(res_all)), (swish_low, gated, value_low, qk_low), vectors, (0, 1, 0, 0), 3
    )
    vector_sums = vector_sums.reshape(-1)[: 4 * each].reshape(4, each)
    return (
        outputs[None],
        input_grad[None],
        sums[3, :, : heads * DK],
        sums[3, :, heads * DK :],
        sums[2],
        sums[0],
        sums[1].T,
        gate_grad,
        up_grad,
        down_grad,
        vector_sums[0],
        vector_sums[1],
        vector_sums[2],
        vector_sums[3],
    )


def solution(mesh):
    return jax.shard_map(
        shards,
        mesh=mesh,
        in_specs=(
            P("tp", "seq", None),
            P(None, "tp"),
            P(None, "tp"),
            P(None, "tp"),
            P(None, "tp"),
            P("tp", None),
            P(None, "tp"),
            P(None, "tp"),
            P("tp", None),
            P(),
            P(),
            P(),
            P(),
            P("tp", "seq", None),
        ),
        out_specs=(
            P("tp", "seq", None),
            P("tp", "seq", None),
            P("seq", "tp"),
            P("seq", "tp"),
            P("seq", "tp"),
            P("seq", "tp"),
            P("tp", "seq"),
            P("seq", "tp"),
            P("seq", "tp"),
            P("tp", "seq"),
            P(("seq", "tp")),
            P(("seq", "tp")),
            P(("seq", "tp")),
            P(("seq", "tp")),
        ),
        check_vma=False,
    )
```

time: 1270 us -> 511 us (0.40)
  waiting for transfers between devices: 909 us -> 1.4 us
  Pallas kernels: 0 us -> 441 us
  matrix products: 127 us -> 16.2 us
  blocking collectives: 64.4 us -> 0 us
  other arithmetic: 86.4 us -> 23.5 us
  local copies, waits for them, and re-layouts: 59.7 us -> 14.2 us
    all_gather x6 -> x0, waiting for transfers between devices: 489 us -> none  [the longest x1 269 us: entering(): gathered = jax.tree.map(lambda a: lax.all_gather(a, axis), part)]
    pallas_call x0 -> x4, Pallas kernels: none -> 441 us  [the longest x1 179 us: weight_sums(): pl.pallas_call(functools.partial(weights_kernel, chips, units, kinds), ou...]
    reduce_scatter x8 -> x3, waiting for transfers between devices: 224 us -> 0.01 us  [the longest x1 0.01 us: shards(): gate_grad = scatter(gatew_low, scatter_dimension=0).astype(F32)]
    unnamed x22 -> x3, waiting for transfers between devices: 196 us -> 1.39 us
    dot_general x36 -> x3, matrix products: 127 us -> 16.2 us  [shards(): jnp.einsum('na,nb->ab', a, b, preferred_element_type=F32).astype(BF)]
    add x9 -> x0, other arithmetic: 41.7 us -> none  [the longest x7 41.7 us: chain_join(): later[0][None, :, None, None] * earlier[1] + later[1]]
    unnamed x1 -> x0, blocking collectives: 40.2 us -> none
    all_gather x2 -> x0, blocking collectives: 24.2 us -> none  [the longest x1 12.5 us: prefix(): lax.all_gather(a.astype(kind), axis)]
  transfers between devices with their start and end apart: 18 -> 3, of which waited for: 16 -> 0; matrix products, arithmetic and copies ran while one was open for 14% -> 4% of each run, Pallas kernels for 0% -> 64%
where the time goes in v2:
time: 511 us; the launch traced here: 510 us
  Pallas kernels  441 us (86%)
  other arithmetic  23.5 us (5%)
  matrix products  16.2 us (3%)
  local copies, waits for them, and re-layouts  14.2 us (3%)
  between operations  14 us (3%)
    pallas_call x1, Pallas kernels, weight_sums(): pl.pallas_call(functools.partial(weights_kernel, chips, units, kinds), ou...  179 us
    pallas_call x1, Pallas kernels, mixer_back(): pl.pallas_call(functools.partial(mixer_back_kernel, n, chips, heads), out...  148 us
    pallas_call x1, Pallas kernels, mixer(): pl.pallas_call(functools.partial(mixer_kernel, n, chips, heads), out_shap...  69.1 us
    pallas_call x1, Pallas kernels, mlp(): pl.pallas_call(functools.partial(mlp_kernel, n), out_shape=(shape((n, row...  44.9 us
    dot_general x3, matrix products, shards(): jnp.einsum('na,nb->ab', a, b, preferred_element_type=F32).astype(BF)  16.2 us
  transfers between devices with their start and end apart: 3, of which 0 were waited for; matrix products, arithmetic and copies ran while one was open for 4% of the time, Pallas kernels for 64%

profile of v2, /device:TPU:0, one launch (start us, length us, event | category | flops | bytes accessed | tf_op | source)
XLA Modules:
  0.0 510.0 jit_solution(8754577087889483319)
XLA Ops:
  7.3 1.2 convert_reduce_fusion
  8.6 1.3 fusion.11
  10.4 1.0 multiply_sine_fusion
  11.4 1.0 broadcast_power_fusion
  12.5 0.9 power_select_fusion.refs_8_.refs_14_
  13.3 1.9 fusion.9.refs_1_
  15.3 69.1 %mixer.1 = (bf16[4,128,2048]{2,1,0:T(8,128)(2,1)}, bf16[4,128,2048]{2,1,0:T(8,128)(2,1)}, bf16[512,512]{1,0:T(8,128)(2,1)}, bf16[512,512]{1,0:T(8,128)(2,1)}, bf...) custom-call(f32[2]{0:T(128)} %get-tuple-element.136.refs_0_, ...), custom_call_target="tpu_custom_call" | custom-call | tf_op jit(solution)/shard_map/mixer/pallas_call | solution.py:418
  84.4 1.4 fusion.22
  86.1 1.0 add_convert_fusion.2.refs_0_
  87.1 44.9 %mlp.1 = (bf16[4,128,2048]{2,1,0:T(8,128)(2,1)}, bf16[512,1024]{1,0:T(8,128)(2,1)}, bf16[512,1024]{1,0:T(8,128)(2,1)}, bf16[512,1024]{1,0:T(8,128)(2,1)}, bf16[4...) custom-call(bf16[128,2048]{1,0:T(8,128)(2,1)} %add_convert_fusion.2.refs_0_, ...), custom_call_target="tpu_custom_call" | custom-call | tf_op jit(solution)/shard_map/mlp/pallas_call | solution.py:535
  132.1 1.7 multiply_reduce_fusion
  134.3 1.1 copy-done.10
  135.7 4.3 convolution_convert_fusion
  140.0 6.3 %convolution_convert_fusion.1 = bf16[2048,1024]{1,0:T(8,128)(2,1)} fusion(bf16[512,2048]{1,0:T(8,128)(2,1)} %bitcast.85, bf16[512,1024]{1,0:T(8,128)(2,1)} %get-tuple-element.46), kind=kOutput, calls=%fused_computation.1 | convolution fusion | flops 2149580800 | bytes 7340032 | tf_op jit(solution)/shard_map/na,nb->ab/dot_general | solution.py:1031
  146.3 1.0 fusion.13.refs_1_
  147.2 0.8 copy-done.5
  148.0 5.6 %convolution_convert_fusion.2 = bf16[1024,2048]{1,0:T(8,128)(2,1)} fusion(bf16[512,1024]{1,0:T(8,128)(2,1)} %get-tuple-element.44, bf16[512,2048]{1,0:T(8,128)(2,1)S(1)} %bitcast.84), kind=kOutput, calls=%fused_computation.2 | convolution fusion | flops 2149580800 | bytes 7340032 | tf_op jit(solution)/shard_map/na,nb->ab/dot_general | solution.py:1031
  153.7 0.7 reduce-scatter.6.cloned.1.call-update
  154.4 0.7 reduce-scatter.8.cloned.1.call-update
  155.1 147.9 %mixer_back.1 = (bf16[4,128,2048]{2,1,0:T(8,128)(2,1)}, bf16[512,1024]{1,0:T(8,128)(2,1)}, bf16[512,1024]{1,0:T(8,128)(2,1)}, bf16[512,1024]{1,0:T(8,128)(2,1)},...) custom-call(f32[2]{0:T(128)} %get-tuple-element.136.refs_0_, bf16[128,2048]{1,0:T(8,128)(2,1)} %fusion.13.refs_1_, ...), custom_call_target="tpu_custom_call" | custom-call | tf_op jit(solution)/shard_map/mixer_back/pallas_call | solution.py:686
  303.1 1.6 fusion.12
  305.8 0.7 copy.34
  306.4 178.7 %weights_3.1 = (f32[4,256,1024]{2,1,0:T(8,128)}, f32[8,128]{1,0:T(8,128)}) custom-call(bf16[512,2048]{1,0:T(8,128)(2,1)} %bitcast.82, bf16[512,2048]{1,0:T(8,128)(2,1)} %bitcast.83, bf16[512,1024]{1,0:T(8,128)(2,1)} %get-tuple-element.61.refs_2_, bf16[512,1024]{1,0:T(8,128)(2,1)} %get-tuple-element.62.refs_3_, bf16[512,1024]{1,0:T(8,128)(2,1)} %get-tuple-element.63.refs_4_, ...), custom_call_target="tpu_custom_call" | custom-call | tf_op jit(solution)/shard_map/weights_3/pallas_call | solution.py:940
  485.1 3.6 slice_bitcast_fusion
  488.7 2.5 copy.31
  491.3 0.7 slice.36
  492.6 2.3 slice_bitcast_fusion.3
  494.9 0.9 fusion.14
  495.8 1.3 fusion.15
  497.1 2.1 convert_element_type.71
  499.2 2.1 convert_element_type.72
  501.3 2.1 convert_element_type.73
  (55 shorter events, 3.5 us)
Async XLA Ops:
  7.2 6.2 %copy-start = (bf16[1,128,2048]{2,1,0:T(8,128)(2,1)S(1)}, bf16[1,128,2048]{2,1,0:T(8,128)(2,1)}, u32[]{:S(2)}) copy-start(bf16[1,128,2048]{2,1,0:T(8,128)(2,1)} %param.14) | copy-start | bytes 1572868
  7.2 489.9 %reduce-scatter.4.cloned.1.call-start = ((), (), s32[]{:S(2)}) async-start(), calls=%async_computation.3 | async-start | bytes 4718592 | tf_op jit(solution)/shard_map/reduce_scatter | solution.py:1042
  84.4 1.7 copy-start.8
  84.4 1.7 copy-start.9
  132.1 1.8 copy-start.4
  133.8 1.6 copy-start.10
  133.8 1.9 copy-start.11
  140.0 6.3 %copy-start.3 = (bf16[1,128,2048]{2,1,0:T(8,128)(2,1)S(1)}, bf16[1,128,2048]{2,1,0:T(8,128)(2,1)}, u32[]{:S(2)}) copy-start(bf16[1,128,2048]{2,1,0:T(8,128)(2,1)} %param.27) | copy-start | bytes 1572868
  146.3 1.8 copy-start.5
  153.6 345.6 %reduce-scatter.6.cloned.1.call-start = ((), (), s32[]{:S(2)}) async-start(), calls=%async_computation.4 | async-start | bytes 4718592 | tf_op jit(solution)/shard_map/reduce_scatter | solution.py:1043
  154.4 346.9 %reduce-scatter.8.cloned.1.call-start = ((), (), s32[]{:S(2)}) async-start(), calls=%async_computation.5 | async-start | bytes 4718592 | tf_op jit(solution)/shard_map/reduce_scatter | solution.py:1044
  155.1 147.9 %copy-start.7 = (f32[2048]{0:T(1024)S(1)}, f32[2048]{0:T(1024)}, u32[]{:S(2)}) copy-start(f32[2048]{0:T(1024)} %param.23) | copy-start | bytes 24580
  303.0 1.6 copy-start.1
  492.0 2.9 copy-start.6
  492.5 3.2 copy-start.2
Sparse Core Ops, SparseCore 0:
  153.8 75.7 reduce-scatter.3
  231.9 60.0 reduce-scatter.5
  294.3 76.4 reduce-scatter.7

commit v3 on v2

--- a/solution.py
+++ b/solution.py
@@ -43,7 +43,7 @@
 
 
 class Gather:
-    def __init__(self, n, x, o, ssem, rsem):
+    def __init__(self, n, x, o, ssem, rsem, base=0):
         s, t = lax.axis_index("seq"), lax.axis_index("tp")
         self.n, self.t = n, t
         rows = x.shape[0]
@@ -54,19 +54,19 @@
             half = rows // 2
             lo, hi = pl.ds(0, half), pl.ds(half, half)
             self.first = [
-                remote(x.at[lo], o.at[t, lo], ssem, rsem, 0, dx),
-                remote(x.at[hi], o.at[t, hi], ssem, rsem, 1, dy),
-                remote(x.at[hi], o.at[t, hi], ssem, rsem, 2, dx),
-                remote(x.at[lo], o.at[t, lo], ssem, rsem, 3, dy),
+                remote(x.at[lo], o.at[base + t, lo], ssem, rsem, 0, dx),
+                remote(x.at[hi], o.at[base + t, hi], ssem, rsem, 1, dy),
+                remote(x.at[hi], o.at[base + t, hi], ssem, rsem, 2, dx),
+                remote(x.at[lo], o.at[base + t, lo], ssem, rsem, 3, dy),
             ]
             self.relay = [
-                remote(o.at[px, lo], o.at[px, lo], ssem, rsem, 4, dy),
-                remote(o.at[py, hi], o.at[py, hi], ssem, rsem, 5, dx),
+                remote(o.at[base + px, lo], o.at[base + px, lo], ssem, rsem, 4, dy),
+                remote(o.at[base + py, hi], o.at[base + py, hi], ssem, rsem, 5, dx),
             ]
         else:
             self.peers = [(s, (t + k) % n) for k in range(1, n)]
             self.first = [
-                remote(x, o.at[t], ssem, rsem, k, dev) for k, dev in enumerate(self.peers)
+                remote(x, o.at[base + t], ssem, rsem, k, dev) for k, dev in enumerate(self.peers)
             ]
             self.relay = []
 
@@ -208,12 +208,23 @@
     return [pltpu.VMEM(near, BF), pltpu.VMEM(far, BF), pltpu.VMEM(far, BF)]
 
 
+class Ends:
+    def __init__(self, chips):
+        s, t = lax.axis_index("seq"), lax.axis_index("tp")
+        chip, span = s // 2, 2 * chips
+        self.gives = (chip == 0) | (chip == chips - 1)
+        self.takes = (chip == 1) | (chip == chips - 2)
+        self.peers = [((s + 2) % span, t), ((s - 2 + span) % span, t)]
+        step = jnp.where(chip == 0, 2, jnp.where(chip == chips - 1, span - 2, 0))
+        self.mate = ((s + step) % span, t)
+
+
 class Chain:
-    def __init__(self, chips, heads, flip, fac, local, out, pair, enter, leave, ps, pr, zs, zr, bs, br):
+    def __init__(self, chips, heads, flip, fac, local, out, pair, enter, ps, pr, zs, zr, bs, br):
         s, t = lax.axis_index("seq"), lax.axis_index("tp")
         core, chip, span = s % 2, s // 2, 2 * chips
         self.chips, self.heads, self.fac = chips, heads, fac
-        self.local, self.out, self.pair, self.enter, self.leave = local, out, pair, enter, leave
+        self.local, self.out, self.pair, self.enter, self.leave = local, out, pair, enter, local
         self.sems = ps, pr, zs, zr, bs, br
         self.partner = (s + 1 - 2 * core, t)
         above, below = ((s + 2) % span, t), ((s - 2 + span) % span, t)
@@ -291,7 +302,7 @@
 
 def chain_scratch(pieces):
     dma = pltpu.SemaphoreType.DMA
-    return [pltpu.VMEM((pieces, DK, DV), BF)] * 3 + [dma((pieces,))] * 6
+    return [pltpu.VMEM((pieces, DK, DV), BF)] * 2 + [dma((pieces,))] * 6
 
 
 def dot(a, b, ca=1, cb=0):
@@ -312,6 +323,203 @@
     center = m - jnp.mean(m, -1, keepdims=True)
     inv = lax.rsqrt(jnp.mean(center * center, -1, keepdims=True) + EPS)
     return center * inv, inv
+
+
+class LineSums:
+    def __init__(self, chips, lo, hi, wide, deep, kinds, refs, swap=False):
+        s, t = lax.axis_index("seq"), lax.axis_index("tp")
+        self.core, self.chip, self.chips, self.lo, self.hi = s % 2, s // 2, chips, lo, hi
+        self.wide, self.deep, self.kinds = wide, deep, kinds
+        (
+            self.xs, self.ys, self.buf, self.out,
+            self.xsem, self.ysem, self.psx, self.prx, self.psy, self.pry, self.ssem, self.rsem,
+        ) = refs
+        self.units = len(deep)
+        self.swap = swap
+        self.tokens = self.ys.shape[1] // 2
+        self.cut = self.xs.shape[3]
+        span = 2 * chips
+        self.partner = (s + 1 - 2 * self.core, t)
+        self.above = ((s + 2) % span, t)
+        self.below = ((s - 2 + span) % span, t)
+        self.peers = [self.partner, self.above, self.below]
+
+    def cols(self, j, core):
+        return pl.ds(pl.multiple_of((2 * j + core) * self.cut, self.cut), self.cut)
+
+    def wide_own(self, kind, j):
+        return pltpu.make_async_copy(
+            self.wide[kind].at[:, self.cols(j, self.core)],
+            self.xs.at[kind, j, pl.ds(0, self.tokens)],
+            self.xsem.at[kind, j],
+        )
+
+    def wide_give(self, kind, j):
+        return pltpu.make_async_remote_copy(
+            src_ref=self.wide[kind].at[:, self.cols(j, 1 - self.core)],
+            dst_ref=self.xs.at[kind, j, pl.ds(self.tokens, self.tokens)],
+            send_sem=self.psx.at[kind, j],
+            recv_sem=self.prx.at[kind, j],
+            device_id=self.partner,
+            device_id_type=MESH,
+        )
+
+    def deep_own(self, u):
+        return pltpu.make_async_copy(
+            self.deep[u], self.ys.at[u, pl.ds(0, self.tokens)], self.ysem.at[u]
+        )
+
+    def deep_give(self, u):
+        return remote(
+            self.deep[u], self.ys.at[u, pl.ds(self.tokens, self.tokens)], self.psy, self.pry, u,
+            self.partner,
+        )
+
+    def adds(self):
+        return (self.chip >= self.lo) & (self.chip <= self.hi)
+
+    def share(self, u):
+        @pl.when(self.adds())
+        def _():
+            if self.kinds[u] not in self.kinds[:u]:
+                for j in range(self.chips):
+                    self.wide_give(self.kinds[u], j).start()
+                    self.wide_own(self.kinds[u], j).start()
+            self.deep_give(u).start()
+            self.deep_own(u).start()
+
+    def ready(self, u):
+        @pl.when(self.adds())
+        def _():
+            self.deep_own(u).wait()
+            self.deep_give(u).wait_recv()
+            if self.kinds[u] not in self.kinds[:u]:
+                for j in range(self.chips):
+                    self.wide_own(self.kinds[u], j).wait()
+                    self.wide_give(self.kinds[u], j).wait_recv()
+
+    def up(self, u, j):
+        return remote(
+            self.buf.at[u, j], self.buf.at[u, j], self.ssem.at[u], self.rsem.at[u], j, self.above
+        )
+
+    def down(self, u, j):
+        slot = jnp.where(j == self.chip - 1, self.chips, j)
+        return pltpu.make_async_remote_copy(
+            src_ref=self.buf.at[u, j],
+            dst_ref=self.buf.at[u, slot],
+            send_sem=self.ssem.at[u, j],
+            recv_sem=self.rsem.at[u, slot],
+            device_id=self.below,
+            device_id_type=MESH,
+        )
+
+    def arrived(self, u, slot):
+        remote(
+            self.buf.at[u, slot], self.buf.at[u, slot], self.ssem.at[u], self.rsem.at[u], slot,
+            self.above,
+        ).wait_recv()
+        return self.buf[u, slot].astype(F32)
+
+    def product(self, u, j):
+        kind = 0
+        for w in range(self.units):
+            if self.kinds[w]:
+                kind = kind + jnp.where(u == w, self.kinds[w], 0)
+        if self.swap:
+            return dot(self.ys[u], self.xs[kind, j], 0, 0)
+        return dot(self.xs[kind, j], self.ys[u], 0, 0)
+
+    def order(self, k):
+        rights = self.chips - 1 - self.chip
+        return jnp.where(
+            self.chip < self.chips // 2,
+            jnp.where(k < rights, self.chips - 1 - k, k - rights),
+            jnp.where(k < self.chip, k, self.chips - 1 - (k - self.chip)),
+        )
+
+    def step(self, u, k):
+        chip = self.chip
+        j = self.order(k)
+
+        @pl.when(self.adds())
+        def _():
+            total = self.product(u, j)
+
+            @pl.when(((j > chip) & (chip == self.lo)) | ((j < chip) & (chip == self.hi)))
+            def _():
+                self.buf[u, j] = total.astype(BF)
+
+            @pl.when(((j > chip) & (chip > self.lo)) | ((j < chip) & (chip < self.hi)))
+            def _():
+                self.buf[u, j] = (total + self.arrived(u, j)).astype(BF)
+
+            @pl.when(j > chip)
+            def _():
+                self.up(u, j).start()
+
+            @pl.when(j < chip)
+            def _():
+                self.down(u, j).start()
+
+    def finish(self, u):
+        chip = self.chip
+
+        @pl.when(self.adds())
+        def _():
+            self.out[u] = self.product(u, chip)
+
+        @pl.when((chip < self.lo) | (chip > self.hi))
+        def _():
+            self.out[u] = jnp.zeros(self.out.shape[1:], F32)
+
+        @pl.when(chip > self.lo)
+        def _():
+            self.out[u] += self.arrived(u, chip)
+
+        @pl.when(chip < self.hi)
+        def _():
+            self.out[u] += self.arrived(u, self.chips)
+
+    def drain(self):
+        @pl.when(self.adds())
+        def _():
+            @pl.loop(0, self.units)
+            def _(u):
+                @pl.loop(0, self.chips)
+                def _(j):
+                    @pl.when(j > self.chip)
+                    def _():
+                        self.up(u, j).wait_send()
+
+                    @pl.when(j < self.chip)
+                    def _():
+                        self.down(u, j).wait_send()
+
+            for u in range(self.units):
+                self.deep_give(u).wait_send()
+            for kind in range(max(self.kinds) + 1):
+                for j in range(self.chips):
+                    self.wide_give(kind, j).wait_send()
+
+
+def line_scratch(chips, units, kinds, tokens, cut, width, swap=False):
+    dma = pltpu.SemaphoreType.DMA
+    block = (width, cut) if swap else (cut, width)
+    return [
+        pltpu.VMEM((kinds, chips, 2 * tokens, cut), BF),
+        pltpu.VMEM((units, 2 * tokens, width), BF),
+        pltpu.VMEM((units, chips + 1) + block, BF),
+        pltpu.VMEM((units,) + block, F32),
+        dma((kinds, chips)),
+        dma((units,)),
+        dma((kinds, chips)),
+        dma((kinds, chips)),
+        dma((units,)),
+        dma((units,)),
+        dma((units, chips + 1)),
+        dma((units, chips + 1)),
+    ]
 
 
 def mixer_kernel(n, chips, heads, *refs):
@@ -321,11 +529,14 @@
         wk, wv, wq, ws, wo, acc, parts, local,
     ) = refs[:31]
     near, far, hold = refs[31:34]
-    chain_refs = refs[34:43]
-    wsem, gs, gr, os, orr, ss, sr = refs[43:]
+    chain_refs = refs[34:42]
+    wsem, gs, gr, os, orr, ss, sr, og_near, es, er, ns, nr = refs[42:]
     rows = x.shape[0]
     gather = Gather(n, x, x_all, gs, gr)
     gather_og = Gather(n, og, og_all, os, orr)
+    ends = Ends(chips)
+    gather_near = Gather(n, og_near, og_all, ns, nr, n)
+    hand = remote(og, og_near, es, er, 0, ends.mate)
     scatter = Scatter(n, parts, near, far, hold, ss, sr)
     chain = Chain(chips, heads, False, fac, local, prior, *chain_refs)
     loads = [
@@ -337,6 +548,11 @@
     greet(gather.peers + chain.peers)
     gather.start()
     gather_og.start()
+
+    @pl.when(ends.gives)
+    def _():
+        hand.start()
+
     me = gather.source(0)
     x_all[me] = x[...]
     og_all[me] = og[...]
@@ -367,11 +583,22 @@
 
     loads[4].wait()
 
+    @pl.when(ends.takes)
+    def _():
+        hand.wait_recv()
+        gather_near.start()
+        og_all[n + me] = og_near[...]
+
     @pl.loop(0, n)
     def _(step):
         i = (step + 1) % n
         j = gather.source(i)
         gather_og.arrive(i)
+
+        @pl.when(ends.takes & (step > 0))
+        def _():
+            gather_near.arrive(step)
+
         at = pl.ds(pl.multiple_of(j * rows, rows), rows)
         for h in range(heads):
             vc = slice(h * DV, (h + 1) * DV)
@@ -396,6 +623,15 @@
     scatter.finish(write)
     gather.drain()
     gather_og.drain()
+
+    @pl.when(ends.gives)
+    def _():
+        hand.wait_send()
+
+    @pl.when(ends.takes)
+    def _():
+        gather_near.drain()
+
     scatter.drain()
 
     @pl.loop(0, n * heads)
@@ -419,7 +655,7 @@
         functools.partial(mixer_kernel, n, chips, heads),
         out_shape=(
             shape((n, rows, model), BF),
-            shape((n, rows, model), BF),
+            shape((2 * n, rows, model), BF),
             shape((total, heads * DK), BF),
             shape((total, heads * DK), BF),
             shape((total, heads * DV), BF),
@@ -439,7 +675,9 @@
         ]
         + scatter_scratch(n, rows, model)
         + chain_scratch(pieces)
-        + [dma((5,))] + [dma((sems,))] * 6,
+        + [dma((5,))]
+        + [dma((sems,))] * 6
+        + [pltpu.VMEM((rows, model), BF), dma((1,)), dma((1,)), dma((sems,)), dma((sems,))],
         compiler_params=params(cid),
         name="mixer",
     )(fac, x, og, wk, wv, wq, ws, wo, decay, qfac, kfac, cos, sin)
@@ -449,28 +687,33 @@
 GELU_A = 0.044715
 
 
-def mlp_kernel(n, *refs):
+def mlp_kernel(n, chips, *refs):
     (
         x, og_all, wg_h, wu_h, wd_h,
         x_all, hidden, gate_low, upper_low, mlp_parts, grad_two,
         wg, wu, wd, hg, acc_g, acc_u, acc, parts, near, far, hold,
-        wsem, gs, gr, ss, sr,
+        wsem, gs, gr, ss, sr, es, er,
     ) = refs
     rows = x.shape[0]
     gather = Gather(n, x, x_all, gs, gr)
     scatter = Scatter(n, parts, near, far, hold, ss, sr)
+    ends = Ends(chips)
     loads = [
         pltpu.make_async_copy(a, w, wsem.at[i])
         for i, (a, w) in enumerate(((wd_h, wd), (wg_h, wg), (wu_h, wu)))
     ]
     for load in loads:
         load.start()
-    greet(gather.peers)
+    greet(gather.peers + ends.peers)
     gather.start()
     me = gather.source(0)
     x_all[me] = x[...]
     loads[0].wait()
 
+    def hand(i):
+        j = gather.source(i)
+        return remote(x_all.at[j], x_all.at[n + j], es, er, i, ends.mate)
+
     @pl.loop(0, n)
     def _(j):
         at = pl.ds(pl.multiple_of(j * rows, rows), rows)
@@ -480,20 +723,17 @@
     loads[2].wait()
     slab = 16
 
-    @pl.loop(0, n)
-    def _(i):
-        j = gather.source(i)
-        gather.arrive(i)
-        start = pl.multiple_of(j * rows, rows)
-        at = pl.ds(start, rows)
-        acc_g[...] = dot(x_all[j], wg[...])
-        acc_u[...] = dot(x_all[j], wu[...])
+    def units(block, back_at):
+        start = pl.multiple_of(block * rows, rows)
+        acc_g[...] = dot(x_all[block], wg[...])
+        acc_u[...] = dot(x_all[block], wu[...])
 
         @pl.loop(0, rows // slab)
         def _(r):
             here = pl.ds(pl.multiple_of(r * slab, slab), slab)
             there = pl.ds(pl.multiple_of(start + r * slab, slab), slab)
-            g, u, back = acc_g[here], acc_u[here], hg[there]
+            g, u = acc_g[here], acc_u[here]
+            back = hg[pl.ds(pl.multiple_of(back_at + r * slab, slab), slab)]
             square = g * g
             th = jnp.tanh(GELU_C * (g + GELU_A * (square * g)))
             half = 0.5 * (1.0 + th)
@@ -503,27 +743,62 @@
             gate_low[there] = (back * u * slope).astype(BF)
             upper_low[there] = (back * gelu).astype(BF)
 
+    @pl.loop(0, n)
+    def _(i):
+        j = gather.source(i)
+        gather.arrive(i)
+
+        @pl.when(ends.gives)
+        def _():
+            hand(i).start()
+
+        units(j, j * rows)
+        at = pl.ds(pl.multiple_of(j * rows, rows), rows)
         acc[...] = dot(gate_low[at], wg[...], 1, 1)
         parts[j] = (acc[...] + dot(upper_low[at], wu[...], 1, 1)).astype(BF)
         scatter.send(i)
+
+    def extra(i):
+        @pl.when(ends.takes)
+        def _():
+            j = gather.source(i)
+            hg[pl.ds(0, rows)] = dot(og_all[n + j], wd[...], 1, 1)
+            hand(i).wait_recv()
+            units(n + j, 0)
+
+    @pl.loop(0, n // 2)
+    def _(i):
+        extra(i)
+
+    scatter.relay()
 
     @pl.loop(0, n)
     def _(j):
         at = pl.ds(pl.multiple_of(j * rows, rows), rows)
         mlp_parts[j] = dot(hidden[at], wd[...]).astype(BF)
 
-    scatter.relay()
-
     def write(cols, total):
         grad_two[:, cols] = total
 
     scatter.finish(write)
+
+    @pl.loop(n // 2, n)
+    def _(i):
+        extra(i)
+
     gather.drain()
     scatter.drain()
 
+    @pl.when(ends.gives)
+    def _():
+        @pl.loop(0, n)
+        def _(i):
+            hand(i).wait_send()
+
 
 def mlp(x, og_all, wg, wu, wd, cid):
     n = lax.axis_size("tp")
+    chips = lax.axis_size("seq") // 2
     rows, model = x.shape
     width = wg.shape[1]
     total = n * rows
@@ -533,12 +808,12 @@
     hbm = pl.BlockSpec(memory_space=pl.ANY)
     shape = jax.ShapeDtypeStruct
     return pl.pallas_call(
-        functools.partial(mlp_kernel, n),
+        functools.partial(mlp_kernel, n, chips),
         out_shape=(
-            shape((n, rows, model), BF),
-            shape((total, width), BF),
-            shape((total, width), BF),
-            shape((total, width), BF),
+            shape((2 * n, rows, model), BF),
+            shape((2 * total, width), BF),
+            shape((2 * total, width), BF),
+            shape((2 * total, width), BF),
             shape((n, rows, model), BF),
             shape((rows, model), F32),
         ),
@@ -553,7 +828,9 @@
             pltpu.VMEM((n, rows, model), BF),
         ]
         + scatter_scratch(n, rows, model)
-        + [dma((3,))] + [dma((sems,))] * 4,
+        + [dma((3,))]
+        + [dma((sems,))] * 4
+        + [dma((n,)), dma((n,))],
         compiler_params=params(cid),
         name="mlp",
     )(x, og_all, wg, wu, wd)
@@ -566,8 +843,8 @@
         wo, wq, wk, wv, ws, mixed_low, acc, parts, local, later,
     ) = refs[:35]
     near, far, hold, mlp_near, mlp_far, mlp_hold = refs[35:41]
-    chain_refs = refs[41:50]
-    wsem, gs, gr, ss, sr, ms, mr = refs[50:]
+    chain_refs = refs[41:49]
+    wsem, gs, gr, ss, sr, ms, mr = refs[49:]
     rows = res.shape[0]
     gather = Gather(n, res, res_all, gs, gr)
     scatter = Scatter(n, parts, near, far, hold, ss, sr)
@@ -713,28 +990,21 @@
     )(fac, res, wo, wq, wk, wv, ws, q, k, v, sp, mx, prior, mlp_parts, decay, qfac, kfac, cos, sin)
 
 
-def weights_kernel(
-    chips, units, kinds, *refs
-):
-    kind_count = max(kinds) + 1
-    wide = refs[:kind_count]
-    deep = refs[kind_count : kind_count + units]
-    vec = refs[kind_count + units]
-    rest = refs[kind_count + units + 1 :]
-    vec_near, vec_sum, vec_far, vs, vr, us, ur = rest[-7:]
-    rest = rest[:-7]
-    o_ref, vec_out, xs, ys, from_low, from_high, out, xsem, ysem, psx, prx, psy, pry, ssem, lsem, hsem = rest
-    s = lax.axis_index("seq")
-    t = lax.axis_index("tp")
-    core = s % 2
-    chip = s // 2
-    tokens = ys.shape[1] // 2
-    cut = xs.shape[3]
-    span = 2 * chips
-    partner = (s + 1 - 2 * core, t)
-    above = ((s + 2) % span, t)
-    below = ((s - 2 + span) % span, t)
-    tp = vec.shape[0]
+def weights_kernel(chips, *refs):
+    (
+        two, og, hidden, gate_low, up_low, one, res, swish_low, gated, value_low, qk_low, vec,
+        down_o, gate_o, up_o, swish_o, mixer_o, value_o, query_o, key_o, vec_out,
+    ) = refs[:21]
+    mlp = LineSums(
+        chips, 1, chips - 2, (two, og), (gate_low, up_low, hidden), (0, 0, 1), refs[21:33]
+    )
+    mix = LineSums(
+        chips, 0, chips - 1, (one, res), (swish_low, gated, value_low, qk_low), (0, 1, 0, 0),
+        refs[33:45],
+    )
+    turned, osem, vec_near, vec_sum, vec_far, vs, vr, us, ur = refs[45:]
+    s, t = lax.axis_index("seq"), lax.axis_index("tp")
+    span, tp = 2 * chips, vec.shape[0]
     ring = [((s + d) % span, t) for d in range(1, span)]
     cross = [(s, (t + d) % tp) for d in range(1, tp)]
     greet(ring + cross)
@@ -748,146 +1018,28 @@
     ]
     for copy in vec_first:
         copy.start()
-
-    def wide_own(kind, j):
-        cols = pl.ds(pl.multiple_of((2 * j + core) * cut, cut), cut)
-        return pltpu.make_async_copy(
-            wide[kind].at[:, cols], xs.at[kind, j, pl.ds(0, tokens)], xsem.at[kind, j]
-        )
-
-    def wide_give(kind, j):
-        cols = pl.ds(pl.multiple_of((2 * j + 1 - core) * cut, cut), cut)
-        return pltpu.make_async_remote_copy(
-            src_ref=wide[kind].at[:, cols],
-            dst_ref=xs.at[kind, j, pl.ds(tokens, tokens)],
-            send_sem=psx.at[kind, j],
-            recv_sem=prx.at[kind, j],
-            device_id=partner,
-            device_id_type=MESH,
-        )
-
-    def deep_own(u):
-        return pltpu.make_async_copy(deep[u], ys.at[u, pl.ds(0, tokens)], ysem.at[u])
-
-    def deep_give(u):
-        return pltpu.make_async_remote_copy(
-            src_ref=deep[u],
-            dst_ref=ys.at[u, pl.ds(tokens, tokens)],
-            send_sem=psy.at[u],
-            recv_sem=pry.at[u],
-            device_id=partner,
-            device_id_type=MESH,
-        )
-
-    seen = set()
-    for u in range(units):
-        deep_give(u).start()
-        deep_own(u).start()
-        if kinds[u] not in seen:
-            seen.add(kinds[u])
-            for j in range(chips):
-                wide_give(kinds[u], j).start()
-                wide_own(kinds[u], j).start()
-
-    def ready(u):
-        deep_own(u).wait()
-        deep_give(u).wait_recv()
-        if kinds[u] not in kinds[:u]:
-            for j in range(chips):
-                wide_own(kinds[u], j).wait()
-                wide_give(kinds[u], j).wait_recv()
-
-    def up(u, j):
-        return pltpu.make_async_remote_copy(
-            src_ref=out.at[u, j],
-            dst_ref=from_low.at[u, j],
-            send_sem=ssem.at[u, j],
-            recv_sem=lsem.at[u, j],
-            device_id=above,
-            device_id_type=MESH,
-        )
-
-    def down(u, j):
-        return pltpu.make_async_remote_copy(
-            src_ref=out.at[u, j],
-            dst_ref=from_high.at[u, j],
-            send_sem=ssem.at[u, j],
-            recv_sem=hsem.at[u, j],
-            device_id=below,
-            device_id_type=MESH,
-        )
-
-    def kind_of(u):
-        kind = 0
-        for w in range(units):
-            if kinds[w]:
-                kind = kind + jnp.where(u == w, kinds[w], 0)
-        return kind
-
-    def product(u, j):
-        return lax.dot_general(
-            xs[kind_of(u), j], ys[u], (((0,), (0,)), ((), ())), preferred_element_type=F32
-        )
-
-    low_half = chip < chips // 2
-    rights = chips - 1 - chip
-
-    def finish(u):
-        total = product(u, chip)
-        o_ref[u] = total
-
-        @pl.when(chip > 0)
-        def _():
-            up(u, chip).wait_recv()
-            o_ref[u] = o_ref[u] + from_low[u, chip].astype(F32)
-
-        @pl.when(chip < chips - 1)
-        def _():
-            down(u, chip).wait_recv()
-            o_ref[u] = o_ref[u] + from_high[u, chip].astype(F32)
-
-    @pl.loop(0, units)
+    for u in range(mix.units):
+        if u < mlp.units:
+            mlp.share(u)
+        mix.share(u)
+
+    @pl.loop(0, mix.units)
     def _(u):
-        for w in range(units):
+        for w in range(mix.units):
 
             @pl.when(u == w)
             def _(w=w):
-                ready(w)
+                if w < mlp.units:
+                    mlp.ready(w)
+                mix.ready(w)
 
         @pl.loop(0, chips - 1)
         def _(k):
-            j = jnp.where(
-                low_half,
-                jnp.where(k < rights, chips - 1 - k, k - rights),
-                jnp.where(k < chip, k, chips - 1 - (k - chip)),
-            )
-            total = product(u, j)
-
-            @pl.when(j > chip)
-            def _():
-                @pl.when(chip == 0)
-                def _():
-                    out[u, j] = total.astype(BF)
-
-                @pl.when(chip > 0)
-                def _():
-                    up(u, j).wait_recv()
-                    out[u, j] = (total + from_low[u, j].astype(F32)).astype(BF)
-
-                up(u, j).start()
-
-            @pl.when(j < chip)
-            def _():
-                @pl.when(chip == chips - 1)
-                def _():
-                    out[u, j] = total.astype(BF)
-
-                @pl.when(chip < chips - 1)
-                def _():
-                    down(u, j).wait_recv()
-                    out[u, j] = (total + from_high[u, j].astype(F32)).astype(BF)
-
-                down(u, j).start()
+            @pl.when(u < mlp.units)
+            def _():
+                mlp.step(u, k)
+
+            mix.step(u, k)
 
         @pl.when(u == 0)
         def _():
@@ -900,78 +1052,87 @@
 
         @pl.when(u > 0)
         def _():
-            finish(u - 1)
-
+            mlp.finish(u - 1)
+            mix.finish(u - 1)
+
+    half = mix.out.shape[2] // 2
+    lo, hi = pl.ds(0, half), pl.ds(half, half)
+    turned[...] = mlp.out[2].T
+    pairs = [
+        (mlp.out.at[0], gate_o),
+        (mlp.out.at[1], up_o),
+        (mix.out.at[0], swish_o),
+        (turned, down_o),
+        (turned, mixer_o),
+        (mix.out.at[2], value_o),
+        (mix.out.at[3, :, lo], query_o),
+        (mix.out.at[3, :, hi], key_o),
+    ]
+    copies = [pltpu.make_async_copy(a, b, osem.at[i]) for i, (a, b) in enumerate(pairs)]
+    for i in (3, 0, 1, 2, 5):
+        copies[i].start()
+    copies[3].wait()
+    turned[...] = mix.out[1].T
+    copies[4].start()
+    mix.finish(mix.units - 1)
+    for copy in copies[6:]:
+        copy.start()
     vec_total = vec_sum[s]
     for copy in vec_last:
         copy.wait_recv()
     vec_out[...] = vec_total + jnp.sum(vec_far[...], 0)
-    finish(units - 1)
-
-    @pl.loop(0, units)
-    def _(u):
-        @pl.loop(0, chips)
-        def _(j):
-            @pl.when(j > chip)
-            def _():
-                up(u, j).wait_send()
-
-            @pl.when(j < chip)
-            def _():
-                down(u, j).wait_send()
-
     for copy in vec_first + vec_last:
         copy.wait_send()
-    for u in range(units):
-        deep_give(u).wait_send()
-    for kind in range(kind_count):
-        for j in range(chips):
-            wide_give(kind, j).wait_send()
-
-
-def weight_sums(wide, deep, vec, kinds, cid):
+    mlp.drain()
+    mix.drain()
+    for i, copy in enumerate(copies):
+        if i != 3:
+            copy.wait()
+
+
+def weight_sums(two, og, hidden, gate_low, up_low, one, res, swish_low, gated, value_low, qk_low, vec, cid):
     chips = lax.axis_size("seq") // 2
-    tokens, model = wide[0].shape
-    width = deep[0].shape[1]
-    units = len(deep)
+    tokens, model = one.shape
+    width = gated.shape[1]
+    mlp_tokens, mlp_width = gate_low.shape
+    keys = qk_low.shape[1] // 2
     cut = model // (2 * chips)
-    block = (units, chips, cut, width)
     dma = pltpu.SemaphoreType.DMA
+    vmem = pl.BlockSpec(memory_space=pltpu.VMEM)
+    hbm = pl.BlockSpec(memory_space=pl.ANY)
+    shape = lambda *a: jax.ShapeDtypeStruct(a, F32)
+    ring, cross = 2 * chips - 1, vec.shape[0] - 1
     return pl.pallas_call(
-        functools.partial(weights_kernel, chips, units, kinds),
+        functools.partial(weights_kernel, chips),
         out_shape=(
-            jax.ShapeDtypeStruct((units, cut, width), F32),
-            jax.ShapeDtypeStruct(vec.shape[2:], F32),
+            shape(mlp_width, cut),
+            shape(cut, mlp_width),
+            shape(cut, mlp_width),
+            shape(cut, width),
+            shape(width, cut),
+            shape(cut, width),
+            shape(cut, keys),
+            shape(cut, keys),
+            shape(*vec.shape[2:]),
         ),
-        in_specs=[pl.BlockSpec(memory_space=pl.ANY)] * (len(wide) + units)
-        + [pl.BlockSpec(memory_space=pltpu.VMEM)],
-        out_specs=(pl.BlockSpec(memory_space=pltpu.VMEM),) * 2,
-        scratch_shapes=[
-            pltpu.VMEM((len(wide), chips, 2 * tokens, cut), BF),
-            pltpu.VMEM((units, 2 * tokens, width), BF),
-            pltpu.VMEM(block, BF),
-            pltpu.VMEM(block, BF),
-            pltpu.VMEM(block, BF),
-            dma((len(wide), chips)),
-            dma((units,)),
-            dma((len(wide), chips)),
-            dma((len(wide), chips)),
-            dma((units,)),
-            dma((units,)),
-            dma((units, chips)),
-            dma((units, chips)),
-            dma((units, chips)),
-            pltpu.VMEM((vec.shape[0] - 1,) + vec.shape[1:], F32),
+        in_specs=[hbm] * 11 + [vmem],
+        out_specs=(hbm,) * 8 + (vmem,),
+        scratch_shapes=line_scratch(chips, 3, 2, mlp_tokens, cut, mlp_width)
+        + line_scratch(chips, 4, 2, tokens, cut, width)
+        + [
+            pltpu.VMEM((width, cut), F32),
+            dma((8,)),
+            pltpu.VMEM((cross,) + vec.shape[1:], F32),
             pltpu.VMEM(vec.shape[1:], F32),
-            pltpu.VMEM((2 * chips - 1,) + vec.shape[2:], F32),
-            dma((vec.shape[0] - 1,)),
-            dma((vec.shape[0] - 1,)),
-            dma((2 * chips - 1,)),
-            dma((2 * chips - 1,)),
+            pltpu.VMEM((ring,) + vec.shape[2:], F32),
+            dma((cross,)),
+            dma((cross,)),
+            dma((ring,)),
+            dma((ring,)),
         ],
         compiler_params=params(cid),
-        name=f"weights_{cid}",
-    )(*wide, *deep, vec)
+        name="weights",
+    )(two, og, hidden, gate_low, up_low, one, res, swish_low, gated, value_low, qk_low, vec)
 
 
 def layer_norm(values, gain, bias):
@@ -1028,23 +1189,11 @@
         normed_two, grad_all, gate_weight, up_weight, down_weight, 1
     )
     flat = lambda a: a.reshape(-1, model)
-    product = lambda a, b: jnp.einsum("na,nb->ab", a, b, preferred_element_type=F32).astype(BF)
     _, pull_two = jax.vjp(layer_norm, hidden_res, mlp_gain, mlp_bias)
     res_back, mlpgain_part, mlpbias_part = pull_two(normed_two_grad)
     res_grad = cotangent.astype(F32) + res_back
-    down_low = product(hidden, flat(grad_all))
-    gatew_low = product(flat(two_all), gate_low)
-    upw_low = product(flat(two_all), upper_low)
-    down_low, gatew_low, upw_low, res_low = lax.optimization_barrier(
-        (down_low, gatew_low, upw_low, res_grad.astype(BF))
-    )
-    scatter = functools.partial(lax.psum_scatter, axis_name="seq", tiled=True)
-    gate_grad = scatter(gatew_low, scatter_dimension=0).astype(F32)
-    up_grad = scatter(upw_low, scatter_dimension=0).astype(F32)
-    down_grad = scatter(down_low, scatter_dimension=1).astype(F32)
-
     res_all, swish_low, value_low, qk_low, normed_one_grad, mlp_out = mixer_back(
-        block_fac, res_low, output_weight, query_weight, key_weight, value_weight, swish_weight,
+        block_fac, res_grad.astype(BF), output_weight, query_weight, key_weight, value_weight, swish_weight,
         query, key, value, swish_pre, mixed, prior, mlp_parts, decay_mat, query_fac, key_fac,
         cosine, sine, 2,
     )
@@ -1058,18 +1207,21 @@
     vectors = jnp.stack([attngain_part, attnbias_part, mlpgain_part, mlpbias_part])
     vectors = vectors.reshape(4, seqs, tps, each).transpose(2, 1, 0, 3).reshape(tps, seqs, 4 * each)
     vectors = jnp.pad(vectors, ((0, 0), (0, 0), (0, 1024 - 4 * each))).reshape(tps, seqs, 8, 128)
-    sums, vector_sums = weight_sums(
-        (flat(one_all), flat(res_all)), (swish_low, gated, value_low, qk_low), vectors, (0, 1, 0, 0), 3
+    down_grad, gate_grad, up_grad, swish_grad, mixer_grad, value_grad, query_grad, key_grad, vector_sums = (
+        weight_sums(
+            flat(two_all), flat(grad_all), hidden, gate_low, upper_low, flat(one_all), flat(res_all), swish_low, gated,
+            value_low, qk_low, vectors, 3,
+        )
     )
     vector_sums = vector_sums.reshape(-1)[: 4 * each].reshape(4, each)
     return (
         outputs[None],
         input_grad[None],
-        sums[3, :, : heads * DK],
-        sums[3, :, heads * DK :],
-        sums[2],
-        sums[0],
-        sums[1].T,
+        query_grad,
+        key_grad,
+        value_grad,
+        swish_grad,
+        mixer_grad,
         gate_grad,
         up_grad,
         down_grad,

time: 511 us -> 454 us (0.89)
  Pallas kernels: 441 us -> 423 us
  matrix products: 16.2 us -> 0 us
  between operations: 14 us -> 0.83 us
    pallas_call x1, Pallas kernels: 148 us -> 91.1 us  [mixer_back(): pl.pallas_call(functools.partial(mixer_back_kernel, n, chips, heads), out...]
    pallas_call x2, Pallas kernels: 224 us -> 261 us  [the longest x1 179 us: weight_sums(): pl.pallas_call(functools.partial(weights_kernel, chips), out_shape=(shape...]
    dot_general x3 -> x0, matrix products: 16.2 us -> none  [shards(): jnp.einsum('na,nb->ab', a, b, preferred_element_type=F32).astype(BF)]
    convert_element_type x3 -> x0, other arithmetic: 6.34 us -> none  [the longest x1 2.13 us: shards(): gate_grad = scatter(gatew_low, scatter_dimension=0).astype(F32)]
  transfers between devices with their start and end apart: 3 -> 0, of which waited for: 0 -> 0; matrix products, arithmetic and copies ran while one was open for 4% -> 0% of each run, Pallas kernels for 64% -> 0%
where the time goes in v3:
time: 454 us
  Pallas kernels  423 us (93%)
  other arithmetic  18.8 us (4%)
  local copies, waits for them, and re-layouts  11.7 us (3%)
    pallas_call x1, Pallas kernels, weight_sums(): pl.pallas_call(functools.partial(weights_kernel, chips), out_shape=(shape...  179 us
    pallas_call x1, Pallas kernels, mixer_back(): pl.pallas_call(functools.partial(mixer_back_kernel, n, chips, heads), out...  91.1 us
    pallas_call x1, Pallas kernels, mlp(): pl.pallas_call(functools.partial(mlp_kernel, n, chips), out_shape=(shape(...  82.2 us
    pallas_call x1, Pallas kernels, mixer(): pl.pallas_call(functools.partial(mixer_kernel, n, chips, heads), out_shap...  70.3 us

profile of v3, /device:TPU:0, one launch (start us, length us, event | category | flops | bytes accessed | tf_op | source)
XLA Modules:
  0.0 453.9 jit_solution(5114987668252954299)
XLA Ops:
  0.6 1.2 convert_reduce_fusion
  1.8 1.3 fusion.11
  3.2 2.3 fusion.9.refs_1_
  5.4 0.5 exponential_subtract_fusion
  6.0 1.0 broadcast_power_fusion
  7.0 1.0 multiply_sine_fusion
  8.1 0.9 power_select_fusion.refs_8_.refs_14_
  9.0 70.3 %mixer.1 = (bf16[4,128,2048]{2,1,0:T(8,128)(2,1)}, bf16[8,128,2048]{2,1,0:T(8,128)(2,1)}, bf16[512,512]{1,0:T(8,128)(2,1)}, bf16[512,512]{1,0:T(8,128)(2,1)}, bf...) custom-call(f32[2]{0:T(128)} %get-tuple-element.95.refs_0_, ...), custom_call_target="tpu_custom_call" | custom-call | tf_op jit(solution)/shard_map/mixer/pallas_call | solution.py:654
  79.3 1.4 fusion.22
  81.0 1.0 add_convert_fusion.2.refs_0_
  82.0 82.2 %mlp.1 = (bf16[8,128,2048]{2,1,0:T(8,128)(2,1)}, bf16[1024,1024]{1,0:T(8,128)(2,1)}, bf16[1024,1024]{1,0:T(8,128)(2,1)}, bf16[1024,1024]{1,0:T(8,128)(2,1)}, bf1...) custom-call(bf16[128,2048]{1,0:T(8,128)(2,1)} %add_convert_fusion.2.refs_0_, ...), custom_call_target="tpu_custom_call" | custom-call | tf_op jit(solution)/shard_map/mlp/pallas_call | solution.py:810
  164.3 1.7 multiply_reduce_fusion
  166.0 0.4 fusion.21
  166.5 0.6 copy-done.2
  167.1 1.0 fusion.13.refs_1_
  168.0 91.1 %mixer_back.1 = (bf16[4,128,2048]{2,1,0:T(8,128)(2,1)}, bf16[512,1024]{1,0:T(8,128)(2,1)}, bf16[512,1024]{1,0:T(8,128)(2,1)}, bf16[512,1024]{1,0:T(8,128)(2,1)},...) custom-call(f32[2]{0:T(128)} %get-tuple-element.95.refs_0_, bf16[128,2048]{1,0:T(8,128)(2,1)} %fusion.13.refs_1_, ...), custom_call_target="tpu_custom_call" | custom-call | tf_op jit(solution)/shard_map/mixer_back/pallas_call | solution.py:963
  259.1 1.6 fusion.12
  260.8 0.6 fusion.10
  261.8 0.7 copy.31
  262.5 179.1 %weights.1 = (f32[1024,256]{1,0:T(8,128)}, f32[256,1024]{1,0:T(8,128)}, f32[256,1024]{1,0:T(8,128)}, f32[256,1024]{1,0:T(8,128)}, f32[1024,256]{1,0:T(8,128)}, /...) custom-call(bf16[1024,2048]{1,0:T(8,128)(2,1)} %bitcast.65, ...), custom_call_target="tpu_custom_call" | custom-call | tf_op jit(solution)/shard_map/weights/pallas_call | solution.py:1105
  441.6 0.7 slice.16
  442.4 0.5 slice_bitcast_fusion
  442.9 2.5 fusion.15
  445.5 0.9 fusion.14
  446.5 0.8 copy.40
  447.3 0.8 copy.41
  448.1 1.0 copy.42
  449.1 1.0 copy.43
  450.0 1.0 copy.44
  451.0 1.0 copy.45
  452.0 1.0 copy.46
  453.0 1.0 copy.47
  (53 shorter events, 1.1 us)
Async XLA Ops:
  9.0 70.3 %copy-start = (bf16[1,128,2048]{2,1,0:T(8,128)(2,1)S(1)}, bf16[1,128,2048]{2,1,0:T(8,128)(2,1)}, u32[]{:S(2)}) copy-start(bf16[1,128,2048]{2,1,0:T(8,128)(2,1)} %param.14) | copy-start | bytes 1572868
  79.3 1.7 copy-start.14
  79.3 1.7 copy-start.15
  164.3 1.7 copy-start.3
  166.0 1.0 copy-start.2
  168.0 91.1 %copy-start.13 = (f32[2048]{0:T(1024)S(1)}, f32[2048]{0:T(1024)}, u32[]{:S(2)}) copy-start(f32[2048]{0:T(1024)} %param.23) | copy-start | bytes 24580
  259.1 1.6 copy-start.1
  442.4 3.1 copy-start.4
  445.5 1.0 copy-start.12
  445.5 1.8 copy-start.11
  445.5 2.6 copy-start.10
  446.5 2.6 copy-start.9
  448.1 1.9 copy-start.8
  449.1 1.9 copy-start.7
  450.0 1.9 copy-start.6
  451.0 1.9 copy-start.5

commit v4 on v3

--- a/solution.py
+++ b/solution.py
@@ -15,7 +15,7 @@
 MESH = pl.DeviceIdType.MESH
 BF = jnp.bfloat16
 F32 = jnp.float32
-VMEM_LIMIT = 60 * 1024 * 1024
+VMEM_LIMIT = 61 * 1024 * 1024
 
 
 def remote(src, dst, ssem, rsem, slot, dev):
@@ -81,15 +81,16 @@
         for copy in self.first:
             copy.start()
 
+    def relays(self):
+        for copy, onward in zip(self.first, self.relay):
+            copy.wait_recv()
+            onward.start()
+
     def arrive(self, i):
         if self.n == 4:
 
             @pl.when(i == 1)
             def _():
-                self.first[0].wait_recv()
-                self.relay[0].start()
-                self.first[1].wait_recv()
-                self.relay[1].start()
                 self.first[2].wait_recv()
 
             @pl.when(i == 2)
@@ -124,13 +125,28 @@
             self.peers = [dx, dy]
             half = parts.shape[-1] // 2
             self.cols = a, b = pl.ds(0, half), pl.ds(half, half)
-            self.far_a = remote(parts.at[pd, :, a], near.at[0, 1], ssem, rsem, 0, dx)
-            self.far_b = remote(parts.at[pd, :, b], near.at[1, 1], ssem, rsem, 1, dy)
+            rows = parts.shape[1] // 2
+            self.halves = (pl.ds(0, rows), pl.ds(rows, rows))
+            self.far_a = [
+                remote(parts.at[pd, r, a], near.at[0, 1, r], ssem, rsem, i, dx)
+                for i, r in enumerate(self.halves)
+            ]
+            self.far_b = [
+                remote(parts.at[pd, r, b], near.at[1, 1, r], ssem, rsem, 6 + i, dy)
+                for i, r in enumerate(self.halves)
+            ]
             self.near_a = remote(parts.at[self.px, :, a], near.at[0, 0], ssem, rsem, 2, dx)
             self.near_b = remote(parts.at[self.py, :, b], near.at[1, 0], ssem, rsem, 3, dy)
-            self.sum_a = remote(hold.at[0], far.at[0], ssem, rsem, 4, dy)
-            self.sum_b = remote(hold.at[1], far.at[1], ssem, rsem, 5, dx)
-            self.copies = [self.far_a, self.far_b, self.near_a, self.near_b, self.sum_a, self.sum_b]
+            self.sum_a = [
+                remote(hold.at[0, r], far.at[0, r], ssem, rsem, 4 + i, dy)
+                for i, r in enumerate(self.halves)
+            ]
+            self.sum_b = [
+                remote(hold.at[1, r], far.at[1, r], ssem, rsem, 8 + i, dx)
+                for i, r in enumerate(self.halves)
+            ]
+            self.copies = self.far_a + self.far_b + [self.near_a, self.near_b]
+            self.copies += self.sum_a + self.sum_b
         else:
             self.peers = [(s, (t + k) % n) for k in range(1, n)]
             self.copies = [
@@ -151,8 +167,9 @@
 
             @pl.when(i == 3)
             def _():
-                self.far_a.start()
-                self.far_b.start()
+                for copy_a, copy_b in zip(self.far_a, self.far_b):
+                    copy_a.start()
+                    copy_b.start()
 
         else:
             for k, copy in enumerate(self.copies):
@@ -163,17 +180,16 @@
 
     def relay(self):
         if self.n == 4:
-            a, b = self.cols
-            self.far_a.wait_recv()
-            self.hold[0] = (
-                self.parts[self.py, :, a].astype(F32) + self.near[0, 1].astype(F32)
-            ).astype(BF)
-            self.sum_a.start()
-            self.far_b.wait_recv()
-            self.hold[1] = (
-                self.parts[self.px, :, b].astype(F32) + self.near[1, 1].astype(F32)
-            ).astype(BF)
-            self.sum_b.start()
+            sides = (self.cols[0], self.py, self.far_a, self.sum_a), (
+                self.cols[1], self.px, self.far_b, self.sum_b
+            )
+            for i, r in enumerate(self.halves):
+                for side, (cols, who, came, onward) in enumerate(sides):
+                    came[i].wait_recv()
+                    self.hold[side, r] = (
+                        self.parts[who, r, cols].astype(F32) + self.near[side, 1, r].astype(F32)
+                    ).astype(BF)
+                    onward[i].start()
 
     def finish(self, write):
         if self.n == 4:
@@ -181,7 +197,8 @@
                 ((self.near_a, self.sum_a), (self.near_b, self.sum_b))
             ):
                 one.wait_recv()
-                two.wait_recv()
+                for copy in two:
+                    copy.wait_recv()
                 write(
                     self.cols[side],
                     self.parts[self.t, :, self.cols[side]].astype(F32)
@@ -244,6 +261,27 @@
     def onward(self, p):
         return remote(self.leave.at[p], self.enter.at[p], self.sems[2], self.sems[3], p, self.ahead)
 
+    def piece(self, gather, index):
+        return gather.source(index // self.heads) * self.heads + index % self.heads
+
+    def open(self, gather, i):
+        @pl.when(self.place == 0)
+        def _():
+            @pl.loop(0, self.heads)
+            def _(h):
+                self.step(self.piece(gather, i * self.heads + h))
+
+    def tick(self, gather, now):
+        total = self.local.shape[0]
+        ends = self.place == self.chips - 1
+        lag = jnp.minimum(3 * (self.place - 1), total - self.heads)
+        index = jnp.where(ends, (self.heads + now) % total, now - lag)
+        due = (self.place > 0) & (index >= 0) & (index < total)
+
+        @pl.when(due & (jnp.logical_not(ends) | (now >= total)))
+        def _():
+            self.step(self.piece(gather, jnp.maximum(index, 0)))
+
     def begin(self, p):
         @pl.when(self.first)
         def _():
@@ -338,6 +376,7 @@
         self.swap = swap
         self.tokens = self.ys.shape[1] // 2
         self.cut = self.xs.shape[3]
+        self.spans = [self.places(parts) for parts in wide], [self.places(parts) for parts in deep]
         span = 2 * chips
         self.partner = (s + 1 - 2 * self.core, t)
         self.above = ((s + 2) % span, t)
@@ -347,33 +386,57 @@
     def cols(self, j, core):
         return pl.ds(pl.multiple_of((2 * j + core) * self.cut, self.cut), self.cut)
 
+    def places(self, parts):
+        found, start = [], 0
+        for part in parts:
+            found.append((start, part.shape[0]))
+            start += part.shape[0]
+        assert start == self.tokens
+        return found
+
     def wide_own(self, kind, j):
-        return pltpu.make_async_copy(
-            self.wide[kind].at[:, self.cols(j, self.core)],
-            self.xs.at[kind, j, pl.ds(0, self.tokens)],
-            self.xsem.at[kind, j],
-        )
+        return [
+            pltpu.make_async_copy(
+                part.at[:, self.cols(j, self.core)],
+                self.xs.at[kind, j, pl.ds(start, size)],
+                self.xsem.at[kind, j, i],
+            )
+            for i, (part, (start, size)) in enumerate(zip(self.wide[kind], self.spans[0][kind]))
+        ]
 
     def wide_give(self, kind, j):
-        return pltpu.make_async_remote_copy(
-            src_ref=self.wide[kind].at[:, self.cols(j, 1 - self.core)],
-            dst_ref=self.xs.at[kind, j, pl.ds(self.tokens, self.tokens)],
-            send_sem=self.psx.at[kind, j],
-            recv_sem=self.prx.at[kind, j],
-            device_id=self.partner,
-            device_id_type=MESH,
-        )
+        return [
+            remote(
+                part.at[:, self.cols(j, 1 - self.core)],
+                self.xs.at[kind, j, pl.ds(self.tokens + start, size)],
+                self.psx.at[kind, j],
+                self.prx.at[kind, j],
+                i,
+                self.partner,
+            )
+            for i, (part, (start, size)) in enumerate(zip(self.wide[kind], self.spans[0][kind]))
+        ]
 
     def deep_own(self, u):
-        return pltpu.make_async_copy(
-            self.deep[u], self.ys.at[u, pl.ds(0, self.tokens)], self.ysem.at[u]
-        )
+        return [
+            pltpu.make_async_copy(
+                part, self.ys.at[u, pl.ds(start, size)], self.ysem.at[u, i]
+            )
+            for i, (part, (start, size)) in enumerate(zip(self.deep[u], self.spans[1][u]))
+        ]
 
     def deep_give(self, u):
-        return remote(
-            self.deep[u], self.ys.at[u, pl.ds(self.tokens, self.tokens)], self.psy, self.pry, u,
-            self.partner,
-        )
+        return [
+            remote(
+                part,
+                self.ys.at[u, pl.ds(self.tokens + start, size)],
+                self.psy.at[u],
+                self.pry.at[u],
+                i,
+                self.partner,
+            )
+            for i, (part, (start, size)) in enumerate(zip(self.deep[u], self.spans[1][u]))
+        ]
 
     def adds(self):
         return (self.chip >= self.lo) & (self.chip <= self.hi)
@@ -383,20 +446,23 @@
         def _():
             if self.kinds[u] not in self.kinds[:u]:
                 for j in range(self.chips):
-                    self.wide_give(self.kinds[u], j).start()
-                    self.wide_own(self.kinds[u], j).start()
-            self.deep_give(u).start()
-            self.deep_own(u).start()
+                    for copy in self.wide_give(self.kinds[u], j) + self.wide_own(self.kinds[u], j):
+                        copy.start()
+            for copy in self.deep_give(u) + self.deep_own(u):
+                copy.start()
 
     def ready(self, u):
         @pl.when(self.adds())
         def _():
-            self.deep_own(u).wait()
-            self.deep_give(u).wait_recv()
+            own, given = self.deep_own(u), self.deep_give(u)
             if self.kinds[u] not in self.kinds[:u]:
                 for j in range(self.chips):
-                    self.wide_own(self.kinds[u], j).wait()
-                    self.wide_give(self.kinds[u], j).wait_recv()
+                    own += self.wide_own(self.kinds[u], j)
+                    given += self.wide_give(self.kinds[u], j)
+            for copy in own:
+                copy.wait()
+            for copy in given:
+                copy.wait_recv()
 
     def up(self, u, j):
         return remote(
@@ -497,10 +563,12 @@
                         self.down(u, j).wait_send()
 
             for u in range(self.units):
-                self.deep_give(u).wait_send()
+                for copy in self.deep_give(u):
+                    copy.wait_send()
             for kind in range(max(self.kinds) + 1):
                 for j in range(self.chips):
-                    self.wide_give(kind, j).wait_send()
+                    for copy in self.wide_give(kind, j):
+                        copy.wait_send()
 
 
 def line_scratch(chips, units, kinds, tokens, cut, width, swap=False):
@@ -511,12 +579,12 @@
         pltpu.VMEM((units, 2 * tokens, width), BF),
         pltpu.VMEM((units, chips + 1) + block, BF),
         pltpu.VMEM((units,) + block, F32),
-        dma((kinds, chips)),
-        dma((units,)),
-        dma((kinds, chips)),
-        dma((kinds, chips)),
-        dma((units,)),
-        dma((units,)),
+        dma((kinds, chips, 2)),
+        dma((units, 2)),
+        dma((kinds, chips, 2)),
+        dma((kinds, chips, 2)),
+        dma((units, 2)),
+        dma((units, 2)),
         dma((units, chips + 1)),
         dma((units, chips + 1)),
     ]
@@ -525,18 +593,21 @@
 def mixer_kernel(n, chips, heads, *refs):
     (
         fac, x, og, wk_h, wv_h, wq_h, ws_h, wo_h, decay, qfac, kfac, cos, sin,
-        x_all, og_all, q, k, v, sp, mx, prior, gated, attn,
-        wk, wv, wq, ws, wo, acc, parts, local,
-    ) = refs[:31]
-    near, far, hold = refs[31:34]
-    chain_refs = refs[34:42]
-    wsem, gs, gr, os, orr, ss, sr, og_near, es, er, ns, nr = refs[42:]
+        x_o, og_o, q_o, k_o, v_o, sp_o, mx_o, prior_o, gated_o, attn,
+        x_all, og_all, q, k, v, sp, mx, prior, gated, wk, wv, wq, ws, wo, acc, parts, local,
+    ) = refs[:40]
+    near, far, hold = refs[40:43]
+    chain_refs = refs[43:51]
+    wsem, gs, gr, os, orr, ss, sr, es, er, osem, bsem = refs[51:]
     rows = x.shape[0]
     gather = Gather(n, x, x_all, gs, gr)
     gather_og = Gather(n, og, og_all, os, orr)
     ends = Ends(chips)
-    gather_near = Gather(n, og_near, og_all, ns, nr, n)
-    hand = remote(og, og_near, es, er, 0, ends.mate)
+    hand_own = remote(og, og_o.at[n], es, er, 0, ends.mate)
+
+    def hand(i):
+        return remote(og_all.at[gather.source(i)], og_o.at[n + i], es, er, i, ends.mate)
+
     scatter = Scatter(n, parts, near, far, hold, ss, sr)
     chain = Chain(chips, heads, False, fac, local, prior, *chain_refs)
     loads = [
@@ -547,16 +618,15 @@
         load.start()
     greet(gather.peers + chain.peers)
     gather.start()
-    gather_og.start()
 
     @pl.when(ends.gives)
     def _():
-        hand.start()
+        hand_own.start()
 
     me = gather.source(0)
     x_all[me] = x[...]
     og_all[me] = og[...]
-    for load in loads[:4]:
+    for load in loads[:2]:
         load.wait()
 
     @pl.loop(0, n)
@@ -565,6 +635,7 @@
         gather.arrive(i)
         at = pl.ds(pl.multiple_of(j * rows, rows), rows)
         acc[:, : heads * DK] = dot(x_all[j], wk[...])
+
         v[at] = dot(x_all[j], wv[...]).astype(BF)
         for h in range(heads):
             vc = slice(h * DV, (h + 1) * DV)
@@ -575,19 +646,53 @@
             p = j * heads + h
             local[p] = dot(key_dec, v[at, vc], 0, 0).astype(BF)
             chain.begin(p)
+
+        chain.open(gather, i)
+
+        @pl.when(i == 0)
+        def _():
+            gather.relays()
+            gather_og.start()
+
+    puts = [
+        pltpu.make_async_copy(a, b, osem.at[i])
+        for i, (a, b) in enumerate(
+            ((x_all, x_o), (k, k_o), (v, v_o), (q, q_o), (sp, sp_o), (og_all, og_o.at[pl.ds(0, n)]))
+        )
+    ]
+    for put in puts[:3]:
+        put.start()
+    for load in loads[2:]:
+        load.wait()
+
+    @pl.loop(0, n)
+    def _(i):
+        j = gather.source(i)
+        at = pl.ds(pl.multiple_of(j * rows, rows), rows)
         acc[:, : heads * DK] = dot(x_all[j], wq[...])
         for h in range(heads):
             kc = slice(h * DK, (h + 1) * DK)
-            q[at, kc] = turn(acc[:, kc], cos[...], sin[...]).astype(BF)
-        sp[at] = dot(x_all[j], ws[...])
-
-    loads[4].wait()
-
-    @pl.when(ends.takes)
-    def _():
-        hand.wait_recv()
-        gather_near.start()
-        og_all[n + me] = og_near[...]
+            vc = slice(h * DV, (h + 1) * DV)
+            query = turn(acc[:, kc], cos[...], sin[...]).astype(BF)
+            q[at, kc] = query
+            scores = (dot(query, k[at, kc], 1, 1) * decay[h]).astype(BF)
+            mx[at, vc] = dot(scores, v[at, vc])
+            sp[at, vc] = dot(x_all[j], ws[:, vc])
+            chain.tick(gather, i * heads + h)
+
+    for put in puts[3:5]:
+        put.start()
+    gather_og.relays()
+
+    def blocks(j):
+        at = pl.ds(pl.multiple_of(j * rows, rows), rows)
+        of = pl.ds(j * heads, heads)
+        return [
+            pltpu.make_async_copy(mx.at[at], mx_o.at[at], bsem.at[0, j]),
+            pltpu.make_async_copy(gated.at[at], gated_o.at[at], bsem.at[1, j]),
+            pltpu.make_async_copy(prior.at[of], prior_o.at[of], bsem.at[2, j]),
+        ]
+
 
     @pl.loop(0, n)
     def _(step):
@@ -595,26 +700,26 @@
         j = gather.source(i)
         gather_og.arrive(i)
 
-        @pl.when(ends.takes & (step > 0))
-        def _():
-            gather_near.arrive(step)
+        @pl.when(ends.gives & (i > 0) & (i < n - 1))
+        def _():
+            hand(i).start()
 
         at = pl.ds(pl.multiple_of(j * rows, rows), rows)
         for h in range(heads):
             vc = slice(h * DV, (h + 1) * DV)
             kc = slice(h * DK, (h + 1) * DK)
             p = j * heads + h
-            query = q[at, kc]
-            scores = (dot(query, k[at, kc], 1, 1) * decay[h]).astype(BF)
-            mx[at, vc] = dot(scores, v[at, vc])
-            query_dec = (query.astype(F32) * qfac[h]).astype(BF)
-            chain.step(p)
+            chain.tick(gather, (n + step) * heads + h)
+            query_dec = (q[at, kc].astype(F32) * qfac[h]).astype(BF)
             mx[at, vc] += dot(query_dec, prior[p])
             pre = sp[at, vc]
             gated[at, vc] = (pre * jax.nn.sigmoid(pre) * norm_of(mx[at, vc])[0]).astype(BF)
         parts[j] = dot(gated[at], wo[...]).astype(BF)
         scatter.send(i)
-
+        for put in blocks(j):
+            put.start()
+
+    puts[5].start()
     scatter.relay()
 
     def write(cols, total):
@@ -623,14 +728,27 @@
     scatter.finish(write)
     gather.drain()
     gather_og.drain()
+    for put in puts:
+        put.wait()
+
+    @pl.loop(0, n)
+    def _(j):
+        for put in blocks(j):
+            put.wait()
 
     @pl.when(ends.gives)
     def _():
-        hand.wait_send()
+        hand_own.wait_send()
+
+        @pl.loop(1, n - 1)
+        def _(i):
+            hand(i).wait_send()
 
     @pl.when(ends.takes)
     def _():
-        gather_near.drain()
+        @pl.loop(0, n - 1)
+        def _(i):
+            hand(i).wait_recv()
 
     scatter.drain()
 
@@ -647,7 +765,7 @@
     pieces = n * heads
     total = n * rows
     dma = pltpu.SemaphoreType.DMA
-    sems = max(6, n - 1)
+    sems = max(10, n - 1)
     vmem = pl.BlockSpec(memory_space=pltpu.VMEM)
     hbm = pl.BlockSpec(memory_space=pl.ANY)
     shape = jax.ShapeDtypeStruct
@@ -655,7 +773,7 @@
         functools.partial(mixer_kernel, n, chips, heads),
         out_shape=(
             shape((n, rows, model), BF),
-            shape((2 * n, rows, model), BF),
+            shape((2 * n - 1, rows, model), BF),
             shape((total, heads * DK), BF),
             shape((total, heads * DK), BF),
             shape((total, heads * DV), BF),
@@ -666,8 +784,19 @@
             shape((rows, model), F32),
         ),
         in_specs=[pl.BlockSpec(memory_space=pltpu.SMEM), vmem, vmem] + [hbm] * 5 + [vmem] * 5,
-        out_specs=(vmem,) * 10,
-        scratch_shapes=[pltpu.VMEM(w.shape, BF) for w in (wk, wv, wq, ws, wo)]
+        out_specs=(hbm,) * 9 + (vmem,),
+        scratch_shapes=[
+            pltpu.VMEM((n, rows, model), BF),
+            pltpu.VMEM((n, rows, model), BF),
+            pltpu.VMEM((total, heads * DK), BF),
+            pltpu.VMEM((total, heads * DK), BF),
+            pltpu.VMEM((total, heads * DV), BF),
+            pltpu.VMEM((total, heads * DV), F32),
+            pltpu.VMEM((total, heads * DV), F32),
+            pltpu.VMEM((pieces, DK, DV), BF),
+            pltpu.VMEM((total, heads * DV), BF),
+        ]
+        + [pltpu.VMEM(w.shape, BF) for w in (wk, wv, wq, ws, wo)]
         + [
             pltpu.VMEM((rows, heads * DK), F32),
             pltpu.VMEM((n, rows, model), BF),
@@ -677,7 +806,7 @@
         + chain_scratch(pieces)
         + [dma((5,))]
         + [dma((sems,))] * 6
-        + [pltpu.VMEM((rows, model), BF), dma((1,)), dma((1,)), dma((sems,)), dma((sems,))],
+        + [dma((n - 1,)), dma((n - 1,)), dma((6,)), dma((3, n))],
         compiler_params=params(cid),
         name="mixer",
     )(fac, x, og, wk, wv, wq, ws, wo, decay, qfac, kfac, cos, sin)
@@ -687,12 +816,20 @@
 GELU_A = 0.044715
 
 
+def gelu_of(g):
+    square = g * g
+    th = jnp.tanh(GELU_C * (g + GELU_A * (square * g)))
+    half = 0.5 * (1.0 + th)
+    slope = half + 0.5 * g * (1.0 - th * th) * (GELU_C * (1.0 + 3.0 * GELU_A * square))
+    return g * half, slope
+
+
 def mlp_kernel(n, chips, *refs):
     (
-        x, og_all, wg_h, wu_h, wd_h,
-        x_all, hidden, gate_low, upper_low, mlp_parts, grad_two,
-        wg, wu, wd, hg, acc_g, acc_u, acc, parts, near, far, hold,
-        wsem, gs, gr, ss, sr, es, er,
+        x, og_h, wg_h, wu_h, wd_h,
+        x_o, hidden_o, gate_o, upper_o, mlp_o, grad_two, gate_late, up_late,
+        og_all, x_all, hidden, gate_low, upper_low, mlp_parts, wg, wu, wd, hg, acc_g, acc_u, acc, parts, near, far, hold,
+        wsem, gs, gr, ss, sr, es, er, osem, bsem,
     ) = refs
     rows = x.shape[0]
     gather = Gather(n, x, x_all, gs, gr)
@@ -702,69 +839,117 @@
         pltpu.make_async_copy(a, w, wsem.at[i])
         for i, (a, w) in enumerate(((wd_h, wd), (wg_h, wg), (wu_h, wu)))
     ]
-    for load in loads:
+    loads.append(pltpu.make_async_copy(og_h, og_all, wsem.at[3]))
+    for load in [loads[0], loads[3], loads[1], loads[2]]:
         load.start()
     greet(gather.peers + ends.peers)
     gather.start()
     me = gather.source(0)
+
+    def hand(i):
+        j = gather.source(i)
+        return remote(x_all.at[j], x_all.at[n + i], es, er, i, ends.mate)
+
+    first = remote(x, x_all.at[n], es, er, 0, ends.mate)
+
+    @pl.when(ends.gives)
+    def _():
+        first.start()
+
     x_all[me] = x[...]
     loads[0].wait()
-
-    def hand(i):
-        j = gather.source(i)
-        return remote(x_all.at[j], x_all.at[n + j], es, er, i, ends.mate)
-
-    @pl.loop(0, n)
-    def _(j):
-        at = pl.ds(pl.multiple_of(j * rows, rows), rows)
-        hg[at] = dot(og_all[j], wd[...], 1, 1)
-
+    loads[3].wait()
+    pair = 2 * rows
+
+    @pl.loop(0, n // 2)
+    def _(c):
+        two = pl.ds(pl.multiple_of(2 * c, 2), 2)
+        at = pl.ds(pl.multiple_of(c * pair, pair), pair)
+        hg[at] = dot(og_all[two].reshape(pair, x.shape[1]), wd[...], 1, 1)
+
+    gather.relays()
     loads[1].wait()
     loads[2].wait()
     slab = 16
 
-    def units(block, back_at):
+    def units(block, back_at, extra):
         start = pl.multiple_of(block * rows, rows)
         acc_g[...] = dot(x_all[block], wg[...])
         acc_u[...] = dot(x_all[block], wu[...])
+        if extra:
+            gate_late[...] = acc_g[...]
+            up_late[...] = acc_u[...]
 
         @pl.loop(0, rows // slab)
         def _(r):
             here = pl.ds(pl.multiple_of(r * slab, slab), slab)
             there = pl.ds(pl.multiple_of(start + r * slab, slab), slab)
             g, u = acc_g[here], acc_u[here]
+            gelu, slope = gelu_of(g)
+            hidden[there] = (gelu * u).astype(BF)
             back = hg[pl.ds(pl.multiple_of(back_at + r * slab, slab), slab)]
-            square = g * g
-            th = jnp.tanh(GELU_C * (g + GELU_A * (square * g)))
-            half = 0.5 * (1.0 + th)
-            gelu = g * half
-            slope = half + 0.5 * g * (1.0 - th * th) * (GELU_C * (1.0 + 3.0 * GELU_A * square))
-            hidden[there] = (gelu * u).astype(BF)
             gate_low[there] = (back * u * slope).astype(BF)
             upper_low[there] = (back * gelu).astype(BF)
 
     @pl.loop(0, n)
-    def _(i):
+    def _(turn):
+        i = jnp.where(turn == 2, 3, jnp.where(turn == 3, 2, turn)) if n == 4 else turn
         j = gather.source(i)
         gather.arrive(i)
 
-        @pl.when(ends.gives)
+        @pl.when(ends.gives & (i > 0))
         def _():
             hand(i).start()
 
-        units(j, j * rows)
+        units(j, j * rows, False)
         at = pl.ds(pl.multiple_of(j * rows, rows), rows)
         acc[...] = dot(gate_low[at], wg[...], 1, 1)
         parts[j] = (acc[...] + dot(upper_low[at], wu[...], 1, 1)).astype(BF)
         scatter.send(i)
 
+    whole = pl.ds(0, n * rows)
+    puts = [
+        pltpu.make_async_copy(a, b, osem.at[i])
+        for i, (a, b) in enumerate(
+            (
+                (x_all.at[pl.ds(0, n)], x_o.at[pl.ds(0, n)]),
+                (hidden.at[whole], hidden_o.at[whole]),
+                (gate_low.at[whole], gate_o.at[whole]),
+                (upper_low.at[whole], upper_o.at[whole]),
+                (mlp_parts, mlp_o),
+            )
+        )
+    ]
+    for put in puts[:4]:
+        put.start()
+
+    def blocks(i):
+        at = pl.ds(pl.multiple_of((n + i) * rows, rows), rows)
+        return [
+            pltpu.make_async_copy(x_all.at[n + i], x_o.at[n + i], bsem.at[0, i]),
+            pltpu.make_async_copy(hidden.at[at], hidden_o.at[at], bsem.at[1, i]),
+        ]
+
+    def late_blocks(i):
+        at = pl.ds(pl.multiple_of((n + i) * rows, rows), rows)
+        return [
+            pltpu.make_async_copy(gate_low.at[at], gate_o.at[at], bsem.at[2, i]),
+            pltpu.make_async_copy(upper_low.at[at], upper_o.at[at], bsem.at[3, i]),
+        ]
+
     def extra(i):
         @pl.when(ends.takes)
         def _():
-            j = gather.source(i)
-            hg[pl.ds(0, rows)] = dot(og_all[n + j], wd[...], 1, 1)
+            hg[pl.ds(0, rows)] = dot(og_all[n + jnp.minimum(i, n - 2)], wd[...], 1, 1)
             hand(i).wait_recv()
-            units(n + j, 0)
+            units(n + i, 0, True)
+            for put in blocks(i):
+                put.start()
+
+            @pl.when(i < n - 1)
+            def _():
+                for put in late_blocks(i):
+                    put.start()
 
     @pl.loop(0, n // 2)
     def _(i):
@@ -772,10 +957,13 @@
 
     scatter.relay()
 
-    @pl.loop(0, n)
-    def _(j):
-        at = pl.ds(pl.multiple_of(j * rows, rows), rows)
-        mlp_parts[j] = dot(hidden[at], wd[...]).astype(BF)
+    @pl.loop(0, n // 2)
+    def _(c):
+        two = pl.ds(pl.multiple_of(2 * c, 2), 2)
+        at = pl.ds(pl.multiple_of(c * pair, pair), pair)
+        mlp_parts[two] = dot(hidden[at], wd[...]).astype(BF).reshape(2, rows, x.shape[1])
+
+    puts[4].start()
 
     def write(cols, total):
         grad_two[:, cols] = total
@@ -786,12 +974,29 @@
     def _(i):
         extra(i)
 
+    @pl.when(ends.takes)
+    def _():
+        @pl.loop(0, n)
+        def _(i):
+            for put in blocks(i):
+                put.wait()
+
+        @pl.loop(0, n - 1)
+        def _(i):
+            for put in late_blocks(i):
+                put.wait()
+
+    for put in puts:
+        put.wait()
+
     gather.drain()
     scatter.drain()
 
     @pl.when(ends.gives)
     def _():
-        @pl.loop(0, n)
+        first.wait_send()
+
+        @pl.loop(1, n)
         def _(i):
             hand(i).wait_send()
 
@@ -803,7 +1008,7 @@
     width = wg.shape[1]
     total = n * rows
     dma = pltpu.SemaphoreType.DMA
-    sems = max(6, n - 1)
+    sems = max(10, n - 1)
     vmem = pl.BlockSpec(memory_space=pltpu.VMEM)
     hbm = pl.BlockSpec(memory_space=pl.ANY)
     shape = jax.ShapeDtypeStruct
@@ -812,14 +1017,24 @@
         out_shape=(
             shape((2 * n, rows, model), BF),
             shape((2 * total, width), BF),
-            shape((2 * total, width), BF),
-            shape((2 * total, width), BF),
+            shape((2 * total - rows, width), BF),
+            shape((2 * total - rows, width), BF),
             shape((n, rows, model), BF),
             shape((rows, model), F32),
+            shape((rows, width), F32),
+            shape((rows, width), F32),
         ),
-        in_specs=[vmem, vmem] + [hbm] * 3,
-        out_specs=(vmem,) * 6,
-        scratch_shapes=[pltpu.VMEM(w.shape, BF) for w in (wg, wu, wd)]
+        in_specs=[vmem] + [hbm] * 4,
+        out_specs=(hbm,) * 5 + (vmem,) * 3,
+        scratch_shapes=[
+            pltpu.VMEM(og_all.shape, BF),
+            pltpu.VMEM((2 * n, rows, model), BF),
+            pltpu.VMEM((2 * total, width), BF),
+            pltpu.VMEM((2 * total, width), BF),
+            pltpu.VMEM((2 * total, width), BF),
+            pltpu.VMEM((n, rows, model), BF),
+        ]
+        + [pltpu.VMEM(w.shape, BF) for w in (wg, wu, wd)]
         + [
             pltpu.VMEM((total, width), F32),
             pltpu.VMEM((rows, width), F32),
@@ -828,9 +1043,9 @@
             pltpu.VMEM((n, rows, model), BF),
         ]
         + scatter_scratch(n, rows, model)
-        + [dma((3,))]
+        + [dma((4,))]
         + [dma((sems,))] * 4
-        + [dma((n,)), dma((n,))],
+        + [dma((n,)), dma((n,)), dma((5,)), dma((4, n))],
         compiler_params=params(cid),
         name="mlp",
     )(x, og_all, wg, wu, wd)
@@ -838,23 +1053,42 @@
 
 def mixer_back_kernel(n, chips, heads, *refs):
     (
-        fac, res, wo_h, wq_h, wk_h, wv_h, ws_h, q, k, v, sp, mx, prior, mlp_parts, decay, qfac, kfac, cos, sin,
-        res_all, swish_low, value_low, qk_low, grad_one, mlp_out,
-        wo, wq, wk, wv, ws, mixed_low, acc, parts, local, later,
-    ) = refs[:35]
-    near, far, hold, mlp_near, mlp_far, mlp_hold = refs[35:41]
-    chain_refs = refs[41:49]
-    wsem, gs, gr, ss, sr, ms, mr = refs[49:]
+        fac, res, wo_h, wq_h, wk_h, wv_h, ws_h, q_h, k_h, v_h, sp_h, mx_h, prior_h, mlp_h, decay, qfac, kfac, cos, sin, og_h, wd_h, gate_late, up_late,
+        res_o, swish_o, value_o, qk_o, grad_one, mlp_out, og_late, gate_low, upper_low,
+        q, k, v, sp, mx, prior, mlp_parts, res_all, swish_low, value_low, qk_low, wo, wq, wk, wv, ws, mixed_low, sums, parts, local, later, key_part, value_part,
+    ) = refs[:55]
+    near, far, hold, mlp_near, mlp_far, mlp_hold = refs[55:61]
+    chain_refs = refs[61:69]
+    wsem, gs, gr, ss, sr, ms, mr, es, er, isem, lsem, osem, bsem = refs[69:]
     rows = res.shape[0]
     gather = Gather(n, res, res_all, gs, gr)
     scatter = Scatter(n, parts, near, far, hold, ss, sr)
     scatter_mlp = Scatter(n, mlp_parts, mlp_near, mlp_far, mlp_hold, ms, mr)
     chain = Chain(chips, heads, True, fac, local, later, *chain_refs)
+    ends = Ends(chips)
+    late = remote(og_h.at[gather.source(n - 1)], og_late, es, er, 0, ends.mate)
+    load_late = pltpu.make_async_copy(wd_h, wo, wsem.at[5])
     loads = [
         pltpu.make_async_copy(a, w, wsem.at[i])
         for i, (a, w) in enumerate(((wo_h, wo), (ws_h, ws), (wq_h, wq), (wk_h, wk), (wv_h, wv)))
     ]
-    for load in loads:
+    def entering(i):
+        j = gather.source(i)
+        at = pl.ds(pl.multiple_of(j * rows, rows), rows)
+        return [
+            pltpu.make_async_copy(a.at[at], b.at[at], isem.at[w, j])
+            for w, (a, b) in enumerate(((mx_h, mx), (sp_h, sp), (q_h, q)))
+        ]
+
+    loads += [
+        pltpu.make_async_copy(a, b, lsem.at[i])
+        for i, (a, b) in enumerate(((k_h, k), (v_h, v), (prior_h, prior), (mlp_h, mlp_parts)))
+    ]
+    loads[0].start()
+    for i in range(n):
+        for load in entering(i):
+            load.start()
+    for load in loads[1:]:
         load.start()
     greet(gather.peers + chain.peers)
     gather.start()
@@ -867,11 +1101,14 @@
         j = gather.source(i)
         gather.arrive(i)
         at = pl.ds(pl.multiple_of(j * rows, rows), rows)
-        acc[:, : heads * DV] = dot(res_all[j], wo[...], 1, 1)
+        for load in entering(i):
+            load.wait()
+        sums[j, :, : heads * DV] = dot(res_all[j], wo[...], 1, 1).astype(sums.dtype)
+
         for h in range(heads):
             vc = slice(h * DV, (h + 1) * DV)
             kc = slice(h * DK, (h + 1) * DK)
-            back = acc[:, vc]
+            back = sums[j, :, vc].astype(F32)
             normed, inv = norm_of(mx[at, vc])
             pre = sp[at, vc]
             sig = jax.nn.sigmoid(pre)
@@ -889,10 +1126,58 @@
             local[p] = dot(query_dec, g, 0, 0).astype(BF)
             chain.begin(p)
 
+        chain.open(gather, i)
+
+        @pl.when(i == 0)
+        def _():
+            gather.relays()
+
+    puts = [
+        pltpu.make_async_copy(res_all, res_o, osem.at[0]),
+        pltpu.make_async_copy(swish_low, swish_o, osem.at[1]),
+    ]
+    for put in puts:
+        put.start()
+
+    def leaving(j):
+        at = pl.ds(pl.multiple_of(j * rows, rows), rows)
+        return [
+            pltpu.make_async_copy(value_low.at[at], value_o.at[at], bsem.at[0, j]),
+            pltpu.make_async_copy(qk_low.at[at], qk_o.at[at], bsem.at[1, j]),
+        ]
+
     for load in loads[1:]:
         load.wait()
     for i in range(1, n):
         scatter_mlp.send(i)
+
+    @pl.when(ends.gives)
+    def _():
+        late.start()
+
+    @pl.when(ends.takes)
+    def _():
+        load_late.start()
+
+    @pl.loop(0, n)
+    def _(i):
+        j = gather.source(i)
+        at = pl.ds(pl.multiple_of(j * rows, rows), rows)
+        for h in range(heads):
+            vc = slice(h * DV, (h + 1) * DV)
+            kc = slice(h * DK, (h + 1) * DK)
+            g, query, key = mixed_low[at, vc], q[at, kc], k[at, kc]
+            chain.tick(gather, i * heads + h)
+            raw_low = (dot(g, v[at, vc], 1, 1) * decay[h]).astype(BF)
+            query_back = dot(raw_low, key) + dot(g, prior[j * heads + h], 1, 1) * qfac[h]
+            qk_low[at, kc] = turn_back(query_back, cos[...], sin[...]).astype(BF)
+            scores = (dot(query, key, 1, 1) * decay[h]).astype(BF)
+            key_part[at, kc] = dot(raw_low, query, 0, 0).astype(key_part.dtype)
+            value_part[at, vc] = dot(scores, g, 0, 0).astype(value_part.dtype)
+        sums[j] = dot(swish_low[at], ws[...], 1, 1).astype(sums.dtype)
+        sums[j] += dot(qk_low[at, : heads * DK], wq[...], 1, 1).astype(sums.dtype)
+
+    scatter_mlp.relay()
 
     @pl.loop(0, n)
     def _(step):
@@ -902,33 +1187,37 @@
         for h in range(heads):
             vc = slice(h * DV, (h + 1) * DV)
             kc = slice(h * DK, (h + 1) * DK)
-            p = j * heads + h
-            g, value, query, key = mixed_low[at, vc], v[at, vc], q[at, kc], k[at, kc]
-            raw_low = (dot(g, value, 1, 1) * decay[h]).astype(BF)
-            query_back = dot(raw_low, key) + dot(g, prior[p], 1, 1) * qfac[h]
-            qk_low[at, kc] = turn_back(query_back, cos[...], sin[...]).astype(BF)
-            scores = (dot(query, key, 1, 1) * decay[h]).astype(BF)
-            key_part = dot(raw_low, query, 0, 0)
-            value_part = dot(scores, g, 0, 0)
-            key_dec = (key.astype(F32) * kfac[h]).astype(BF)
-            chain.step(p)
-            after = later[p]
-            key_back = key_part + dot(value, after, 1, 1) * kfac[h]
+            chain.tick(gather, (n + step) * heads + h)
+            after = later[j * heads + h]
+            key_dec = (k[at, kc].astype(F32) * kfac[h]).astype(BF)
+            key_back = key_part[at, kc].astype(F32) + dot(v[at, vc], after, 1, 1) * kfac[h]
             qk_low[at, slice((heads + h) * DK, (heads + h + 1) * DK)] = turn_back(
                 key_back, cos[...], sin[...]
             ).astype(BF)
-            value_low[at, vc] = (value_part + dot(key_dec, after)).astype(BF)
-        acc[...] = dot(swish_low[at], ws[...], 1, 1)
-        acc[...] += dot(value_low[at], wv[...], 1, 1)
-        acc[...] += dot(qk_low[at, : heads * DK], wq[...], 1, 1)
-        parts[j] = (acc[...] + dot(qk_low[at, heads * DK :], wk[...], 1, 1)).astype(BF)
+            value_low[at, vc] = (value_part[at, vc] + dot(key_dec, after)).astype(BF)
+        sums[j] += dot(value_low[at], wv[...], 1, 1).astype(sums.dtype)
+        parts[j] = (sums[j].astype(F32) + dot(qk_low[at, heads * DK :], wk[...], 1, 1)).astype(BF)
         scatter.send(i)
-
-        @pl.when(step == n - 2)
-        def _():
-            scatter_mlp.relay()
+        for put in leaving(j):
+            put.start()
 
     scatter.relay()
+
+    @pl.when(ends.takes)
+    def _():
+        width = gate_late.shape[1]
+        load_late.wait()
+        late.wait_recv()
+        sums[0, :, :width] = dot(og_late[...], wo[...], 1, 1).astype(sums.dtype)
+        slab = 16
+
+        @pl.loop(0, rows // slab)
+        def _(r):
+            here = pl.ds(pl.multiple_of(r * slab, slab), slab)
+            gelu, slope = gelu_of(gate_late[here])
+            back = sums[0, here, :width].astype(F32)
+            gate_low[here] = (back * up_late[here] * slope).astype(BF)
+            upper_low[here] = (back * gelu).astype(BF)
 
     def write(cols, total):
         grad_one[:, cols] = total
@@ -943,20 +1232,33 @@
     scatter.drain()
     scatter_mlp.drain()
 
+    @pl.when(ends.gives)
+    def _():
+        late.wait_send()
+
+    for put in puts:
+        put.wait()
+
+    @pl.loop(0, n)
+    def _(j):
+        for put in leaving(j):
+            put.wait()
+
     @pl.loop(0, n * heads)
     def _(p):
         chain.drain(p)
 
 
-def mixer_back(fac, res, wo, wq, wk, wv, ws, q, k, v, sp, mx, prior, mlp_parts, decay, qfac, kfac, cos, sin, cid):
+def mixer_back(fac, res, wo, wq, wk, wv, ws, q, k, v, sp, mx, prior, mlp_parts, decay, qfac, kfac, cos, sin, og_all, wd, gate_late, up_late, cid):
     n = lax.axis_size("tp")
     chips = lax.axis_size("seq") // 2
     rows, model = res.shape
     heads = q.shape[1] // DK
     pieces = n * heads
     total = n * rows
+    keep = F32 if n <= 4 else BF
     dma = pltpu.SemaphoreType.DMA
-    sems = max(6, n - 1)
+    sems = max(10, n - 1)
     vmem = pl.BlockSpec(memory_space=pltpu.VMEM)
     hbm = pl.BlockSpec(memory_space=pl.ANY)
     shape = jax.ShapeDtypeStruct
@@ -969,40 +1271,55 @@
             shape((total, 2 * heads * DK), BF),
             shape((rows, model), F32),
             shape((rows, model), F32),
+            shape((rows, model), BF),
+            shape(gate_late.shape, BF),
+            shape(gate_late.shape, BF),
         ),
-        in_specs=[pl.BlockSpec(memory_space=pltpu.SMEM), vmem] + [hbm] * 5 + [vmem] * 12,
-        out_specs=(vmem,) * 6,
-        scratch_shapes=[pltpu.VMEM(w.shape, BF) for w in (wo, wq, wk, wv, ws)]
+        in_specs=[pl.BlockSpec(memory_space=pltpu.SMEM), vmem] + [hbm] * 12 + [vmem] * 5 + [hbm, hbm, vmem, vmem],
+        out_specs=(hbm,) * 4 + (vmem,) * 5,
+        scratch_shapes=[pltpu.VMEM(a.shape, a.dtype) for a in (q, k, v, sp, mx, prior, mlp_parts)]
+        + [
+            pltpu.VMEM((n, rows, model), BF),
+            pltpu.VMEM((total, heads * DV), BF),
+            pltpu.VMEM((total, heads * DV), BF),
+            pltpu.VMEM((total, 2 * heads * DK), BF),
+        ]
+        + [pltpu.VMEM(w.shape, BF) for w in (wo, wq, wk, wv, ws)]
         + [
             pltpu.VMEM((total, heads * DV), BF),
-            pltpu.VMEM((rows, model), F32),
+            pltpu.VMEM((n, rows, model), keep),
             pltpu.VMEM((n, rows, model), BF),
             pltpu.VMEM((pieces, DK, DV), BF),
             pltpu.VMEM((pieces, DK, DV), BF),
+            pltpu.VMEM((total, heads * DK), keep),
+            pltpu.VMEM((total, heads * DV), BF),
         ]
         + scatter_scratch(n, rows, model)
         + scatter_scratch(n, rows, model)
         + chain_scratch(pieces)
-        + [dma((5,))]
-        + [dma((sems,))] * 6,
+        + [dma((6,))]
+        + [dma((sems,))] * 6
+        + [dma((1,)), dma((1,)), dma((3, n)), dma((4,)), dma((2,)), dma((2, n))],
         compiler_params=params(cid),
         name="mixer_back",
-    )(fac, res, wo, wq, wk, wv, ws, q, k, v, sp, mx, prior, mlp_parts, decay, qfac, kfac, cos, sin)
+    )(fac, res, wo, wq, wk, wv, ws, q, k, v, sp, mx, prior, mlp_parts, decay, qfac, kfac, cos, sin, og_all, wd, gate_late, up_late)
 
 
 def weights_kernel(chips, *refs):
     (
-        two, og, hidden, gate_low, up_low, one, res, swish_low, gated, value_low, qk_low, vec,
+        two, og, og_late, hidden, gate_low, gate_late, up_low, up_late,
+        one, res, swish_low, gated, value_low, qk_low, vec,
         down_o, gate_o, up_o, swish_o, mixer_o, value_o, query_o, key_o, vec_out,
-    ) = refs[:21]
+    ) = refs[:24]
     mlp = LineSums(
-        chips, 1, chips - 2, (two, og), (gate_low, up_low, hidden), (0, 0, 1), refs[21:33]
+        chips, 1, chips - 2, ((two,), (og, og_late)),
+        ((gate_low, gate_late), (up_low, up_late), (hidden,)), (0, 0, 1), refs[24:36],
     )
     mix = LineSums(
-        chips, 0, chips - 1, (one, res), (swish_low, gated, value_low, qk_low), (0, 1, 0, 0),
-        refs[33:45],
+        chips, 0, chips - 1, ((one,), (res,)), ((swish_low,), (gated,), (value_low,), (qk_low,)),
+        (0, 1, 0, 0), refs[36:48],
     )
-    turned, osem, vec_near, vec_sum, vec_far, vs, vr, us, ur = refs[45:]
+    turned, osem, vec_near, vec_sum, vec_far, vs, vr, us, ur = refs[48:]
     s, t = lax.axis_index("seq"), lax.axis_index("tp")
     span, tp = 2 * chips, vec.shape[0]
     ring = [((s + d) % span, t) for d in range(1, span)]
@@ -1031,11 +1348,20 @@
             def _(w=w):
                 if w < mlp.units:
                     mlp.ready(w)
+
+        @pl.when(u < mlp.units)
+        def _():
+            mlp.step(u, 0)
+
+        for w in range(mix.units):
+
+            @pl.when(u == w)
+            def _(w=w):
                 mix.ready(w)
 
         @pl.loop(0, chips - 1)
         def _(k):
-            @pl.when(u < mlp.units)
+            @pl.when((u < mlp.units) & (k > 0))
             def _():
                 mlp.step(u, k)
 
@@ -1090,11 +1416,14 @@
             copy.wait()
 
 
-def weight_sums(two, og, hidden, gate_low, up_low, one, res, swish_low, gated, value_low, qk_low, vec, cid):
+def weight_sums(
+    two, og, og_late, hidden, gate_low, gate_late, up_low, up_late, one, res, swish_low, gated, value_low,
+    qk_low, vec, cid,
+):
     chips = lax.axis_size("seq") // 2
     tokens, model = one.shape
     width = gated.shape[1]
-    mlp_tokens, mlp_width = gate_low.shape
+    mlp_tokens, mlp_width = hidden.shape
     keys = qk_low.shape[1] // 2
     cut = model // (2 * chips)
     dma = pltpu.SemaphoreType.DMA
@@ -1115,7 +1444,7 @@
             shape(cut, keys),
             shape(*vec.shape[2:]),
         ),
-        in_specs=[hbm] * 11 + [vmem],
+        in_specs=[hbm] * 14 + [vmem],
         out_specs=(hbm,) * 8 + (vmem,),
         scratch_shapes=line_scratch(chips, 3, 2, mlp_tokens, cut, mlp_width)
         + line_scratch(chips, 4, 2, tokens, cut, width)
@@ -1132,7 +1461,7 @@
         ],
         compiler_params=params(cid),
         name="weights",
-    )(two, og, hidden, gate_low, up_low, one, res, swish_low, gated, value_low, qk_low, vec)
+    )(two, og, og_late, hidden, gate_low, gate_late, up_low, up_late, one, res, swish_low, gated, value_low, qk_low, vec)
 
 
 def layer_norm(values, gain, bias):
@@ -1185,17 +1514,17 @@
     )
     hidden_res = inputs_full + attn_out
     normed_two = layer_norm(hidden_res, mlp_gain, mlp_bias).astype(BF)
-    two_all, hidden, gate_low, upper_low, mlp_parts, normed_two_grad = mlp(
+    two_all, hidden, gate_low, upper_low, mlp_parts, normed_two_grad, gate_pre, up_pre = mlp(
         normed_two, grad_all, gate_weight, up_weight, down_weight, 1
     )
     flat = lambda a: a.reshape(-1, model)
     _, pull_two = jax.vjp(layer_norm, hidden_res, mlp_gain, mlp_bias)
     res_back, mlpgain_part, mlpbias_part = pull_two(normed_two_grad)
     res_grad = cotangent.astype(F32) + res_back
-    res_all, swish_low, value_low, qk_low, normed_one_grad, mlp_out = mixer_back(
+    res_all, swish_low, value_low, qk_low, normed_one_grad, mlp_out, og_late, gate_late, up_late = mixer_back(
         block_fac, res_grad.astype(BF), output_weight, query_weight, key_weight, value_weight, swish_weight,
         query, key, value, swish_pre, mixed, prior, mlp_parts, decay_mat, query_fac, key_fac,
-        cosine, sine, 2,
+        cosine, sine, grad_all, down_weight, gate_pre, up_pre, 2,
     )
     outputs = (hidden_res + mlp_out).astype(BF)
     _, pull_one = jax.vjp(layer_norm, inputs_full, attn_gain, attn_bias)
@@ -1209,7 +1538,7 @@
     vectors = jnp.pad(vectors, ((0, 0), (0, 0), (0, 1024 - 4 * each))).reshape(tps, seqs, 8, 128)
     down_grad, gate_grad, up_grad, swish_grad, mixer_grad, value_grad, query_grad, key_grad, vector_sums = (
         weight_sums(
-            flat(two_all), flat(grad_all), hidden, gate_low, upper_low, flat(one_all), flat(res_all), swish_low, gated,
+            flat(two_all), flat(grad_all), og_late, hidden, gate_low, gate_late, upper_low, up_late, flat(one_all), flat(res_all), swish_low, gated,
             value_low, qk_low, vectors, 3,
         )
     )

time: 454 us -> 417 us (0.919); the launches traced: 454 us -> 411 us
  Pallas kernels: 423 us -> 379 us
    pallas_call x1, Pallas kernels: 82.2 us -> 59.1 us  [mlp(): pl.pallas_call(functools.partial(mlp_kernel, n, chips), out_shape=(shape(...]
    pallas_call x1, Pallas kernels: 91.1 us -> 80.6 us  [mixer_back(): pl.pallas_call(functools.partial(mixer_back_kernel, n, chips, heads), out...]
    pallas_call x1, Pallas kernels: 70.3 us -> 62.6 us  [mixer(): pl.pallas_call(functools.partial(mixer_kernel, n, chips, heads), out_shap...]
where the time goes in v4:
time: 417 us; the launch traced here: 411 us
  Pallas kernels  379 us (91%)
  other arithmetic  18.9 us (5%)
  local copies, waits for them, and re-layouts  11.7 us (3%)
    pallas_call x1, Pallas kernels, weight_sums(): pl.pallas_call(functools.partial(weights_kernel, chips), out_shape=(shape...  177 us
    pallas_call x1, Pallas kernels, mixer_back(): pl.pallas_call(functools.partial(mixer_back_kernel, n, chips, heads), out...  80.6 us
    pallas_call x1, Pallas kernels, mixer(): pl.pallas_call(functools.partial(mixer_kernel, n, chips, heads), out_shap...  62.6 us
    pallas_call x1, Pallas kernels, mlp(): pl.pallas_call(functools.partial(mlp_kernel, n, chips), out_shape=(shape(...  59.1 us
    unnamed x42, local copies, waits for them, and re-layouts  8.86 us

profile of v4, /device:TPU:0, one launch (start us, length us, event | category | flops | bytes accessed | tf_op | source)
XLA Modules:
  0.0 410.8 jit_solution(17563306458736983626)
XLA Ops:
  0.6 1.2 convert_reduce_fusion
  1.8 1.3 fusion.11
  3.2 2.3 fusion.9.refs_1_
  5.4 0.5 exponential_subtract_fusion
  6.0 1.0 broadcast_power_fusion
  7.0 1.0 multiply_sine_fusion
  8.1 0.9 power_select_fusion.refs_8_.refs_14_
  9.0 62.6 %mixer.1 = (bf16[4,128,2048]{2,1,0:T(8,128)(2,1)}, bf16[7,128,2048]{2,1,0:T(8,128)(2,1)}, bf16[512,512]{1,0:T(8,128)(2,1)}, bf16[512,512]{1,0:T(8,128)(2,1)}, bf...) custom-call(f32[2]{0:T(128)} %get-tuple-element.105.refs_0_, ...), custom_call_target="tpu_custom_call" | custom-call | tf_op jit(solution)/shard_map/mixer/pallas_call | solution.py:772
  71.6 1.4 fusion.22
  73.3 1.0 add_convert_fusion.2.refs_0_
  74.4 59.1 %mlp.1 = (bf16[8,128,2048]{2,1,0:T(8,128)(2,1)}, bf16[1024,1024]{1,0:T(8,128)(2,1)}, bf16[896,1024]{1,0:T(8,128)(2,1)}, bf16[896,1024]{1,0:T(8,128)(2,1)}, bf16[...) custom-call(bf16[128,2048]{1,0:T(8,128)(2,1)} %add_convert_fusion.2.refs_0_, ...), custom_call_target="tpu_custom_call" | custom-call | tf_op jit(solution)/shard_map/mlp/pallas_call | solution.py:1015
  133.5 1.7 multiply_reduce_fusion
  135.2 0.4 fusion.21
  135.6 0.6 copy-done.2
  136.2 1.0 fusion.13.refs_1_
  137.2 80.6 %mixer_back.1 = (bf16[4,128,2048]{2,1,0:T(8,128)(2,1)}, bf16[512,1024]{1,0:T(8,128)(2,1)}, bf16[512,1024]{1,0:T(8,128)(2,1)}, bf16[512,1024]{1,0:T(8,128)(2,1)},...) custom-call(f32[2]{0:T(128)} %get-tuple-element.105.refs_0_, ...), custom_call_target="tpu_custom_call" | custom-call | tf_op jit(solution)/shard_map/mixer_back/pallas_call | solution.py:1265
  217.8 1.6 fusion.12
  219.5 0.6 fusion.10
  220.5 0.7 copy.31
  221.2 176.7 %weights.1 = (f32[1024,256]{1,0:T(8,128)}, f32[256,1024]{1,0:T(8,128)}, f32[256,1024]{1,0:T(8,128)}, f32[256,1024]{1,0:T(8,128)}, f32[1024,256]{1,0:T(8,128)}, /...) custom-call(bf16[1024,2048]{1,0:T(8,128)(2,1)} %bitcast.65, ...), custom_call_target="tpu_custom_call" | custom-call | tf_op jit(solution)/shard_map/weights/pallas_call | solution.py:1434
  397.9 0.7 slice.16
  398.7 0.5 slice_bitcast_fusion
  399.2 2.7 fusion.15
  401.9 0.9 fusion.14
  402.9 0.8 copy.40
  403.7 0.8 copy.41
  404.5 1.0 copy.42
  405.5 1.0 copy.43
  406.5 1.0 copy.44
  407.4 1.0 copy.45
  408.4 1.0 copy.46
  409.4 1.0 copy.47
  (53 shorter events, 1.1 us)
Async XLA Ops:
  9.0 62.6 %copy-start = (bf16[1,128,2048]{2,1,0:T(8,128)(2,1)S(1)}, bf16[1,128,2048]{2,1,0:T(8,128)(2,1)}, u32[]{:S(2)}) copy-start(bf16[1,128,2048]{2,1,0:T(8,128)(2,1)} %param.14) | copy-start | bytes 1572868
  71.6 1.7 copy-start.14
  71.6 1.7 copy-start.15
  133.4 1.7 copy-start.3
  135.2 1.0 copy-start.2
  137.2 80.6 %copy-start.13 = (f32[2048]{0:T(1024)S(1)}, f32[2048]{0:T(1024)}, u32[]{:S(2)}) copy-start(f32[2048]{0:T(1024)} %param.23) | copy-start | bytes 24580
  217.8 1.6 copy-start.1
  398.7 3.2 copy-start.4
  401.9 1.0 copy-start.12
  401.9 1.8 copy-start.11
  401.9 2.6 copy-start.10
  402.9 2.6 copy-start.9
  404.5 1.9 copy-start.8
  405.5 1.9 copy-start.7
  406.5 1.9 copy-start.6
  407.4 1.9 copy-start.5

commit v5 on v4

--- a/solution.py
+++ b/solution.py
@@ -2,6 +2,7 @@
 
 import jax
 import jax.numpy as jnp
+import numpy as np
 from jax import lax
 from jax.experimental import pallas as pl
 from jax.experimental.pallas import tpu as pltpu
@@ -300,7 +301,7 @@
 
         @pl.when(self.last)
         def _():
-            fac = self.fac[p % self.heads]
+            fac = self.fac[0, lax.axis_index("tp") * self.heads + p % self.heads]
             self.give(p).wait_recv()
             early = self.pair[p].astype(F32)
             chip_sum = early * fac + self.local[p].astype(F32)
@@ -355,6 +356,16 @@
 def turn_back(g, cos, sin):
     lo, hi = g[:, : DK // 2], g[:, DK // 2 :]
     return jnp.concatenate([lo * cos + hi * sin, hi * cos - lo * sin], 1)
+
+
+def row_stats(v):
+    center = v - jnp.mean(v, -1, keepdims=True)
+    return center, lax.rsqrt(jnp.mean(center * center, -1, keepdims=True) + EPS)
+
+
+def norm_pull(grad, hat, inv, gain):
+    g = grad * gain
+    return (g - jnp.mean(g, -1, keepdims=True) - hat * jnp.mean(g * hat, -1, keepdims=True)) * inv
 
 
 def norm_of(m):
@@ -592,14 +603,14 @@
 
 def mixer_kernel(n, chips, heads, *refs):
     (
-        fac, x, og, wk_h, wv_h, wq_h, ws_h, wo_h, decay, qfac, kfac, cos, sin,
-        x_o, og_o, q_o, k_o, v_o, sp_o, mx_o, prior_o, gated_o, attn,
-        x_all, og_all, q, k, v, sp, mx, prior, gated, wk, wv, wq, ws, wo, acc, parts, local,
-    ) = refs[:40]
-    near, far, hold = refs[40:43]
-    chain_refs = refs[43:51]
-    wsem, gs, gr, os, orr, ss, sr, es, er, osem, bsem = refs[51:]
-    rows = x.shape[0]
+        fac, raw, og, wk_h, wv_h, wq_h, ws_h, wo_h, gain, bias, freq,
+        x_o, og_o, q_o, k_o, v_o, sp_o, mx_o, prior_o, gated_o, attn, decay, qfac, kfac, cos, sin,
+        x_all, og_all, q, k, v, sp, mx, prior, gated, x, wk, wv, wq, ws, wo, acc, parts, local,
+    ) = refs[:44]
+    near, far, hold = refs[44:47]
+    chain_refs = refs[47:55]
+    wsem, gs, gr, os, orr, ss, sr, es, er, osem, bsem = refs[55:]
+    rows = raw.shape[0]
     gather = Gather(n, x, x_all, gs, gr)
     gather_og = Gather(n, og, og_all, os, orr)
     ends = Ends(chips)
@@ -616,8 +627,26 @@
     ]
     for load in loads:
         load.start()
+    slab = 16
+
+    @pl.loop(0, rows // slab)
+    def _(r):
+        here = pl.ds(pl.multiple_of(r * slab, slab), slab)
+        center, inv = row_stats(raw[here].astype(F32))
+        x[here] = (center * inv * gain[...] + bias[...]).astype(BF)
+
     greet(gather.peers + chain.peers)
     gather.start()
+    place = lax.broadcasted_iota(jnp.int32, (rows, 1), 0).astype(F32)
+    angles = (lax.axis_index("seq").astype(F32) * rows + place) * freq[...]
+    cos[...] = jnp.cos(angles)
+    sin[...] = jnp.sin(angles)
+    lag = place - lax.broadcasted_iota(jnp.int32, (rows, rows), 1).astype(F32)
+    for h in range(heads):
+        rate = fac[1, lax.axis_index("tp") * heads + h]
+        decay[h] = jnp.where(lag >= 0, jnp.exp(jnp.maximum(lag, 0.0) * rate), 0.0)
+        qfac[h] = jnp.exp((place + 1.0) * rate)
+        kfac[h] = jnp.exp((rows - 1.0 - place) * rate)
 
     @pl.when(ends.gives)
     def _():
@@ -757,7 +786,7 @@
         chain.drain(p)
 
 
-def mixer(fac, x, og, wk, wv, wq, ws, wo, decay, qfac, kfac, cos, sin, cid):
+def mixer(fac, x, og, wk, wv, wq, ws, wo, gain, bias, freq, cid):
     n = lax.axis_size("tp")
     chips = lax.axis_size("seq") // 2
     rows, model = x.shape
@@ -782,9 +811,14 @@
             shape((pieces, DK, DV), BF),
             shape((total, heads * DV), BF),
             shape((rows, model), F32),
+            shape((heads, rows, rows), F32),
+            shape((heads, rows, 1), F32),
+            shape((heads, rows, 1), F32),
+            shape((rows, DK // 2), F32),
+            shape((rows, DK // 2), F32),
         ),
-        in_specs=[pl.BlockSpec(memory_space=pltpu.SMEM), vmem, vmem] + [hbm] * 5 + [vmem] * 5,
-        out_specs=(hbm,) * 9 + (vmem,),
+        in_specs=[pl.BlockSpec(memory_space=pltpu.SMEM), vmem, vmem] + [hbm] * 5 + [vmem] * 3,
+        out_specs=(hbm,) * 9 + (vmem,) * 6,
         scratch_shapes=[
             pltpu.VMEM((n, rows, model), BF),
             pltpu.VMEM((n, rows, model), BF),
@@ -795,6 +829,7 @@
             pltpu.VMEM((total, heads * DV), F32),
             pltpu.VMEM((pieces, DK, DV), BF),
             pltpu.VMEM((total, heads * DV), BF),
+            pltpu.VMEM((rows, model), BF),
         ]
         + [pltpu.VMEM(w.shape, BF) for w in (wk, wv, wq, ws, wo)]
         + [
@@ -809,7 +844,7 @@
         + [dma((n - 1,)), dma((n - 1,)), dma((6,)), dma((3, n))],
         compiler_params=params(cid),
         name="mixer",
-    )(fac, x, og, wk, wv, wq, ws, wo, decay, qfac, kfac, cos, sin)
+    )(fac, x, og, wk, wv, wq, ws, wo, gain, bias, freq)
 
 
 GELU_C = 0.7978845608028654
@@ -826,12 +861,13 @@
 
 def mlp_kernel(n, chips, *refs):
     (
-        x, og_h, wg_h, wu_h, wd_h,
-        x_o, hidden_o, gate_o, upper_o, mlp_o, grad_two, gate_late, up_late,
-        og_all, x_all, hidden, gate_low, upper_low, mlp_parts, wg, wu, wd, hg, acc_g, acc_u, acc, parts, near, far, hold,
+        raw, attn, cot, gain, bias, og_h, wg_h, wu_h, wd_h,
+        x_o, hidden_o, gate_o, upper_o, mlp_o, res_grad, res_low, vec, gate_late, up_late,
+        og_all, x, grad_two, x_all, hidden, gate_low, upper_low, mlp_parts, wg, wu, wd, hg, acc_g, acc_u, acc, parts, near, far, hold,
         wsem, gs, gr, ss, sr, es, er, osem, bsem,
     ) = refs
-    rows = x.shape[0]
+    rows = raw.shape[0]
+    slab = 16
     gather = Gather(n, x, x_all, gs, gr)
     scatter = Scatter(n, parts, near, far, hold, ss, sr)
     ends = Ends(chips)
@@ -842,6 +878,12 @@
     loads.append(pltpu.make_async_copy(og_h, og_all, wsem.at[3]))
     for load in [loads[0], loads[3], loads[1], loads[2]]:
         load.start()
+    @pl.loop(0, rows // slab)
+    def _(r):
+        here = pl.ds(pl.multiple_of(r * slab, slab), slab)
+        center, inv = row_stats(raw[here].astype(F32) + attn[here])
+        x[here] = (center * inv * gain[...] + bias[...]).astype(BF)
+
     greet(gather.peers + ends.peers)
     gather.start()
     me = gather.source(0)
@@ -870,7 +912,6 @@
     gather.relays()
     loads[1].wait()
     loads[2].wait()
-    slab = 16
 
     def units(block, back_at, extra):
         start = pl.multiple_of(block * rows, rows)
@@ -969,6 +1010,18 @@
         grad_two[:, cols] = total
 
     scatter.finish(write)
+    vec[...] = jnp.zeros_like(vec)
+
+    @pl.loop(0, rows // slab)
+    def _(r):
+        here = pl.ds(pl.multiple_of(r * slab, slab), slab)
+        center, inv = row_stats(raw[here].astype(F32) + attn[here])
+        hat, grad = center * inv, grad_two[here]
+        total = cot[here].astype(F32) + norm_pull(grad, hat, inv, gain[...])
+        res_grad[here] = total
+        res_low[here] = total.astype(BF)
+        vec[2:3] += jnp.sum(grad * hat, 0, keepdims=True)
+        vec[3:4] += jnp.sum(grad, 0, keepdims=True)
 
     @pl.loop(n // 2, n)
     def _(i):
@@ -1001,10 +1054,10 @@
             hand(i).wait_send()
 
 
-def mlp(x, og_all, wg, wu, wd, cid):
+def mlp(raw, attn, cot, gain, bias, og_all, wg, wu, wd, cid):
     n = lax.axis_size("tp")
     chips = lax.axis_size("seq") // 2
-    rows, model = x.shape
+    rows, model = raw.shape
     width = wg.shape[1]
     total = n * rows
     dma = pltpu.SemaphoreType.DMA
@@ -1021,13 +1074,17 @@
             shape((2 * total - rows, width), BF),
             shape((n, rows, model), BF),
             shape((rows, model), F32),
+            shape((rows, model), BF),
+            shape((8, model), F32),
             shape((rows, width), F32),
             shape((rows, width), F32),
         ),
-        in_specs=[vmem] + [hbm] * 4,
-        out_specs=(hbm,) * 5 + (vmem,) * 3,
+        in_specs=[vmem] * 5 + [hbm] * 4,
+        out_specs=(hbm,) * 5 + (vmem,) * 5,
         scratch_shapes=[
             pltpu.VMEM(og_all.shape, BF),
+            pltpu.VMEM((rows, model), BF),
+            pltpu.VMEM((rows, model), F32),
             pltpu.VMEM((2 * n, rows, model), BF),
             pltpu.VMEM((2 * total, width), BF),
             pltpu.VMEM((2 * total, width), BF),
@@ -1048,7 +1105,7 @@
         + [dma((n,)), dma((n,)), dma((5,)), dma((4, n))],
         compiler_params=params(cid),
         name="mlp",
-    )(x, og_all, wg, wu, wd)
+    )(raw, attn, cot, gain, bias, og_all, wg, wu, wd)
 
 
 def mixer_back_kernel(n, chips, heads, *refs):
@@ -1308,33 +1365,40 @@
 def weights_kernel(chips, *refs):
     (
         two, og, og_late, hidden, gate_low, gate_late, up_low, up_late,
-        one, res, swish_low, gated, value_low, qk_low, vec,
-        down_o, gate_o, up_o, swish_o, mixer_o, value_o, query_o, key_o, vec_out,
-    ) = refs[:24]
+        one, res, swish_low, gated, value_low, qk_low,
+        vec_two, gain, grad_h, raw_h, res_h, attn_h, mlp_h,
+        down_o, gate_o, up_o, swish_o, mixer_o, value_o, query_o, key_o, back_o, outs_o, vec_out,
+    ) = refs[:32]
     mlp = LineSums(
         chips, 1, chips - 2, ((two,), (og, og_late)),
-        ((gate_low, gate_late), (up_low, up_late), (hidden,)), (0, 0, 1), refs[24:36],
+        ((gate_low, gate_late), (up_low, up_late), (hidden,)), (0, 0, 1), refs[32:44],
     )
     mix = LineSums(
         chips, 0, chips - 1, ((one,), (res,)), ((swish_low,), (gated,), (value_low,), (qk_low,)),
-        (0, 1, 0, 0), refs[36:48],
+        (0, 1, 0, 0), refs[44:56],
     )
-    turned, osem, vec_near, vec_sum, vec_far, vs, vr, us, ur = refs[48:]
+    (
+        turned, osem, grad, raw, res_grad, attn, mlp_out, back, outs, csem, dsem,
+        vec, vec_near, vec_mid, vec_far, vs, vr, us, ur,
+    ) = refs[56:]
     s, t = lax.axis_index("seq"), lax.axis_index("tp")
-    span, tp = 2 * chips, vec.shape[0]
+    span, tp = 2 * chips, vec_far.shape[0] + 1
+    share = vec_mid.shape[1]
     ring = [((s + d) % span, t) for d in range(1, span)]
     cross = [(s, (t + d) % tp) for d in range(1, tp)]
+
+    def part(who):
+        return pl.ds(pl.multiple_of(who * share, share), share)
+
     greet(ring + cross)
     vec_first = [
-        remote(vec.at[(t + d) % tp], vec_near.at[d - 1], vs, vr, d - 1, cross[d - 1])
-        for d in range(1, tp)
+        remote(vec.at[:, part((s + d) % span)], vec_near.at[d - 1], vs, vr, d - 1, ring[d - 1])
+        for d in range(1, span)
     ]
     vec_last = [
-        remote(vec_sum.at[(s + d) % span], vec_far.at[d - 1], us, ur, d - 1, ring[d - 1])
-        for d in range(1, span)
+        remote(vec_mid, vec_far.at[d - 1], us, ur, d - 1, cross[d - 1]) for d in range(1, tp)
     ]
-    for copy in vec_first:
-        copy.start()
+    vec[...] = vec_two[...]
     for u in range(mix.units):
         if u < mlp.units:
             mlp.share(u)
@@ -1369,10 +1433,44 @@
 
         @pl.when(u == 0)
         def _():
-            total = vec[t]
+            chunk = raw.shape[0]
+
+            @pl.loop(0, grad_h.shape[0] // chunk)
+            def _(c):
+                here = pl.ds(pl.multiple_of(c * chunk, chunk), chunk)
+                pairs = (grad_h, grad), (raw_h, raw), (res_h, res_grad), (attn_h, attn), (mlp_h, mlp_out)
+                ins = [
+                    pltpu.make_async_copy(a.at[here], b, csem.at[i])
+                    for i, (a, b) in enumerate(pairs)
+                ]
+                for copy in ins:
+                    copy.start()
+                for copy in ins:
+                    copy.wait()
+                value = raw[...].astype(F32)
+                outs[...] = (value + attn[...] + mlp_out[...]).astype(BF)
+                center, inv = row_stats(value)
+                hat = center * inv
+                vec[0:1] += jnp.sum(grad[...] * hat, 0, keepdims=True)
+                vec[1:2] += jnp.sum(grad[...], 0, keepdims=True)
+                back[...] = (res_grad[...] + norm_pull(grad[...], hat, inv, gain[...])).astype(BF)
+                puts = [
+                    pltpu.make_async_copy(a, b.at[0, here], dsem.at[i])
+                    for i, (a, b) in enumerate(((back, back_o), (outs, outs_o)))
+                ]
+                for copy in puts:
+                    copy.start()
+                for copy in puts:
+                    copy.wait()
+
+            for copy in vec_first:
+                copy.start()
+
+        @pl.when(u == 1)
+        def _():
             for copy in vec_first:
                 copy.wait_recv()
-            vec_sum[...] = total + jnp.sum(vec_near[...], 0)
+            vec_mid[...] = vec[:, part(s)] + jnp.sum(vec_near[...], 0)
             for copy in vec_last:
                 copy.start()
 
@@ -1403,10 +1501,9 @@
     mix.finish(mix.units - 1)
     for copy in copies[6:]:
         copy.start()
-    vec_total = vec_sum[s]
     for copy in vec_last:
         copy.wait_recv()
-    vec_out[...] = vec_total + jnp.sum(vec_far[...], 0)
+    vec_out[...] = vec_mid[...] + jnp.sum(vec_far[...], 0)
     for copy in vec_first + vec_last:
         copy.wait_send()
     mlp.drain()
@@ -1418,7 +1515,7 @@
 
 def weight_sums(
     two, og, og_late, hidden, gate_low, gate_late, up_low, up_late, one, res, swish_low, gated, value_low,
-    qk_low, vec, cid,
+    qk_low, vec_two, gain, grad, raw, res_grad, attn, mlp_out, cid,
 ):
     chips = lax.axis_size("seq") // 2
     tokens, model = one.shape
@@ -1430,7 +1527,9 @@
     vmem = pl.BlockSpec(memory_space=pltpu.VMEM)
     hbm = pl.BlockSpec(memory_space=pl.ANY)
     shape = lambda *a: jax.ShapeDtypeStruct(a, F32)
-    ring, cross = 2 * chips - 1, vec.shape[0] - 1
+    ring, cross = 2 * chips - 1, lax.axis_size("tp") - 1
+    rows, share, chunk = raw.shape[0], model // (2 * chips), 16
+    part = lambda dtype: pltpu.VMEM((chunk, model), dtype)
     return pl.pallas_call(
         functools.partial(weights_kernel, chips),
         out_shape=(
@@ -1442,32 +1541,39 @@
             shape(cut, width),
             shape(cut, keys),
             shape(cut, keys),
-            shape(*vec.shape[2:]),
+            jax.ShapeDtypeStruct((1, rows, model), BF),
+            jax.ShapeDtypeStruct((1, rows, model), BF),
+            shape(8, share),
         ),
-        in_specs=[hbm] * 14 + [vmem],
-        out_specs=(hbm,) * 8 + (vmem,),
+        in_specs=[hbm] * 14 + [vmem] * 2 + [hbm] * 5,
+        out_specs=(hbm,) * 10 + (vmem,),
         scratch_shapes=line_scratch(chips, 3, 2, mlp_tokens, cut, mlp_width)
         + line_scratch(chips, 4, 2, tokens, cut, width)
         + [
             pltpu.VMEM((width, cut), F32),
             dma((8,)),
-            pltpu.VMEM((cross,) + vec.shape[1:], F32),
-            pltpu.VMEM(vec.shape[1:], F32),
-            pltpu.VMEM((ring,) + vec.shape[2:], F32),
+            part(F32),
+            part(BF),
+            part(F32),
+            part(F32),
+            part(F32),
+            part(BF),
+            part(BF),
+            dma((5,)),
+            dma((2,)),
+            pltpu.VMEM((8, model), F32),
+            pltpu.VMEM((ring, 8, share), F32),
+            pltpu.VMEM((8, share), F32),
+            pltpu.VMEM((cross, 8, share), F32),
+            dma((ring,)),
+            dma((ring,)),
             dma((cross,)),
             dma((cross,)),
-            dma((ring,)),
-            dma((ring,)),
         ],
         compiler_params=params(cid),
         name="weights",
-    )(two, og, og_late, hidden, gate_low, gate_late, up_low, up_late, one, res, swish_low, gated, value_low, qk_low, vec)
-
-
-def layer_norm(values, gain, bias):
-    center = values - jnp.mean(values, -1, keepdims=True)
-    spread = jnp.mean(center * center, -1, keepdims=True)
-    return center * lax.rsqrt(spread + EPS) * gain + bias
+    )(two, og, og_late, hidden, gate_low, gate_late, up_low, up_late, one, res, swish_low, gated, value_low,
+      qk_low, vec_two, gain, grad, raw, res_grad, attn, mlp_out)
 
 
 def shards(
@@ -1488,64 +1594,49 @@
 ):
     _, rows, model = inputs.shape
     heads = query_weight.shape[1] // DK
-    inputs_full = inputs[0].astype(F32)
-    cotangent = output_grad[0]
+    seqs, tps = lax.axis_size("seq"), lax.axis_size("tp")
+    raw, cotangent = inputs[0], output_grad[0]
+    row = lambda v: v.reshape(1, model)
+    flat = lambda a: a.reshape(-1, model)
 
     half_width = DK // 2
-    frequencies = jnp.power(10000.0, -jnp.arange(half_width, dtype=F32) / half_width)
-    steps_in = jnp.arange(rows, dtype=F32)
-    positions = lax.axis_index("seq").astype(F32) * rows + steps_in
-    angles = positions[:, None] * frequencies[None, :]
-    cosine, sine = jnp.cos(angles), jnp.sin(angles)
-    head_ids = (lax.axis_index("tp") * heads + jnp.arange(heads)).astype(F32)
-    decays = 1.0 - jnp.exp2(-5.0 - head_ids)
-    lag = steps_in[:, None] - steps_in[None, :]
-    decay_mat = jnp.where(
-        lag[None] >= 0, jnp.power(decays[:, None, None], jnp.maximum(lag, 0.0)[None]), 0.0
+    frequencies = np.power(
+        np.float32(10000.0), -np.arange(half_width, dtype=np.float32) / np.float32(half_width)
+    )[None]
+    decays = 1.0 - np.exp2(-5.0 - np.arange(heads * tps))
+    factors = np.stack([np.power(decays, rows), np.log(decays)]).astype(np.float32)
+
+    (
+        one_all, grad_all, query, key, value, swish_pre, mixed, prior, gated, attn_out,
+        decay_mat, query_fac, key_fac, cosine, sine,
+    ) = mixer(
+        factors, raw, cotangent, key_weight, value_weight, query_weight, swish_weight,
+        output_weight, row(attn_gain), row(attn_bias), frequencies, 0,
     )
-    query_fac = jnp.power(decays[:, None], steps_in[None, :] + 1.0)[:, :, None]
-    key_fac = jnp.power(decays[:, None], rows - 1.0 - steps_in[None, :])[:, :, None]
-    block_fac = jnp.power(decays, rows * 1.0)
-
-    normed_one = layer_norm(inputs_full, attn_gain, attn_bias).astype(BF)
-    one_all, grad_all, query, key, value, swish_pre, mixed, prior, gated, attn_out = mixer(
-        block_fac, normed_one, cotangent, key_weight, value_weight, query_weight, swish_weight,
-        output_weight, decay_mat, query_fac, key_fac, cosine, sine, 0,
+    two_all, hidden, gate_low, upper_low, mlp_parts, res_grad, res_low, vectors, gate_pre, up_pre = mlp(
+        raw, attn_out, cotangent, row(mlp_gain), row(mlp_bias), grad_all, gate_weight, up_weight,
+        down_weight, 1,
     )
-    hidden_res = inputs_full + attn_out
-    normed_two = layer_norm(hidden_res, mlp_gain, mlp_bias).astype(BF)
-    two_all, hidden, gate_low, upper_low, mlp_parts, normed_two_grad, gate_pre, up_pre = mlp(
-        normed_two, grad_all, gate_weight, up_weight, down_weight, 1
-    )
-    flat = lambda a: a.reshape(-1, model)
-    _, pull_two = jax.vjp(layer_norm, hidden_res, mlp_gain, mlp_bias)
-    res_back, mlpgain_part, mlpbias_part = pull_two(normed_two_grad)
-    res_grad = cotangent.astype(F32) + res_back
-    res_all, swish_low, value_low, qk_low, normed_one_grad, mlp_out, og_late, gate_late, up_late = mixer_back(
-        block_fac, res_grad.astype(BF), output_weight, query_weight, key_weight, value_weight, swish_weight,
+    (
+        res_all, swish_low, value_low, qk_low, normed_one_grad, mlp_out, og_late, gate_late, up_late,
+    ) = mixer_back(
+        factors, res_low, output_weight, query_weight, key_weight, value_weight, swish_weight,
         query, key, value, swish_pre, mixed, prior, mlp_parts, decay_mat, query_fac, key_fac,
         cosine, sine, grad_all, down_weight, gate_pre, up_pre, 2,
     )
-    outputs = (hidden_res + mlp_out).astype(BF)
-    _, pull_one = jax.vjp(layer_norm, inputs_full, attn_gain, attn_bias)
-    input_back, attngain_part, attnbias_part = pull_one(normed_one_grad)
-    input_grad = (res_grad + input_back).astype(BF)
-
-    seqs, tps = lax.axis_size("seq"), lax.axis_size("tp")
+    (
+        down_grad, gate_grad, up_grad, swish_grad, mixer_grad, value_grad, query_grad, key_grad,
+        input_grad, outputs, vector_sums,
+    ) = weight_sums(
+        flat(two_all), flat(grad_all), og_late, hidden, gate_low, gate_late, upper_low, up_late,
+        flat(one_all), flat(res_all), swish_low, gated, value_low, qk_low, vectors, row(attn_gain),
+        normed_one_grad, raw, res_grad, attn_out, mlp_out, 3,
+    )
     each = model // (seqs * tps)
-    vectors = jnp.stack([attngain_part, attnbias_part, mlpgain_part, mlpbias_part])
-    vectors = vectors.reshape(4, seqs, tps, each).transpose(2, 1, 0, 3).reshape(tps, seqs, 4 * each)
-    vectors = jnp.pad(vectors, ((0, 0), (0, 0), (0, 1024 - 4 * each))).reshape(tps, seqs, 8, 128)
-    down_grad, gate_grad, up_grad, swish_grad, mixer_grad, value_grad, query_grad, key_grad, vector_sums = (
-        weight_sums(
-            flat(two_all), flat(grad_all), og_late, hidden, gate_low, gate_late, upper_low, up_late, flat(one_all), flat(res_all), swish_low, gated,
-            value_low, qk_low, vectors, 3,
-        )
-    )
-    vector_sums = vector_sums.reshape(-1)[: 4 * each].reshape(4, each)
+    vector_sums = lax.dynamic_slice(vector_sums, (0, lax.axis_index("tp") * each), (4, each))
     return (
-        outputs[None],
-        input_grad[None],
+        outputs,
+        input_grad,
         query_grad,
         key_grad,
         value_grad,

time: 417 us -> 398 us (0.954); the launches traced: 411 us -> 398 us
  other arithmetic: 18.9 us -> 0 us
  Pallas kernels: 379 us -> 385 us
    reduce_sum x8 -> x0, other arithmetic: 8.48 us -> none  [the longest x3 3.88 us: layer_norm(): return center * lax.rsqrt(spread + EPS) * gain + bias]
    convert_element_type x3 -> x0, other arithmetic: 4.29 us -> none  [the longest x1 2.26 us: shards(): normed_one = layer_norm(inputs_full, attn_gain, attn_bias).astype(BF)]
    unnamed x42 -> x26, local copies, waits for them, and re-layouts: 8.86 us -> 11.3 us
where the time goes in v5:
time: 398 us
  Pallas kernels  385 us (97%)
  local copies, waits for them, and re-layouts  12.7 us (3%)
    pallas_call x1, Pallas kernels, weight_sums(): pl.pallas_call(functools.partial(weights_kernel, chips), out_shape=(shape...  177 us
    pallas_call x1, Pallas kernels, mixer_back(): pl.pallas_call(functools.partial(mixer_back_kernel, n, chips, heads), out...  80.9 us
    pallas_call x1, Pallas kernels, mixer(): pl.pallas_call(functools.partial(mixer_kernel, n, chips, heads), out_shap...  64.2 us
    pallas_call x1, Pallas kernels, mlp(): pl.pallas_call(functools.partial(mlp_kernel, n, chips), out_shape=(shape(...  62 us
    unnamed x26, local copies, waits for them, and re-layouts  11.3 us

profile of v5, /device:TPU:0, one launch (start us, length us, event | category | flops | bytes accessed | tf_op | source)
XLA Modules:
  0.0 397.9 jit_solution(1334017324209587570)
XLA Ops:
  0.6 64.2 %mixer.1 = (bf16[4,128,2048]{2,1,0:T(8,128)(2,1)}, bf16[7,128,2048]{2,1,0:T(8,128)(2,1)}, bf16[512,512]{1,0:T(8,128)(2,1)}, bf16[512,512]{1,0:T(8,128)(2,1)}, bf...) custom-call(f32[2,8]{1,0:T(2,128)} %constant.14.clone.refs_0_, ...), custom_call_target="tpu_custom_call" | custom-call | tf_op jit(solution)/shard_map/mixer/pallas_call | solution.py:801
  64.8 62.0 %mlp.1 = (bf16[8,128,2048]{2,1,0:T(8,128)(2,1)}, bf16[1024,1024]{1,0:T(8,128)(2,1)}, bf16[896,1024]{1,0:T(8,128)(2,1)}, bf16[896,1024]{1,0:T(8,128)(2,1)}, bf16[...) custom-call(bf16[128,2048]{1,0:T(8,128)(2,1)} %bitcast.20, ...), custom_call_target="tpu_custom_call" | custom-call | tf_op jit(solution)/shard_map/mlp/pallas_call | solution.py:1068
  126.8 80.9 %mixer_back.1 = (bf16[4,128,2048]{2,1,0:T(8,128)(2,1)}, bf16[512,1024]{1,0:T(8,128)(2,1)}, bf16[512,1024]{1,0:T(8,128)(2,1)}, bf16[512,1024]{1,0:T(8,128)(2,1)},...) custom-call(f32[2,8]{1,0:T(2,128)} %constant.14.clone.refs_0_, ...), custom_call_target="tpu_custom_call" | custom-call | tf_op jit(solution)/shard_map/mixer_back/pallas_call | solution.py:1322
  207.8 177.5 %weights.1 = (f32[1024,256]{1,0:T(8,128)}, f32[256,1024]{1,0:T(8,128)}, f32[256,1024]{1,0:T(8,128)}, f32[256,1024]{1,0:T(8,128)}, f32[1024,256]{1,0:T(8,128)}, /...) custom-call(bf16[1024,2048]{1,0:T(8,128)(2,1)} %bitcast.22, ...), custom_call_target="tpu_custom_call" | custom-call | tf_op jit(solution)/shard_map/weights/pallas_call | solution.py:1533
  385.2 0.0 copy-start.7
  385.2 0.0 copy-start.6
  385.3 0.8 constant_dynamic-slice_fusion
  386.1 0.5 slice_bitcast_fusion
  386.6 0.0 copy-start.5
  386.6 2.0 copy.40
  388.6 1.9 copy.41
  390.5 0.0 copy-done.7
  390.5 0.0 copy-start.4
  390.5 0.8 copy.42
  391.3 0.0 copy-done.6
  391.3 0.8 copy.43
  392.1 0.0 copy-done.5
  392.1 0.0 copy-start.3
  392.1 1.0 copy.44
  393.1 0.0 copy-done.4
  393.1 0.0 copy-start.2
  393.1 1.0 copy.45
  394.0 0.0 copy-done.3
  394.0 0.0 copy-start.1
  394.0 1.0 copy.46
  395.0 0.0 copy-done.2
  395.0 0.0 copy-start
  395.0 1.0 copy.47
  396.0 0.0 copy-done.1
  396.0 1.0 copy.48
  397.0 0.0 copy-done
  397.0 1.0 copy.49
Async XLA Ops:
  385.2 5.2 %copy-start.7 = (f32[256,512]{1,0:T(8,128)S(1)}, f32[256,512]{1,0:T(8,128)}, u32[]{:S(2)}) copy-start(f32[256,512]{1,0:T(8,128)} %get-tuple-element.124) | copy-start | bytes 1572868
  385.2 6.0 %copy-start.6 = (f32[256,512]{1,0:T(8,128)S(1)}, f32[256,512]{1,0:T(8,128)}, u32[]{:S(2)}) copy-start(f32[256,512]{1,0:T(8,128)} %get-tuple-element.125) | copy-start | bytes 1572868
  386.6 5.4 %copy-start.5 = (f32[256,1024]{1,0:T(8,128)S(1)}, f32[256,1024]{1,0:T(8,128)}, u32[]{:S(2)}) copy-start(f32[256,1024]{1,0:T(8,128)} %get-tuple-element.126) | copy-start | bytes 3145732
  390.5 2.6 copy-start.4
  392.1 1.9 copy-start.3
  393.1 1.9 copy-start.2
  394.0 1.9 copy-start.1
  395.0 1.9 copy-start

commit v6 on v5

--- a/solution.py
+++ b/solution.py
@@ -16,7 +16,7 @@
 MESH = pl.DeviceIdType.MESH
 BF = jnp.bfloat16
 F32 = jnp.float32
-VMEM_LIMIT = 61 * 1024 * 1024
+VMEM_LIMIT = 63 * 1024 * 1024 - 512 * 1024
 
 
 def remote(src, dst, ssem, rsem, slot, dev):
@@ -201,17 +201,23 @@
                 for copy in two:
                     copy.wait_recv()
                 write(
+                    slice(None),
                     self.cols[side],
                     self.parts[self.t, :, self.cols[side]].astype(F32)
                     + self.near[side, 0].astype(F32)
                     + self.far[side].astype(F32),
                 )
         else:
-            total = self.parts[self.t].astype(F32)
-            for k, copy in enumerate(self.copies):
+            for copy in self.copies:
                 copy.wait_recv()
-                total = total + self.near[k].astype(F32)
-            write(slice(None), total)
+
+            @pl.loop(0, self.parts.shape[1] // 16)
+            def _(r):
+                at = pl.ds(pl.multiple_of(r * 16, 16), 16)
+                total = self.parts[self.t, at].astype(F32)
+                for k in range(self.n - 1):
+                    total = total + self.near[k, at].astype(F32)
+                write(at, slice(None), total)
 
     def drain(self):
         for copy in self.copies:
@@ -282,6 +288,28 @@
         @pl.when(due & (jnp.logical_not(ends) | (now >= total)))
         def _():
             self.step(self.piece(gather, jnp.maximum(index, 0)))
+
+    def planned(self, gather, i, plan):
+        block = jnp.int32(0)
+        for place, turn, ahead in plan:
+            block = jnp.where((self.place == place) & (i == turn), ahead, block)
+
+        @pl.when(block > 0)
+        def _():
+            @pl.loop(0, self.heads)
+            def _(h):
+                self.step(self.piece(gather, block * self.heads + h))
+
+    def due(self, gather, i, plan):
+        now = self.place > 0
+        for place, _, ahead in plan:
+            now = now & ((self.place != place) | (i != ahead))
+
+        @pl.when(now)
+        def _():
+            @pl.loop(0, self.heads)
+            def _(h):
+                self.step(self.piece(gather, i * self.heads + h))
 
     def begin(self, p):
         @pl.when(self.first)
@@ -544,19 +572,19 @@
 
         @pl.when(self.adds())
         def _():
-            self.out[u] = self.product(u, chip)
+            self.out[0] = self.product(u, chip)
 
         @pl.when((chip < self.lo) | (chip > self.hi))
         def _():
-            self.out[u] = jnp.zeros(self.out.shape[1:], F32)
+            self.out[0] = jnp.zeros(self.out.shape[1:], F32)
 
         @pl.when(chip > self.lo)
         def _():
-            self.out[u] += self.arrived(u, chip)
+            self.out[0] += self.arrived(u, chip)
 
         @pl.when(chip < self.hi)
         def _():
-            self.out[u] += self.arrived(u, self.chips)
+            self.out[0] += self.arrived(u, self.chips)
 
     def drain(self):
         @pl.when(self.adds())
@@ -589,7 +617,7 @@
         pltpu.VMEM((kinds, chips, 2 * tokens, cut), BF),
         pltpu.VMEM((units, 2 * tokens, width), BF),
         pltpu.VMEM((units, chips + 1) + block, BF),
-        pltpu.VMEM((units,) + block, F32),
+        pltpu.VMEM((1,) + block, F32),
         dma((kinds, chips, 2)),
         dma((units, 2)),
         dma((kinds, chips, 2)),
@@ -628,6 +656,7 @@
     for load in loads:
         load.start()
     slab = 16
+    plan = ((1, 1, 1), (1, 3, 2)) if n == 4 else ()
 
     @pl.loop(0, rows // slab)
     def _(r):
@@ -707,7 +736,7 @@
             scores = (dot(query, k[at, kc], 1, 1) * decay[h]).astype(BF)
             mx[at, vc] = dot(scores, v[at, vc])
             sp[at, vc] = dot(x_all[j], ws[:, vc])
-            chain.tick(gather, i * heads + h)
+        chain.planned(gather, i, plan)
 
     for put in puts[3:5]:
         put.start()
@@ -727,9 +756,10 @@
     def _(step):
         i = (step + 1) % n
         j = gather.source(i)
+        chain.due(gather, i, plan)
         gather_og.arrive(i)
 
-        @pl.when(ends.gives & (i > 0) & (i < n - 1))
+        @pl.when(ends.gives & (chain.place > 0) & (i > 0) & (i < n - 1))
         def _():
             hand(i).start()
 
@@ -738,21 +768,27 @@
             vc = slice(h * DV, (h + 1) * DV)
             kc = slice(h * DK, (h + 1) * DK)
             p = j * heads + h
-            chain.tick(gather, (n + step) * heads + h)
             query_dec = (q[at, kc].astype(F32) * qfac[h]).astype(BF)
             mx[at, vc] += dot(query_dec, prior[p])
             pre = sp[at, vc]
             gated[at, vc] = (pre * jax.nn.sigmoid(pre) * norm_of(mx[at, vc])[0]).astype(BF)
         parts[j] = dot(gated[at], wo[...]).astype(BF)
         scatter.send(i)
+
+        @pl.when(ends.gives & (chain.place == 0) & (step == n - 2))
+        def _():
+            @pl.loop(1, n - 1)
+            def _(c):
+                hand(c).start()
+
         for put in blocks(j):
             put.start()
 
     puts[5].start()
     scatter.relay()
 
-    def write(cols, total):
-        attn[:, cols] = total
+    def write(at, cols, total):
+        attn[at, cols] = total
 
     scatter.finish(write)
     gather.drain()
@@ -1006,8 +1042,8 @@
 
     puts[4].start()
 
-    def write(cols, total):
-        grad_two[:, cols] = total
+    def write(at, cols, total):
+        grad_two[at, cols] = total
 
     scatter.finish(write)
     vec[...] = jnp.zeros_like(vec)
@@ -1111,15 +1147,14 @@
 def mixer_back_kernel(n, chips, heads, *refs):
     (
         fac, res, wo_h, wq_h, wk_h, wv_h, ws_h, q_h, k_h, v_h, sp_h, mx_h, prior_h, mlp_h, decay, qfac, kfac, cos, sin, og_h, wd_h, gate_late, up_late,
-        res_o, swish_o, value_o, qk_o, grad_one, mlp_out, og_late, gate_low, upper_low,
+        res_o, swish_o, value_o, qk_o, parts_o, mlp_out, og_late, gate_low, upper_low,
         q, k, v, sp, mx, prior, mlp_parts, res_all, swish_low, value_low, qk_low, wo, wq, wk, wv, ws, mixed_low, sums, parts, local, later, key_part, value_part,
     ) = refs[:55]
-    near, far, hold, mlp_near, mlp_far, mlp_hold = refs[55:61]
-    chain_refs = refs[61:69]
-    wsem, gs, gr, ss, sr, ms, mr, es, er, isem, lsem, osem, bsem = refs[69:]
+    mlp_near, mlp_far, mlp_hold = refs[55:58]
+    chain_refs = refs[58:66]
+    wsem, gs, gr, ms, mr, es, er, isem, lsem, osem, bsem = refs[66:]
     rows = res.shape[0]
     gather = Gather(n, res, res_all, gs, gr)
-    scatter = Scatter(n, parts, near, far, hold, ss, sr)
     scatter_mlp = Scatter(n, mlp_parts, mlp_near, mlp_far, mlp_hold, ms, mr)
     chain = Chain(chips, heads, True, fac, local, later, *chain_refs)
     ends = Ends(chips)
@@ -1201,6 +1236,7 @@
         return [
             pltpu.make_async_copy(value_low.at[at], value_o.at[at], bsem.at[0, j]),
             pltpu.make_async_copy(qk_low.at[at], qk_o.at[at], bsem.at[1, j]),
+            pltpu.make_async_copy(parts.at[j], parts_o.at[j], bsem.at[2, j]),
         ]
 
     for load in loads[1:]:
@@ -1254,11 +1290,8 @@
             value_low[at, vc] = (value_part[at, vc] + dot(key_dec, after)).astype(BF)
         sums[j] += dot(value_low[at], wv[...], 1, 1).astype(sums.dtype)
         parts[j] = (sums[j].astype(F32) + dot(qk_low[at, heads * DK :], wk[...], 1, 1)).astype(BF)
-        scatter.send(i)
         for put in leaving(j):
             put.start()
-
-    scatter.relay()
 
     @pl.when(ends.takes)
     def _():
@@ -1276,17 +1309,11 @@
             gate_low[here] = (back * up_late[here] * slope).astype(BF)
             upper_low[here] = (back * gelu).astype(BF)
 
-    def write(cols, total):
-        grad_one[:, cols] = total
-
-    scatter.finish(write)
-
-    def write_mlp(cols, total):
-        mlp_out[:, cols] = total
+    def write_mlp(at, cols, total):
+        mlp_out[at, cols] = total
 
     scatter_mlp.finish(write_mlp)
     gather.drain()
-    scatter.drain()
     scatter_mlp.drain()
 
     @pl.when(ends.gives)
@@ -1326,14 +1353,14 @@
             shape((total, heads * DV), BF),
             shape((total, heads * DV), BF),
             shape((total, 2 * heads * DK), BF),
-            shape((rows, model), F32),
+            shape((n, rows, model), BF),
             shape((rows, model), F32),
             shape((rows, model), BF),
             shape(gate_late.shape, BF),
             shape(gate_late.shape, BF),
         ),
         in_specs=[pl.BlockSpec(memory_space=pltpu.SMEM), vmem] + [hbm] * 12 + [vmem] * 5 + [hbm, hbm, vmem, vmem],
-        out_specs=(hbm,) * 4 + (vmem,) * 5,
+        out_specs=(hbm,) * 5 + (vmem,) * 4,
         scratch_shapes=[pltpu.VMEM(a.shape, a.dtype) for a in (q, k, v, sp, mx, prior, mlp_parts)]
         + [
             pltpu.VMEM((n, rows, model), BF),
@@ -1352,11 +1379,10 @@
             pltpu.VMEM((total, heads * DV), BF),
         ]
         + scatter_scratch(n, rows, model)
-        + scatter_scratch(n, rows, model)
         + chain_scratch(pieces)
         + [dma((6,))]
-        + [dma((sems,))] * 6
-        + [dma((1,)), dma((1,)), dma((3, n)), dma((4,)), dma((2,)), dma((2, n))],
+        + [dma((sems,))] * 4
+        + [dma((1,)), dma((1,)), dma((3, n)), dma((4,)), dma((2,)), dma((3, n))],
         compiler_params=params(cid),
         name="mixer_back",
     )(fac, res, wo, wq, wk, wv, ws, q, k, v, sp, mx, prior, mlp_parts, decay, qfac, kfac, cos, sin, og_all, wd, gate_late, up_late)
@@ -1366,7 +1392,7 @@
     (
         two, og, og_late, hidden, gate_low, gate_late, up_low, up_late,
         one, res, swish_low, gated, value_low, qk_low,
-        vec_two, gain, grad_h, raw_h, res_h, attn_h, mlp_h,
+        vec_two, gain, parts_h, raw_h, res_h, attn_h, mlp_h,
         down_o, gate_o, up_o, swish_o, mixer_o, value_o, query_o, key_o, back_o, outs_o, vec_out,
     ) = refs[:32]
     mlp = LineSums(
@@ -1379,8 +1405,12 @@
     )
     (
         turned, osem, grad, raw, res_grad, attn, mlp_out, back, outs, csem, dsem,
-        vec, vec_near, vec_mid, vec_far, vs, vr, us, ur,
+        vec, vec_near, vec_mid, vec_far, vs, vr, us, ur, parts, near, far, hold, lsem, ss, sr,
     ) = refs[56:]
+    grad = grad if parts.shape[0] == 4 else near.at[0]
+    scatter = Scatter(parts.shape[0], parts, near, far, hold, ss, sr)
+    load = pltpu.make_async_copy(parts_h, parts, lsem.at[0])
+    load.start()
     s, t = lax.axis_index("seq"), lax.axis_index("tp")
     span, tp = 2 * chips, vec_far.shape[0] + 1
     share = vec_mid.shape[1]
@@ -1404,6 +1434,36 @@
             mlp.share(u)
         mix.share(u)
 
+    half = mix.out.shape[2] // 2
+    lo, hi = pl.ds(0, half), pl.ds(half, half)
+
+    def put(pairs):
+        copies = [pltpu.make_async_copy(a, b, osem.at[i]) for i, (a, b) in enumerate(pairs)]
+        for copy in copies:
+            copy.start()
+        for copy in copies:
+            copy.wait()
+
+    def put_mlp(w):
+        if w == 2:
+            turned[...] = mlp.out[0].T
+            put([(turned, down_o)])
+        else:
+            put([(mlp.out.at[0], (gate_o, up_o)[w])])
+
+    def put_mix(w):
+        if w == 1:
+            turned[...] = mix.out[0].T
+            put([(turned, mixer_o)])
+        elif w == 3:
+            put([(mix.out.at[0, :, lo], query_o), (mix.out.at[0, :, hi], key_o)])
+        else:
+            put([(mix.out.at[0], (swish_o, None, value_o)[w])])
+
+    load.wait()
+    for i in range(1, scatter.n):
+        scatter.send(i)
+
     @pl.loop(0, mix.units)
     def _(u):
         for w in range(mix.units):
@@ -1435,10 +1495,17 @@
         def _():
             chunk = raw.shape[0]
 
-            @pl.loop(0, grad_h.shape[0] // chunk)
+            scatter.relay()
+
+            def write(at, cols, total):
+                grad[at, cols] = total.astype(grad.dtype)
+
+            scatter.finish(write)
+
+            @pl.loop(0, parts.shape[1] // chunk)
             def _(c):
                 here = pl.ds(pl.multiple_of(c * chunk, chunk), chunk)
-                pairs = (grad_h, grad), (raw_h, raw), (res_h, res_grad), (attn_h, attn), (mlp_h, mlp_out)
+                pairs = (raw_h, raw), (res_h, res_grad), (attn_h, attn), (mlp_h, mlp_out)
                 ins = [
                     pltpu.make_async_copy(a.at[here], b, csem.at[i])
                     for i, (a, b) in enumerate(pairs)
@@ -1450,10 +1517,10 @@
                 value = raw[...].astype(F32)
                 outs[...] = (value + attn[...] + mlp_out[...]).astype(BF)
                 center, inv = row_stats(value)
-                hat = center * inv
-                vec[0:1] += jnp.sum(grad[...] * hat, 0, keepdims=True)
-                vec[1:2] += jnp.sum(grad[...], 0, keepdims=True)
-                back[...] = (res_grad[...] + norm_pull(grad[...], hat, inv, gain[...])).astype(BF)
+                hat, given = center * inv, grad[here].astype(F32)
+                vec[0:1] += jnp.sum(given * hat, 0, keepdims=True)
+                vec[1:2] += jnp.sum(given, 0, keepdims=True)
+                back[...] = (res_grad[...] + norm_pull(given, hat, inv, gain[...])).astype(BF)
                 puts = [
                     pltpu.make_async_copy(a, b.at[0, here], dsem.at[i])
                     for i, (a, b) in enumerate(((back, back_o), (outs, outs_o)))
@@ -1478,39 +1545,23 @@
         def _():
             mlp.finish(u - 1)
             mix.finish(u - 1)
-
-    half = mix.out.shape[2] // 2
-    lo, hi = pl.ds(0, half), pl.ds(half, half)
-    turned[...] = mlp.out[2].T
-    pairs = [
-        (mlp.out.at[0], gate_o),
-        (mlp.out.at[1], up_o),
-        (mix.out.at[0], swish_o),
-        (turned, down_o),
-        (turned, mixer_o),
-        (mix.out.at[2], value_o),
-        (mix.out.at[3, :, lo], query_o),
-        (mix.out.at[3, :, hi], key_o),
-    ]
-    copies = [pltpu.make_async_copy(a, b, osem.at[i]) for i, (a, b) in enumerate(pairs)]
-    for i in (3, 0, 1, 2, 5):
-        copies[i].start()
-    copies[3].wait()
-    turned[...] = mix.out[1].T
-    copies[4].start()
+            for w in range(mix.units - 1):
+
+                @pl.when(u - 1 == w)
+                def _(w=w):
+                    put_mlp(w)
+                    put_mix(w)
+
     mix.finish(mix.units - 1)
-    for copy in copies[6:]:
-        copy.start()
+    put_mix(mix.units - 1)
     for copy in vec_last:
         copy.wait_recv()
     vec_out[...] = vec_mid[...] + jnp.sum(vec_far[...], 0)
     for copy in vec_first + vec_last:
         copy.wait_send()
+    scatter.drain()
     mlp.drain()
     mix.drain()
-    for i, copy in enumerate(copies):
-        if i != 3:
-            copy.wait()
 
 
 def weight_sums(
@@ -1552,7 +1603,7 @@
         + [
             pltpu.VMEM((width, cut), F32),
             dma((8,)),
-            part(F32),
+            pltpu.VMEM((rows, model) if cross < 4 else (16, 128), F32),
             part(BF),
             part(F32),
             part(F32),
@@ -1569,6 +1620,13 @@
             dma((ring,)),
             dma((cross,)),
             dma((cross,)),
+            pltpu.VMEM((cross + 1, rows, model), BF),
+        ]
+        + scatter_scratch(cross + 1, rows, model)
+        + [
+            dma((1,)),
+            dma((max(10, cross),)),
+            dma((max(10, cross),)),
         ],
         compiler_params=params(cid),
         name="weights",

time: 398 us -> 389 us (0.977)
  Pallas kernels: 385 us -> 375 us
    pallas_call x1, Pallas kernels: 80.9 us -> 69.7 us  [mixer_back(): pl.pallas_call(functools.partial(mixer_back_kernel, n, chips, heads), out...]
    pallas_call x1, Pallas kernels: 62 us -> 55.8 us  [mlp(): pl.pallas_call(functools.partial(mlp_kernel, n, chips), out_shape=(shape(...]
    pallas_call x1, Pallas kernels: 64.2 us -> 69.1 us  [mixer(): pl.pallas_call(functools.partial(mixer_kernel, n, chips, heads), out_shap...]
where the time goes in v6:
time: 389 us; the launch traced here: 388 us
  Pallas kernels  375 us (96%)
  local copies, waits for them, and re-layouts  12.7 us (3%)
    pallas_call x1, Pallas kernels, weight_sums(): pl.pallas_call(functools.partial(weights_kernel, chips), out_shape=(shape...  180 us
    pallas_call x1, Pallas kernels, mixer_back(): pl.pallas_call(functools.partial(mixer_back_kernel, n, chips, heads), out...  69.7 us
    pallas_call x1, Pallas kernels, mixer(): pl.pallas_call(functools.partial(mixer_kernel, n, chips, heads), out_shap...  69.1 us
    pallas_call x1, Pallas kernels, mlp(): pl.pallas_call(functools.partial(mlp_kernel, n, chips), out_shape=(shape(...  55.8 us
    unnamed x26, local copies, waits for them, and re-layouts  11.3 us

profile of v6, /device:TPU:0, one launch (start us, length us, event | category | flops | bytes accessed | tf_op | source)
XLA Modules:
  0.0 388.2 jit_solution(14596492359180310884)
XLA Ops:
  0.6 69.1 %mixer.1 = (bf16[4,128,2048]{2,1,0:T(8,128)(2,1)}, bf16[7,128,2048]{2,1,0:T(8,128)(2,1)}, bf16[512,512]{1,0:T(8,128)(2,1)}, bf16[512,512]{1,0:T(8,128)(2,1)}, bf...) custom-call(f32[2,8]{1,0:T(2,128)} %constant.14.clone.refs_0_, ...), custom_call_target="tpu_custom_call" | custom-call | tf_op jit(solution)/shard_map/mixer/pallas_call | solution.py:837
  69.8 55.8 %mlp.1 = (bf16[8,128,2048]{2,1,0:T(8,128)(2,1)}, bf16[1024,1024]{1,0:T(8,128)(2,1)}, bf16[896,1024]{1,0:T(8,128)(2,1)}, bf16[896,1024]{1,0:T(8,128)(2,1)}, bf16[...) custom-call(bf16[128,2048]{1,0:T(8,128)(2,1)} %bitcast.20, ...), custom_call_target="tpu_custom_call" | custom-call | tf_op jit(solution)/shard_map/mlp/pallas_call | solution.py:1104
  125.6 69.7 %mixer_back.1 = (bf16[4,128,2048]{2,1,0:T(8,128)(2,1)}, bf16[512,1024]{1,0:T(8,128)(2,1)}, bf16[512,1024]{1,0:T(8,128)(2,1)}, bf16[512,1024]{1,0:T(8,128)(2,1)},...) custom-call(f32[2,8]{1,0:T(2,128)} %constant.14.clone.refs_0_, ...), custom_call_target="tpu_custom_call" | custom-call | tf_op jit(solution)/shard_map/mixer_back/pallas_call | solution.py:1349
  195.3 180.2 %weights.1 = (f32[1024,256]{1,0:T(8,128)}, f32[256,1024]{1,0:T(8,128)}, f32[256,1024]{1,0:T(8,128)}, f32[256,1024]{1,0:T(8,128)}, f32[1024,256]{1,0:T(8,128)}, /...) custom-call(bf16[1024,2048]{1,0:T(8,128)(2,1)} %bitcast.22, ...), custom_call_target="tpu_custom_call" | custom-call | tf_op jit(solution)/shard_map/weights/pallas_call | solution.py:1584
  375.5 0.0 copy-start.7
  375.5 0.0 copy-start.6
  375.6 0.8 constant_dynamic-slice_fusion
  376.4 0.5 slice_bitcast_fusion
  376.9 0.0 copy-start.5
  376.9 2.0 copy.40
  378.9 1.9 copy.41
  380.8 0.0 copy-done.7
  380.8 0.0 copy-start.4
  380.8 0.8 copy.42
  381.6 0.0 copy-done.6
  381.6 0.8 copy.43
  382.4 0.0 copy-done.5
  382.4 0.0 copy-start.3
  382.4 1.0 copy.44
  383.3 0.0 copy-done.4
  383.3 0.0 copy-start.2
  383.4 1.0 copy.45
  384.3 0.0 copy-done.3
  384.3 0.0 copy-start.1
  384.3 1.0 copy.46
  385.3 0.0 copy-done.2
  385.3 0.0 copy-start
  385.3 1.0 copy.47
  386.3 0.0 copy-done.1
  386.3 1.0 copy.48
  387.2 0.0 copy-done
  387.2 1.0 copy.49
Async XLA Ops:
  375.5 5.2 %copy-start.7 = (f32[256,512]{1,0:T(8,128)S(1)}, f32[256,512]{1,0:T(8,128)}, u32[]{:S(2)}) copy-start(f32[256,512]{1,0:T(8,128)} %get-tuple-element.124) | copy-start | bytes 1572868
  375.5 6.0 %copy-start.6 = (f32[256,512]{1,0:T(8,128)S(1)}, f32[256,512]{1,0:T(8,128)}, u32[]{:S(2)}) copy-start(f32[256,512]{1,0:T(8,128)} %get-tuple-element.125) | copy-start | bytes 1572868
  376.9 5.4 %copy-start.5 = (f32[256,1024]{1,0:T(8,128)S(1)}, f32[256,1024]{1,0:T(8,128)}, u32[]{:S(2)}) copy-start(f32[256,1024]{1,0:T(8,128)} %get-tuple-element.126) | copy-start | bytes 3145732
  380.8 2.6 copy-start.4
  382.4 1.9 copy-start.3
  383.3 1.9 copy-start.2
  384.3 1.9 copy-start.1
  385.3 1.9 copy-start

commit v7 on v6

--- a/solution.py
+++ b/solution.py
@@ -1460,10 +1460,6 @@
         else:
             put([(mix.out.at[0], (swish_o, None, value_o)[w])])
 
-    load.wait()
-    for i in range(1, scatter.n):
-        scatter.send(i)
-
     @pl.loop(0, mix.units)
     def _(u):
         for w in range(mix.units):
@@ -1476,6 +1472,12 @@
         @pl.when(u < mlp.units)
         def _():
             mlp.step(u, 0)
+
+        @pl.when(u == 0)
+        def _():
+            load.wait()
+            for i in range(1, scatter.n):
+                scatter.send(i)
 
         for w in range(mix.units):
 
@@ -1515,14 +1517,14 @@
                 for copy in ins:
                     copy.wait()
                 value = raw[...].astype(F32)
-                outs[...] = (value + attn[...] + mlp_out[...]).astype(BF)
+                outs[...] = value + attn[...] + mlp_out[...]
                 center, inv = row_stats(value)
                 hat, given = center * inv, grad[here].astype(F32)
                 vec[0:1] += jnp.sum(given * hat, 0, keepdims=True)
                 vec[1:2] += jnp.sum(given, 0, keepdims=True)
-                back[...] = (res_grad[...] + norm_pull(given, hat, inv, gain[...])).astype(BF)
+                back[...] = res_grad[...] + norm_pull(given, hat, inv, gain[...])
                 puts = [
-                    pltpu.make_async_copy(a, b.at[0, here], dsem.at[i])
+                    pltpu.make_async_copy(a, b.at[here], dsem.at[i])
                     for i, (a, b) in enumerate(((back, back_o), (outs, outs_o)))
                 ]
                 for copy in puts:
@@ -1592,8 +1594,8 @@
             shape(cut, width),
             shape(cut, keys),
             shape(cut, keys),
-            jax.ShapeDtypeStruct((1, rows, model), BF),
-            jax.ShapeDtypeStruct((1, rows, model), BF),
+            shape(rows, model),
+            shape(rows, model),
             shape(8, share),
         ),
         in_specs=[hbm] * 14 + [vmem] * 2 + [hbm] * 5,
@@ -1608,8 +1610,8 @@
             part(F32),
             part(F32),
             part(F32),
-            part(BF),
-            part(BF),
+            part(F32),
+            part(F32),
             dma((5,)),
             dma((2,)),
             pltpu.VMEM((8, model), F32),
@@ -1693,8 +1695,8 @@
     each = model // (seqs * tps)
     vector_sums = lax.dynamic_slice(vector_sums, (0, lax.axis_index("tp") * each), (4, each))
     return (
-        outputs,
-        input_grad,
+        outputs.astype(BF)[None],
+        input_grad.astype(BF)[None],
         query_grad,
         key_grad,
         value_grad,

time: 389 us -> 388 us (level)
  local copies, waits for them, and re-layouts: 12.7 us -> 8.71 us
    unnamed x26 -> x24, local copies, waits for them, and re-layouts: 11.3 us -> 7.44 us
where the time goes in v7:
time: 388 us; the launch traced here: 387 us
  Pallas kernels  375 us (97%)
  local copies, waits for them, and re-layouts  8.71 us (2%)
    pallas_call x1, Pallas kernels, weight_sums(): pl.pallas_call(functools.partial(weights_kernel, chips), out_shape=(shape...  180 us
    pallas_call x1, Pallas kernels, mixer_back(): pl.pallas_call(functools.partial(mixer_back_kernel, n, chips, heads), out...  69.7 us
    pallas_call x1, Pallas kernels, mixer(): pl.pallas_call(functools.partial(mixer_kernel, n, chips, heads), out_shap...  69.1 us
    pallas_call x1, Pallas kernels, mlp(): pl.pallas_call(functools.partial(mlp_kernel, n, chips), out_shape=(shape(...  55.8 us

profile of v7, /device:TPU:0, one launch (start us, length us, event | category | flops | bytes accessed | tf_op | source)
XLA Modules:
  0.0 387.3 jit_solution(7548486485553873165)
XLA Ops:
  0.6 69.1 %mixer.1 = (bf16[4,128,2048]{2,1,0:T(8,128)(2,1)}, bf16[7,128,2048]{2,1,0:T(8,128)(2,1)}, bf16[512,512]{1,0:T(8,128)(2,1)}, bf16[512,512]{1,0:T(8,128)(2,1)}, bf...) custom-call(f32[2,8]{1,0:T(2,128)} %constant.14.clone.refs_0_, ...), custom_call_target="tpu_custom_call" | custom-call | tf_op jit(solution)/shard_map/mixer/pallas_call | solution.py:837
  69.8 55.8 %mlp.1 = (bf16[8,128,2048]{2,1,0:T(8,128)(2,1)}, bf16[1024,1024]{1,0:T(8,128)(2,1)}, bf16[896,1024]{1,0:T(8,128)(2,1)}, bf16[896,1024]{1,0:T(8,128)(2,1)}, bf16[...) custom-call(bf16[128,2048]{1,0:T(8,128)(2,1)} %bitcast.24, ...), custom_call_target="tpu_custom_call" | custom-call | tf_op jit(solution)/shard_map/mlp/pallas_call | solution.py:1104
  125.6 69.7 %mixer_back.1 = (bf16[4,128,2048]{2,1,0:T(8,128)(2,1)}, bf16[512,1024]{1,0:T(8,128)(2,1)}, bf16[512,1024]{1,0:T(8,128)(2,1)}, bf16[512,1024]{1,0:T(8,128)(2,1)},...) custom-call(f32[2,8]{1,0:T(2,128)} %constant.14.clone.refs_0_, ...), custom_call_target="tpu_custom_call" | custom-call | tf_op jit(solution)/shard_map/mixer_back/pallas_call | solution.py:1349
  195.3 180.5 %weights.1 = (f32[1024,256]{1,0:T(8,128)}, f32[256,1024]{1,0:T(8,128)}, f32[256,1024]{1,0:T(8,128)}, f32[256,1024]{1,0:T(8,128)}, f32[1024,256]{1,0:T(8,128)}, /...) custom-call(bf16[1024,2048]{1,0:T(8,128)(2,1)} %bitcast.26, ...), custom_call_target="tpu_custom_call" | custom-call | tf_op jit(solution)/shard_map/weights/pallas_call | solution.py:1586
  375.8 0.0 copy-start.7
  375.8 0.0 copy-start.6
  375.8 0.0 copy-start.5
  375.8 2.8 convert_bitcast_fusion
  378.6 0.7 constant_dynamic-slice_fusion
  379.4 0.5 slice_bitcast_fusion
  379.9 0.0 copy-done.7
  379.9 0.0 copy-start.4
  379.9 0.8 copy.38
  380.7 0.0 copy-done.6
  380.7 0.8 copy.39
  381.5 0.0 copy-done.5
  381.5 0.0 copy-start.3
  381.5 1.0 copy.40
  382.5 0.0 copy-done.4
  382.5 0.0 copy-start.2
  382.5 1.0 copy.41
  383.4 0.0 copy-done.3
  383.4 0.0 copy-start.1
  383.4 1.0 copy.42
  384.4 0.0 copy-done.2
  384.4 0.0 copy-start
  384.4 1.0 copy.43
  385.4 0.0 copy-done.1
  385.4 1.0 copy.44
  386.4 0.0 copy-done
  386.4 1.0 copy.45
Async XLA Ops:
  375.8 4.1 %copy-start.7 = (f32[256,512]{1,0:T(8,128)S(1)}, f32[256,512]{1,0:T(8,128)}, u32[]{:S(2)}) copy-start(f32[256,512]{1,0:T(8,128)} %get-tuple-element.126) | copy-start | bytes 1572868
  375.8 4.9 %copy-start.6 = (f32[256,512]{1,0:T(8,128)S(1)}, f32[256,512]{1,0:T(8,128)}, u32[]{:S(2)}) copy-start(f32[256,512]{1,0:T(8,128)} %get-tuple-element.127) | copy-start | bytes 1572868
  375.8 5.7 %copy-start.5 = (f32[256,1024]{1,0:T(8,128)S(1)}, f32[256,1024]{1,0:T(8,128)}, u32[]{:S(2)}) copy-start(f32[256,1024]{1,0:T(8,128)} %get-tuple-element.128) | copy-start | bytes 3145732
  379.9 2.6 copy-start.4
  381.5 1.9 copy-start.3
  382.5 1.9 copy-start.2
  383.4 1.9 copy-start.1
  384.4 1.9 copy-start

commit v8 on v7

--- a/solution.py
+++ b/solution.py
@@ -1581,7 +1581,7 @@
     hbm = pl.BlockSpec(memory_space=pl.ANY)
     shape = lambda *a: jax.ShapeDtypeStruct(a, F32)
     ring, cross = 2 * chips - 1, lax.axis_size("tp") - 1
-    rows, share, chunk = raw.shape[0], model // (2 * chips), 16
+    rows, share, chunk = raw.shape[0], model // (2 * chips), 32 if cross < 4 else 16
     part = lambda dtype: pltpu.VMEM((chunk, model), dtype)
     return pl.pallas_call(
         functools.partial(weights_kernel, chips),

time: 388 us -> 386 us (level)
  no operation moved by 1% of the time
where the time goes in v8:
time: 386 us
  Pallas kernels  373 us (97%)
  local copies, waits for them, and re-layouts  8.71 us (2%)
    pallas_call x1, Pallas kernels, weight_sums(): pl.pallas_call(functools.partial(weights_kernel, chips), out_shape=(shape...  179 us
    pallas_call x1, Pallas kernels, mixer_back(): pl.pallas_call(functools.partial(mixer_back_kernel, n, chips, heads), out...  69.7 us
    pallas_call x1, Pallas kernels, mixer(): pl.pallas_call(functools.partial(mixer_kernel, n, chips, heads), out_shap...  69.1 us
    pallas_call x1, Pallas kernels, mlp(): pl.pallas_call(functools.partial(mlp_kernel, n, chips), out_shape=(shape(...  55.8 us

profile of v8, /device:TPU:0, one launch (start us, length us, event | category | flops | bytes accessed | tf_op | source)
XLA Modules:
  0.0 385.6 jit_solution(3195536279366772750)
XLA Ops:
  0.6 69.1 %mixer.1 = (bf16[4,128,2048]{2,1,0:T(8,128)(2,1)}, bf16[7,128,2048]{2,1,0:T(8,128)(2,1)}, bf16[512,512]{1,0:T(8,128)(2,1)}, bf16[512,512]{1,0:T(8,128)(2,1)}, bf...) custom-call(f32[2,8]{1,0:T(2,128)} %constant.14.clone.refs_0_, ...), custom_call_target="tpu_custom_call" | custom-call | tf_op jit(solution)/shard_map/mixer/pallas_call | solution.py:837
  69.8 55.8 %mlp.1 = (bf16[8,128,2048]{2,1,0:T(8,128)(2,1)}, bf16[1024,1024]{1,0:T(8,128)(2,1)}, bf16[896,1024]{1,0:T(8,128)(2,1)}, bf16[896,1024]{1,0:T(8,128)(2,1)}, bf16[...) custom-call(bf16[128,2048]{1,0:T(8,128)(2,1)} %bitcast.24, ...), custom_call_target="tpu_custom_call" | custom-call | tf_op jit(solution)/shard_map/mlp/pallas_call | solution.py:1104
  125.6 69.7 %mixer_back.1 = (bf16[4,128,2048]{2,1,0:T(8,128)(2,1)}, bf16[512,1024]{1,0:T(8,128)(2,1)}, bf16[512,1024]{1,0:T(8,128)(2,1)}, bf16[512,1024]{1,0:T(8,128)(2,1)},...) custom-call(f32[2,8]{1,0:T(2,128)} %constant.14.clone.refs_0_, ...), custom_call_target="tpu_custom_call" | custom-call | tf_op jit(solution)/shard_map/mixer_back/pallas_call | solution.py:1349
  195.3 178.7 %weights.1 = (f32[1024,256]{1,0:T(8,128)}, f32[256,1024]{1,0:T(8,128)}, f32[256,1024]{1,0:T(8,128)}, f32[256,1024]{1,0:T(8,128)}, f32[1024,256]{1,0:T(8,128)}, /...) custom-call(bf16[1024,2048]{1,0:T(8,128)(2,1)} %bitcast.26, ...), custom_call_target="tpu_custom_call" | custom-call | tf_op jit(solution)/shard_map/weights/pallas_call | solution.py:1586
  374.0 0.0 copy-start.7
  374.0 0.0 copy-start.6
  374.0 0.0 copy-start.5
  374.0 2.8 convert_bitcast_fusion
  376.8 0.7 constant_dynamic-slice_fusion
  377.6 0.5 slice_bitcast_fusion
  378.1 0.0 copy-done.7
  378.1 0.0 copy-start.4
  378.1 0.8 copy.38
  378.9 0.0 copy-done.6
  378.9 0.8 copy.39
  379.7 0.0 copy-done.5
  379.7 0.0 copy-start.3
  379.7 1.0 copy.40
  380.7 0.0 copy-done.4
  380.7 0.0 copy-start.2
  380.7 1.0 copy.41
  381.7 0.0 copy-done.3
  381.7 0.0 copy-start.1
  381.7 1.0 copy.42
  382.6 0.0 copy-done.2
  382.6 0.0 copy-start
  382.6 1.0 copy.43
  383.6 0.0 copy-done.1
  383.6 1.0 copy.44
  384.6 0.0 copy-done
  384.6 1.0 copy.45
Async XLA Ops:
  374.0 4.1 %copy-start.7 = (f32[256,512]{1,0:T(8,128)S(1)}, f32[256,512]{1,0:T(8,128)}, u32[]{:S(2)}) copy-start(f32[256,512]{1,0:T(8,128)} %get-tuple-element.126) | copy-start | bytes 1572868
  374.0 4.9 %copy-start.6 = (f32[256,512]{1,0:T(8,128)S(1)}, f32[256,512]{1,0:T(8,128)}, u32[]{:S(2)}) copy-start(f32[256,512]{1,0:T(8,128)} %get-tuple-element.127) | copy-start | bytes 1572868
  374.0 5.7 %copy-start.5 = (f32[256,1024]{1,0:T(8,128)S(1)}, f32[256,1024]{1,0:T(8,128)}, u32[]{:S(2)}) copy-start(f32[256,1024]{1,0:T(8,128)} %get-tuple-element.128) | copy-start | bytes 3145732
  378.1 2.6 copy-start.4
  379.7 1.9 copy-start.3
  380.7 1.9 copy-start.2
  381.7 1.9 copy-start.1
  382.6 1.9 copy-start
